TPU v7x, 32 devices: a whole 2x2x4 slice. The times are simulated.
32 devices in a mesh: seq: 16 (over z, y, x), head: 2 (over core).
Axes of the slice: x: 2, y: 2, z: 4, core: 2. Of those that a mesh axis runs over, the one named last changes fastest.
Arguments:
- queries: bfloat16 [4096, 5120], P('seq', 'head'), may hold values from -100 to 100
- keys: bfloat16 [4096, 5120], P('seq', 'head'), may hold values from -12 to 12
- values: bfloat16 [4096, 5120], P('seq', 'head'), may hold values from -6 to 6
- hidden: bfloat16 [4096, 5120], P('seq', 'head'), may hold values from -3 to 3
- cached: bfloat16 [4096, 5120], P('seq', 'head'), may hold values from -6 to 6
- active: int32 [4096], P('seq'), may hold values from 0 to 1, as said below
- w_out: bfloat16 [5120, 5120], P('head', 'seq'), may hold values from -0.078125 to 0.078125
Outputs:
- block_output: bfloat16 [4096, 5120], P('seq', 'head')
Inputs may be any that keep to these rules, and one draw needn't show every extreme that they name: `active`: exactly 176 ones in all; among the 256 tokens of one index of seq at most 32 ones, and that many on some of them.
All inputs are finite; a program needn't handle non-finite values.
Results may differ from a plain program's by a relative error of at most 0.0039.
Values may be sent and summed in bfloat16 or wider, within the bound.
No kernel may reach another device: no remote copies, remote signals or barrier semaphores. Data moves between devices by JAX's collectives and lax.ppermute only.
A program may use at most 64 MiB of HBM per device.

v0:
```python
import jax
import jax.numpy as jnp
from jax import lax
from jax.sharding import PartitionSpec as P

HD = 128


def for_sending(value):

    def short(part):
        return part.astype(jnp.bfloat16) if part.dtype == jnp.float32 else part

    return jax.tree.map(short, value)


def local_partials(query_rows, keys, values):
    head_count = keys.shape[1] // HD
    inv_root = 1.0 / HD**0.5

    def one_head(head):
        start = head * HD
        q_head = lax.dynamic_slice_in_dim(query_rows, start, HD, 1)
        k_head = lax.dynamic_slice_in_dim(keys, start, HD, 1)
        v_head = lax.dynamic_slice_in_dim(values, start, HD, 1)
        scores = (
            lax.dot_general(
                q_head, k_head, (((1,), (1,)), ((), ())), preferred_element_type=jnp.float32
            )
            * inv_root
        )
        peak = jnp.max(scores, axis=1)
        expo = jnp.exp(scores - peak[:, None])
        total = jnp.sum(expo, axis=1)
        block_out = jnp.dot(expo.astype(jnp.bfloat16), v_head, preferred_element_type=jnp.float32)
        return ((block_out / total[:, None]).astype(jnp.bfloat16), peak, total)

    return lax.map(one_head, jnp.arange(head_count, dtype=jnp.int32))


def shards(queries, keys, values, hidden, cached, active, w_out):
    tok_dev, features = queries.shape
    head_count = features // HD
    devices = lax.axis_size("seq")
    capacity = tok_dev // 8
    act_rows = jnp.nonzero(active, size=capacity, fill_value=tok_dev)[0].astype(jnp.int32)
    safe_rows = jnp.minimum(act_rows, tok_dev - 1)
    own_queries = queries[safe_rows]
    gathered = lax.all_gather(own_queries, "seq", axis=0, tiled=True)
    block_out, block_peak, block_total = local_partials(gathered, keys, values)
    block_out = block_out.reshape(head_count, devices, capacity, HD)
    peak_in, total_in = (
        lax.all_to_all(
            block_peak.reshape(head_count, devices, capacity),
            "seq",
            split_axis=1,
            concat_axis=1,
            tiled=True,
        ),
        lax.all_to_all(
            block_total.reshape(head_count, devices, capacity),
            "seq",
            split_axis=1,
            concat_axis=1,
            tiled=True,
        ),
    )
    out_in = lax.all_to_all(
        for_sending(block_out), "seq", split_axis=1, concat_axis=1, tiled=True
    ).astype(block_out.dtype)
    top_max = jnp.max(peak_in, axis=1, keepdims=True)
    weight = total_in * jnp.exp(peak_in - top_max)
    mixed = jnp.einsum("hnc,hncd->hcd", weight, out_in.astype(jnp.float32))
    mixed = mixed / jnp.sum(weight, axis=1)[:, :, None]
    attn = jnp.transpose(mixed, (1, 0, 2)).reshape(capacity, features).astype(jnp.bfloat16)
    own_columns = w_out.shape[1]
    terms = jnp.dot(
        lax.all_gather(attn, "seq", axis=0, tiled=True), w_out, preferred_element_type=jnp.float32
    )
    terms = lax.psum(terms.astype(jnp.bfloat16), "head").astype(jnp.float32)
    terms = terms.reshape(devices, capacity, own_columns)
    arrived = lax.all_to_all(
        terms.astype(jnp.bfloat16), "seq", split_axis=0, concat_axis=2, tiled=True
    ).astype(terms.dtype)
    summed = lax.dynamic_slice_in_dim(arrived[0], lax.axis_index("head") * features, features, 1)
    updated = (hidden[safe_rows].astype(jnp.float32) + summed).astype(jnp.bfloat16)
    return cached.at[act_rows].set(updated, mode="drop")


def solution(mesh):
    placed = (
        P("seq", "head"),
        P("seq", "head"),
        P("seq", "head"),
        P("seq", "head"),
        P("seq", "head"),
        P("seq"),
        P("head", "seq"),
    )
    return jax.shard_map(
        shards, mesh=mesh, in_specs=placed, out_specs=P("seq", "head"), check_vma=False
    )
```

profile of v0, /device:TPU:0, one launch (start us, length us, event | category | flops | bytes accessed | tf_op | source)
XLA Modules:
  0.0 377.9 jit_solution(9547690487952534565)
XLA Ops:
  6.5 2.6 copy.57
  10.5 2.3 scatter_custom_fusion
  13.8 1.3 gather_fusion
  15.2 66.8 %all-gather.6.cloned.1.call-done = bf16[512,2560]{1,0:T(8,128)(2,1)} async-done(((bf16[32,2560]{1,0:T(8,128)(2,1)}), bf16[512,2560]{1,0:T(8,128)(2,1)}) %all-gather.6.cloned.1.call-update) | async-done | bytes 2621456 | tf_op jit(solution)/shard_map/all_gather | solution.py:49
  82.0 88.6 %while.14 = (s32[]{:T(128)}, bf16[20,512,128]{2,1,0:T(8,128)(2,1)}, f32[20,512]{1,0:T(8,128)S(1)}, f32[20,512]{1,0:T(8,128)S(1)}, s32[20]{0:T(128)S(1)}, /*index...) while((s32[]{:T(128)}, bf16[20,512,128]{2,1,0:T(8,128)(2,1)}, ...), condition=%wide.region_8.9_spmd, body=%wide.region_5.8_spmd.sunk | while | flops 68025344 | bytes 1986235 | solution.py:38
  83.3 1.2 fusion.40
  84.5 1.8 fusion.42
  89.0 1.8 fusion.42
  93.4 1.8 fusion.42
  96.6 1.2 fusion.40
  97.8 1.8 fusion.42
  101.0 1.2 fusion.40
  102.3 1.8 fusion.42
  105.4 1.2 fusion.40
  106.7 1.8 fusion.42
  111.1 1.8 fusion.42
  115.6 1.8 fusion.42
  118.7 1.2 fusion.40
  120.0 1.8 fusion.42
  124.4 1.8 fusion.42
  127.6 1.2 fusion.40
  128.8 1.8 fusion.42
  132.0 1.2 fusion.40
  133.3 1.8 fusion.42
  137.7 1.8 fusion.42
  142.1 1.8 fusion.42
  146.5 1.8 fusion.42
  151.0 1.8 fusion.42
  154.1 1.2 fusion.40
  155.4 1.8 fusion.42
  158.6 1.2 fusion.40
  159.8 1.8 fusion.42
  164.3 1.8 fusion.42
  168.7 1.8 fusion.42
  171.5 4.1 %all-to-all-start.2 = ((f32[16,1,640]{2,1,0:T(1,128)}), f32[16,1,640]{2,1,0:T(1,128)S(1)}, u32[]{:S(2)}, u32[]{:S(2)}) async-start(f32[16,1,640]{2,1,0:T(1,128)} %reshape.215), calls=%async_computation.2 | async-start | bytes 81920 | tf_op jit(solution)/shard_map/all_to_all | solution.py:53
  176.5 6.5 %all-to-all-done.2 = f32[16,1,640]{2,1,0:T(1,128)S(1)} async-done(((f32[16,1,640]{2,1,0:T(1,128)}), f32[16,1,640]{2,1,0:T(1,128)S(1)}, u32[]{:S(2)}, u32[]{:S(2)}) %all-to-all-start.2) | async-done | bytes 40992 | tf_op jit(solution)/shard_map/all_to_all | solution.py:53
  183.1 3.5 all-to-all-start.1
  186.6 3.9 %copy.18 = bf16[20,16,32,128]{3,2,0,1:T(8,128)(2,1)} copy(bf16[20,16,32,128]{3,2,1,0:T(8,128)(2,1)} %bitcast.61) | data formatting | bytes 5242880 | tf_op jit(solution)/shard_map/reshape | solution.py:51
  190.5 3.5 all-to-all-done.1
  194.0 4.4 %all-to-all-start = ((bf16[20,16,32,128]{3,2,0,1:T(8,128)(2,1)}), bf16[20,16,32,128]{3,2,0,1:T(8,128)(2,1)}, u32[]{:S(2)}, u32[]{:S(2)}) async-start(bf16[20,16,32,128]{3,2,0,1:T(8,128)(2,1)} %copy.18), calls=%async_computation | async-start | bytes 5242880 | tf_op jit(solution)/shard_map/all_to_all | solution.py:68
  201.1 46.9 %all-to-all-done = bf16[20,16,32,128]{3,2,0,1:T(8,128)(2,1)} async-done(((bf16[20,16,32,128]{3,2,0,1:T(8,128)(2,1)}), bf16[20,16,32,128]{3,2,0,1:T(8,128)(2,1)}, u32[]{:S(2)}, u32[]{:S(2)}) %all-to-all-start) | async-done | bytes 2621472 | tf_op jit(solution)/shard_map/all_to_all | solution.py:68
  248.0 4.9 %fusion.12 = f32[32,20,1,128]{3,2,1,0:T(1,128)S(1)} fusion(bf16[20,16,32,1]{1,3,0,2:T(2,128)(2,1)S(1)} %copy.26, bf16[20,16,32,128]{3,2,0,1:T(8,128)(2,1)} %all-to-all-done), kind=kOutput, calls=%fused_computation.18 | convolution fusion | flops 2621440 | bytes 2969600 | tf_op jit(solution)/shard_map/hnc,hncd->hcd/dot_general | solution.py:73
  253.9 70.8 %all-gather.4.cloned.1.call-done = bf16[512,2560]{1,0:T(8,128)(2,1)} async-done(((bf16[32,2560]{1,0:T(8,128)(2,1)}), bf16[512,2560]{1,0:T(8,128)(2,1)}) %all-gather.4.cloned.1.call-update) | async-done | bytes 2621456 | tf_op jit(solution)/shard_map/all_gather | solution.py:78
  324.7 2.8 convolution_convert_fusion
  328.4 17.1 %all-reduce.2.cloned.1.call-done = bf16[16,32,320]{2,1,0:T(8,128)(2,1)} async-done(((bf16[16,32,320]{2,1,0:T(8,128)(2,1)}), bf16[16,32,320]{2,1,0:T(8,128)(2,1)}) %all-reduce.2.cloned.1.call-update) | async-done | bytes 327696 | tf_op jit(solution)/shard_map/psum | solution.py:80
  345.5 6.8 %all-to-all-start.3 = ((bf16[16,32,320]{2,1,0:T(8,128)(2,1)}), bf16[16,32,320]{2,1,0:T(8,128)(2,1)S(1)}, u32[]{:S(2)}, u32[]{:S(2)}) async-start(bf16[16,32,320]{2,1,0:T(8,128)(2,1)} %all-reduce.2.cloned.1.call-done), calls=%async_computation.3 | async-start | bytes 786432 | tf_op jit(solution)/shard_map/all_to_all | solution.py:82
  352.3 13.0 %all-to-all-done.3 = bf16[16,32,320]{2,1,0:T(8,128)(2,1)S(1)} async-done(((bf16[16,32,320]{2,1,0:T(8,128)(2,1)}), bf16[16,32,320]{2,1,0:T(8,128)(2,1)S(1)}, u32[]{:S(2)}, u32[]{:S(2)}) %all-to-all-start.3) | async-done | bytes 327712 | tf_op jit(solution)/shard_map/all_to_all | solution.py:82
  366.1 5.3 %scatter_custom_fusion.1 = bf16[256,2560]{1,0:T(8,128)(2,1)} fusion(bf16[256,2560]{1,0:T(8,128)(2,1)} %copy.57, s32[32]{0:T(128)S(1)} %get-tuple-element.53, f32[1,32,5120]{2,1,0:T(8,128)S(1)} %reshape.161, s32[]{:T(128)} %constant.71.clone.1, s32[]{:T(128)S(6)} %select_n.87, bf16[256,2560]{1,0:T(8,128)(2,1)} %param.12, s32[1024]{0:T(1024)S(1)} %pad_clamp_fusion), kind=kCustom, calls=%fused_computation.27 | custom fusion | flops 245760 | bytes 2953732 | tf_op jit(solution)/shard_map/scatter | solution.py:87
  (142 shorter events, 38.4 us)
Async XLA Ops:
  6.5 318.2 %copy-start = (bf16[2560,320]{0,1:T(8,128)(2,1)S(1)}, bf16[2560,320]{0,1:T(8,128)(2,1)}, u32[]{:S(2)}) copy-start(bf16[2560,320]{0,1:T(8,128)(2,1)} %param.15) | copy-start | bytes 4915204
  6.5 7.3 %copy-start.1 = (bf16[256,2560]{1,0:T(8,128)(2,1)S(1)}, bf16[256,2560]{1,0:T(8,128)(2,1)}, u32[]{:S(2)}) copy-start(bf16[256,2560]{1,0:T(8,128)(2,1)} %param.9) | copy-start | bytes 3932164
  6.5 2.6 copy-start.2
  6.5 75.5 %all-gather.6.cloned.1.call-start = ((), (), s32[]{:S(2)}) async-start(), calls=%async_computation.6 | async-start | bytes 2785280 | tf_op jit(solution)/shard_map/all_gather | solution.py:49
  171.5 11.6 %all-to-all-start.2 = ((f32[16,1,640]{2,1,0:T(1,128)}), f32[16,1,640]{2,1,0:T(1,128)S(1)}, u32[]{:S(2)}, u32[]{:S(2)}) async-start(f32[16,1,640]{2,1,0:T(1,128)} %reshape.215), calls=%async_computation.2 | async-start | bytes 81920 | tf_op jit(solution)/shard_map/all_to_all | solution.py:53
  183.1 10.9 %all-to-all-start.1 = ((f32[16,1,640]{2,1,0:T(1,128)}), f32[16,1,640]{2,1,0:T(1,128)S(1)}, u32[]{:S(2)}, u32[]{:S(2)}) async-start(f32[16,1,640]{2,1,0:T(1,128)} %reshape.213), calls=%async_computation.1 | async-start | bytes 81920 | tf_op jit(solution)/shard_map/all_to_all | solution.py:60
  194.0 54.0 %all-to-all-start = ((bf16[20,16,32,128]{3,2,0,1:T(8,128)(2,1)}), bf16[20,16,32,128]{3,2,0,1:T(8,128)(2,1)}, u32[]{:S(2)}, u32[]{:S(2)}) async-start(bf16[20,16,32,128]{3,2,0,1:T(8,128)(2,1)} %copy.18), calls=%async_computation | async-start | bytes 5242880 | tf_op jit(solution)/shard_map/all_to_all | solution.py:68
  198.4 126.3 %all-gather.4.cloned.1.call-start = ((), (), s32[]{:S(2)}) async-start(), calls=%async_computation.4 | async-start | bytes 2785280 | tf_op jit(solution)/shard_map/all_gather | solution.py:78
  253.8 91.7 %all-reduce.2.cloned.1.call-start = ((), (), s32[]{:S(2)}) async-start(), calls=%async_computation.5 | async-start | bytes 786432 | tf_op jit(solution)/shard_map/psum | solution.py:80
  345.5 19.8 %all-to-all-start.3 = ((bf16[16,32,320]{2,1,0:T(8,128)(2,1)}), bf16[16,32,320]{2,1,0:T(8,128)(2,1)S(1)}, u32[]{:S(2)}, u32[]{:S(2)}) async-start(bf16[16,32,320]{2,1,0:T(8,128)(2,1)} %all-reduce.2.cloned.1.call-done), calls=%async_computation.3 | async-start | bytes 786432 | tf_op jit(solution)/shard_map/all_to_all | solution.py:82
Sparse Core Ops, SparseCore 0:
  15.3 66.7 all-gather.5
  253.9 70.6 all-gather.3
  328.5 16.8 all-reduce.1
where the time goes:
time: 380 us; the launch traced here: 378 us
  waiting for transfers between devices  225 us (59%)
  matrix products  66.3 us (17%)
  local copies, waits for them, and re-layouts  27.4 us (7%)
  starting transfers between devices  19 us (5%)
  other arithmetic  13.7 us (4%)
  loops' own time  13.6 us (4%)
  between operations  13.3 us (4%)
    all_gather x1, waiting for transfers between devices, shards(): lax.all_gather(attn, 'seq', axis=0, tiled=True)  70.8 us
    all_gather x1, waiting for transfers between devices, shards(): gathered = lax.all_gather(own_queries, 'seq', axis=0, tiled=True)  66.8 us
    all_to_all x1, waiting for transfers between devices, shards(): lax.all_to_all(for_sending(block_out), 'seq', split_axis=1, concat_axis=1...  46.9 us
    dot_general x20, matrix products, one_head(): jnp.dot(expo.astype(jnp.bfloat16), v_head, preferred_element_type=jnp.flo...  35.6 us
    dot_general x20, matrix products, one_head(): lax.dot_general(q_head, k_head, (((1,), (1,)), ((), ())), preferred_eleme...  23 us
    psum x1, waiting for transfers between devices, shards(): terms = lax.psum(terms.astype(jnp.bfloat16), 'head').astype(jnp.float32)  17.1 us
    another operation x1, loops' own time, local_partials(): return lax.map(one_head, jnp.arange(head_count, dtype=jnp.int32))  13.6 us
    all_to_all x1, waiting for transfers between devices, shards(): lax.all_to_all(terms.astype(jnp.bfloat16), 'seq', split_axis=0, concat_ax...  13 us
  transfers between devices with their start and end apart: 7, of which 7 were waited for; matrix products, arithmetic and copies ran while one was open for 2% of the time, Pallas kernels for 0%

commit v1 on v0

v1 whole, which is shorter than its diff:
```python
import functools
import math

import jax
import jax.numpy as jnp
from jax import lax
from jax.experimental import pallas as pl
from jax.experimental.pallas import tpu as pltpu
from jax.sharding import PartitionSpec as P

HD = 128
TILE = 16
LOG_LANES = 32
F32 = jnp.float32
BF16 = jnp.bfloat16
VMEM = pl.BlockSpec(memory_space=pltpu.VMEM)
LANES_BOTH = (((1,), (1,)), ((), ()))
ROWS_BOTH = (((0,), (0,)), ((), ()))


def iota(shape, dim):
    return lax.broadcasted_iota(jnp.int32, shape, dim).astype(F32)


class Plan:
    def __init__(self, devices, tok_dev, features):
        self.devices = devices
        self.heads = features // HD
        self.cap = tok_dev // 8
        self.total = devices * tok_dev * 11 // 256
        groups = -(-self.total // TILE)
        self.tok = groups * TILE
        self.whole = self.heads // devices
        self.rest = self.heads - self.whole * devices
        self.per_rest = devices // self.rest if self.rest else 0
        self.part = -(-groups // self.per_rest) * TILE if self.rest else 0
        self.rows = self.whole * self.tok + self.part
        self.slices = self.whole + (1 if self.rest else 0)
        self.sent = self.slices * self.cap + 8
        assert self.rows // TILE <= LOG_LANES

    def rest_of(self, device):
        return min(device // self.per_rest, self.rest - 1)

    def head_rows(self, ref, head):
        if head < self.whole * self.devices:
            first = head // self.devices * self.tok
            return ref[head % self.devices, first : first + self.tok, :]
        first = (head - self.whole * self.devices) * self.per_rest
        parts = [ref[first + i, self.whole * self.tok : self.rows, :] for i in range(self.per_rest)]
        return jnp.concatenate(parts, axis=0)[: self.tok]


def own_selection(act_ref, cap):
    tokens = act_ref.shape[1]
    act = act_ref[...].astype(F32)
    before = (iota((tokens, tokens), 0) < iota((tokens, tokens), 1)).astype(BF16)
    many = jnp.broadcast_to(act, (TILE, tokens)).astype(BF16)
    rank = jnp.dot(many, before, preferred_element_type=F32)[0:1]
    rank = jnp.where(act > 0, rank, -1.0)
    return (iota((cap, tokens), 0) == rank).astype(BF16), act


def select_kernel(plan, act_ref, q_ref, out_ref):
    chosen, act = own_selection(act_ref, plan.cap)
    count = jnp.broadcast_to(jnp.sum(act, axis=1, keepdims=True), (8, HD)).astype(BF16)
    own = jnp.dot(chosen, q_ref[...], preferred_element_type=F32).astype(BF16)
    for device in range(plan.devices):
        heads = [i * plan.devices + device for i in range(plan.whole)]
        if plan.rest:
            heads.append(plan.whole * plan.devices + plan.rest_of(device))
        for i, head in enumerate(heads):
            out_ref[device, i * plan.cap : (i + 1) * plan.cap, :] = own[:, head * HD : (head + 1) * HD]
        out_ref[device, plan.slices * plan.cap :, :] = count


def compact_kernel(plan, where_ref, in_ref, out_ref, info_ref):
    devices, cap = plan.devices, plan.cap
    count = jnp.max(in_ref[:, plan.slices * cap :, :].astype(F32), axis=1)
    earlier = (iota((devices, devices), 1) < iota((devices, devices), 0)).astype(BF16)
    offset = jnp.dot(earlier, count.astype(BF16), preferred_element_type=F32)
    info_ref[0] = count
    info_ref[1] = offset
    slots = devices * cap
    place = iota((devices, slots), 1) - iota((devices, slots), 0) * cap
    held = (place >= 0) & (place < jnp.minimum(count[:, 0:1], float(cap)))
    rank = jnp.sum(jnp.where(held, offset[:, 0:1] + place + 1.0, 0.0), axis=0, keepdims=True) - 1.0

    def put(first, rows, base, index):
        pick = (iota((rows, slots), 0) + base == rank).astype(BF16)
        source = in_ref[:, index * cap : (index + 1) * cap, :].reshape(slots, HD)
        packed = jnp.dot(pick, source, preferred_element_type=F32).astype(BF16)
        for device in range(devices):
            out_ref[device, first : first + rows, :] = packed

    for i in range(plan.whole):
        put(i * plan.tok, plan.tok, 0.0, i)
    if plan.rest:
        me = where_ref[0]
        index = me - jnp.minimum(me // plan.per_rest, plan.rest - 1) * plan.per_rest
        put(plan.whole * plan.tok, plan.part, (index * plan.part).astype(F32), plan.whole)


def spread_logs(logs, first, count):
    lane = lax.broadcasted_iota(jnp.int32, (TILE, HD), 1)
    laid = jnp.zeros((TILE, HD), F32)
    for i in range(count):
        laid = jnp.where(lane == first + i, logs[i * TILE : (i + 1) * TILE], laid)
    high = laid.astype(BF16).astype(F32)
    mid = (laid - high).astype(BF16).astype(F32)
    low = (laid - high - mid).astype(BF16).astype(F32)
    return (high + pltpu.roll(mid, LOG_LANES, 1) + pltpu.roll(low, 2 * LOG_LANES, 1)).astype(BF16)


def attention_kernel(plan, q_ref, k_ref, v_ref, out_ref):
    devices, tok, part = plan.devices, plan.tok, plan.part
    inv_root = 1.0 / HD**0.5
    tail = plan.whole * tok

    def attend(query, head):
        columns = pl.ds(pl.multiple_of(head * HD, HD), HD)
        scores = (
            lax.dot_general(query, k_ref[:, columns], LANES_BOTH, preferred_element_type=F32)
            * inv_root
        )
        peak = jnp.max(scores, axis=1, keepdims=True)
        expo = jnp.exp(scores - peak)
        total = jnp.sum(expo, axis=1, keepdims=True)
        block = jnp.dot(expo.astype(BF16), v_ref[:, columns], preferred_element_type=F32)
        return (block / total).astype(BF16), peak + jnp.log(total)

    if plan.rest * plan.per_rest < devices or not plan.whole:
        out_ref[...] = jnp.zeros_like(out_ref)
    for i in range(plan.whole):
        def whole_head(device, carry, i=i):
            result, logs = attend(q_ref[device, i * tok : (i + 1) * tok, :], device + i * devices)
            out_ref[device, i * tok : (i + 1) * tok, :] = result
            laid = spread_logs(logs, i * (tok // TILE), tok // TILE)
            if i:
                laid = out_ref[device, plan.rows :, :] + laid
            out_ref[device, plan.rows :, :] = laid
            return carry

        lax.fori_loop(0, devices, whole_head, 0, unroll=2)

    def rest_head(index, carry):
        first = index * plan.per_rest
        query = jnp.concatenate(
            [q_ref[first + j, tail : plan.rows, :] for j in range(plan.per_rest)], axis=0
        )
        result, logs = attend(query, index + plan.whole * devices)
        for j in range(plan.per_rest):
            mine = slice(j * part, (j + 1) * part)
            out_ref[first + j, tail : plan.rows, :] = result[mine]
            laid = spread_logs(logs[mine], tail // TILE, part // TILE)
            out_ref[first + j, plan.rows :, :] = out_ref[first + j, plan.rows :, :] + laid
        return carry

    if plan.rest:
        lax.fori_loop(0, plan.rest, rest_head, 0)


def combine_kernel(plan, in_ref, out_ref, weight_ref):
    devices, rows = plan.devices, plan.rows

    def logs(device):
        kept = in_ref[device, rows:, :].astype(F32)
        return (
            kept
            + pltpu.roll(kept, HD - LOG_LANES, 1)
            + pltpu.roll(kept, HD - 2 * LOG_LANES, 1)
        )

    top = logs(0)
    for device in range(1, devices):
        top = jnp.maximum(top, logs(device))
    total = jnp.zeros((TILE, HD), F32)
    for device in range(devices):
        weight = jnp.exp(logs(device) - top)
        weight_ref[device] = weight
        total = total + weight
    scale = 1.0 / total

    def add(device, carry):
        weight = weight_ref[device] * scale
        return tuple(
            held
            + weight[:, i : i + 1] * in_ref[device, i * TILE : (i + 1) * TILE, :].astype(F32)
            for i, held in enumerate(carry)
        )

    start = tuple(jnp.zeros((TILE, HD), F32) for _ in range(rows // TILE))
    done = lax.fori_loop(0, devices, add, start, unroll=2)
    for i, held in enumerate(done):
        block = held.astype(BF16)
        for device in range(devices):
            out_ref[device, i * TILE : (i + 1) * TILE, :] = block


def project_kernel(plan, attn_ref, w_ref, info_ref, out_ref):
    devices, cap, tok = plan.devices, plan.cap, plan.tok
    attn = jnp.concatenate([plan.head_rows(attn_ref, h) for h in range(plan.heads)], axis=1)
    proj = lax.dot_general(attn, w_ref[...], LANES_BOTH, preferred_element_type=F32).astype(BF16)
    picks = []
    for device in range(devices):
        place = iota((cap, tok), 0)
        count = info_ref[0, device : device + 1, 0:1]
        offset = info_ref[1, device : device + 1, 0:1]
        picks.append(
            ((iota((cap, tok), 1) - offset == place) & (place < count)).astype(F32).astype(BF16)
        )
    pick = jnp.concatenate(picks, axis=0)
    laid = jnp.dot(pick, proj, preferred_element_type=F32).astype(BF16)
    out_ref[...] = laid.reshape(devices, cap, w_ref.shape[0])


def update_kernel(cap, act_ref, *refs):
    *term_refs, hidden_ref, cached_ref, out_ref = refs
    chosen, _ = own_selection(act_ref, cap)
    mask = lax.dot_general(chosen, jnp.ones((cap, HD), BF16), ROWS_BOTH, preferred_element_type=F32)
    terms = []
    for ref in term_refs:
        for i in range(ref.shape[0]):
            wide = [ref[i, j].astype(F32) for j in range(ref.shape[1])]
            terms.append(jnp.concatenate(wide, axis=1).astype(BF16))
    many = jnp.concatenate([chosen] * len(terms), axis=0)
    summed = lax.dot_general(
        many, jnp.concatenate(terms, axis=0), ROWS_BOTH, preferred_element_type=F32
    )
    updated = (hidden_ref[...].astype(F32) + summed).astype(BF16)
    out_ref[...] = jnp.where(mask[:, 0:1] > 0, updated, cached_ref[...])


def call(kernel, name, out_shape, *args, **options):
    return pl.pallas_call(
        kernel,
        name=name,
        out_shape=out_shape,
        in_specs=options.pop("in_specs", [VMEM] * len(args)),
        out_specs=options.pop("out_specs", jax.tree.map(lambda _: VMEM, out_shape)),
        compiler_params=pltpu.CompilerParams(vmem_limit_bytes=48 << 20),
        **options,
    )(*args)


def exchange(value):
    return lax.all_to_all(value, "seq", split_axis=0, concat_axis=0, tiled=True)


def shards(queries, keys, values, hidden, cached, active, w_out):
    tok_dev, features = queries.shape
    devices, halves = lax.axis_size("seq"), lax.axis_size("head")
    plan = Plan(devices, tok_dev, features)
    cap = plan.cap
    act = active.reshape(1, tok_dev)
    shape = jax.ShapeDtypeStruct
    me = lax.axis_index("seq").astype(jnp.int32).reshape(1)

    sent = call(
        functools.partial(select_kernel, plan), "select",
        shape((devices, plan.sent, HD), BF16), act, queries,
    )
    chunk, info = call(
        functools.partial(compact_kernel, plan), "compact",
        (shape((devices, plan.rows, HD), BF16), shape((2, devices, HD), F32)),
        me, exchange(sent),
        in_specs=[pl.BlockSpec(memory_space=pltpu.SMEM), VMEM],
    )
    partials = call(
        functools.partial(attention_kernel, plan), "attend",
        shape((devices, plan.rows + TILE, HD), BF16), exchange(chunk), keys, values,
    )
    mixed = call(
        functools.partial(combine_kernel, plan), "combine",
        shape((devices, plan.rows, HD), BF16), exchange(partials),
        scratch_shapes=[pltpu.VMEM((devices, TILE, HD), F32)],
    )
    columns = w_out.shape[1]
    terms = call(
        functools.partial(project_kernel, plan), "project",
        shape((devices, cap, columns), BF16), exchange(mixed), w_out.T, info,
    )
    arrived = exchange(terms)

    half = lax.axis_index("head").astype(jnp.int32).reshape(1)
    wide = math.lcm(columns, HD)
    blocks = wide // columns
    steps = features // wide
    if halves == 2:
        other = lax.ppermute(arrived, "head", [(0, 1), (1, 0)])
        term_args = [arrived[None], other[None]]
        term_spec = pl.BlockSpec((1, blocks, cap, columns), lambda i, h: (0, h[0] * steps + i, 0, 0))
    else:
        split = arrived.reshape(halves, devices // halves, cap, columns)
        term_args = [lax.all_to_all(split, "head", split_axis=0, concat_axis=0, tiled=True)]
        term_spec = pl.BlockSpec((halves, blocks, cap, columns), lambda i, h: (0, i, 0, 0))
    column_spec = pl.BlockSpec((tok_dev, wide), lambda i, h: (0, i))

    def update(half_ref, *refs):
        update_kernel(cap, *refs)

    return pl.pallas_call(
        update,
        name="update",
        out_shape=shape((tok_dev, features), BF16),
        grid_spec=pltpu.PrefetchScalarGridSpec(
            num_scalar_prefetch=1,
            grid=(steps,),
            in_specs=[
                pl.BlockSpec((1, tok_dev), lambda i, h: (0, 0)),
                *[term_spec] * len(term_args),
                column_spec,
                column_spec,
            ],
            out_specs=column_spec,
        ),
    )(half, act, *term_args, hidden, cached)


def solution(mesh):
    placed = (
        P("seq", "head"),
        P("seq", "head"),
        P("seq", "head"),
        P("seq", "head"),
        P("seq", "head"),
        P("seq"),
        P("head", "seq"),
    )
    return jax.shard_map(
        shards, mesh=mesh, in_specs=placed, out_specs=P("seq", "head"), check_vma=False
    )
```

time: 380 us -> 137 us (0.36)
  waiting for transfers between devices: 225 us -> 12.4 us
  blocking collectives: 0 us -> 96.1 us
  matrix products: 66.3 us -> 0 us
  local copies, waits for them, and re-layouts: 27.4 us -> 2.75 us
  Pallas kernels: 0 us -> 16.5 us
  other arithmetic: 13.7 us -> 0 us
  loops' own time: 13.6 us -> 0 us
  between operations: 13.3 us -> 0.05 us
  starting transfers between devices: 19 us -> 8.61 us
    all_gather x2 -> x0, waiting for transfers between devices: 138 us -> none  [the longest x1 70.8 us: shards(): lax.all_gather(attn, 'seq', axis=0, tiled=True)]
    all_to_all x0 -> x4, blocking collectives: none -> 96.1 us  [exchange(): return lax.all_to_all(value, 'seq', split_axis=0, concat_axis=0, tiled=True)]
    dot_general x42 -> x0, matrix products: 66.3 us -> none  [the longest x20 35.6 us: one_head(): jnp.dot(expo.astype(jnp.bfloat16), v_head, preferred_element_type=jnp.flo...]
    all_to_all x4 -> x1, waiting for transfers between devices: 69.9 us -> 10.7 us  [exchange(): return lax.all_to_all(value, 'seq', split_axis=0, concat_axis=0, tiled=True)]
    psum x1 -> x0, waiting for transfers between devices: 17.1 us -> none  [shards(): terms = lax.psum(terms.astype(jnp.bfloat16), 'head').astype(jnp.float32)]
    pallas_call x0 -> x6, Pallas kernels: none -> 16.5 us  [the longest x5 11.8 us: call(): pl.pallas_call(kernel, name=name, out_shape=out_shape, in_specs=options.p...]
    another operation x1 -> x0, loops' own time: 13.6 us -> none  [local_partials(): return lax.map(one_head, jnp.arange(head_count, dtype=jnp.int32))]
    dynamic_slice x20 -> x0, local copies, waits for them, and re-layouts: 12.3 us -> none  [local_partials(): return lax.map(one_head, jnp.arange(head_count, dtype=jnp.int32))]
  transfers between devices with their start and end apart: 7 -> 2, of which waited for: 7 -> 2; matrix products, arithmetic and copies ran while one was open for 2% -> 0% of each run, Pallas kernels for 0% -> 0%
where the time goes in v1:
time: 137 us; the launch traced here: 136 us
  blocking collectives  96.1 us (70%)
  Pallas kernels  16.5 us (12%)
  waiting for transfers between devices  12.4 us (9%)
  starting transfers between devices  8.61 us (6%)
  local copies, waits for them, and re-layouts  2.75 us (2%)
    all_to_all x4, blocking collectives, exchange(): return lax.all_to_all(value, 'seq', split_axis=0, concat_axis=0, tiled=True)  96.1 us
    pallas_call x5, Pallas kernels, call(): pl.pallas_call(kernel, name=name, out_shape=out_shape, in_specs=options.p...  11.8 us
    all_to_all x1, waiting for transfers between devices, exchange(): return lax.all_to_all(value, 'seq', split_axis=0, concat_axis=0, tiled=True)  10.7 us
    all_to_all x1, starting transfers between devices, exchange(): return lax.all_to_all(value, 'seq', split_axis=0, concat_axis=0, tiled=True)  8.6 us
    pallas_call x1, Pallas kernels, shards(): pl.pallas_call(update, name='update', out_shape=shape((tok_dev, features)...  4.76 us
    unnamed x14, local copies, waits for them, and re-layouts  2.75 us
  transfers between devices with their start and end apart: 2, of which 2 were waited for; matrix products, arithmetic and copies ran while one was open for 0% of the time, Pallas kernels for 0%

profile of v1, /device:TPU:0, one launch (start us, length us, event | category | flops | bytes accessed | tf_op | source)
XLA Modules:
  0.0 136.4 jit_solution(14054596716779248425)
XLA Ops:
  0.0 0.0 copy-start.1
  0.0 1.3 copy-done.1
  1.3 0.0 copy-start.4
  1.3 0.7 copy-done.4
  2.0 1.2 select.1
  3.2 0.0 copy-start.2
  3.2 0.0 copy-start.3
  3.2 8.6 %all-to-all-start = ((bf16[16,72,128]{2,1,0:T(8,128)(2,1)}), bf16[16,72,128]{2,1,0:T(8,128)(2,1)S(1)}, u32[]{:S(2)}, u32[]{:S(2)}) async-start(bf16[16,72,128]{2,1,0:T(8,128)(2,1)} %select.1), calls=%async_computation | async-start | bytes 589824 | tf_op jit(solution)/shard_map/all_to_all | solution.py:247
  11.8 10.7 %all-to-all-done.in_ref = bf16[16,72,128]{2,1,0:T(8,128)(2,1)S(1)} async-done(((bf16[16,72,128]{2,1,0:T(8,128)(2,1)}), bf16[16,72,128]{2,1,0:T(8,128)(2,1)S(1)}, u32[]{:S(2)}, u32[]{:S(2)}) %all-to-all-start) | async-done | bytes 294944 | tf_op jit(solution)/shard_map/all_to_all | solution.py:247
  22.5 0.4 compact.1
  22.9 26.4 %all_to_all.25.q_ref = bf16[16,224,128]{2,1,0:T(8,128)(2,1)S(1)} all-to-all(bf16[16,224,128]{2,1,0:T(8,128)(2,1)S(1)} %get-tuple-element.7), channel_id=1, replica_groups=mesh['seq'=16,'head'=2] {'seq'}, dimensions={0} | all-to-all | bytes 1835008 | tf_op jit(solution)/shard_map/all_to_all | solution.py:247
  49.3 0.0 copy-done.2
  49.3 0.0 copy-done.3
  49.4 7.4 %attend.1 = bf16[16,240,128]{2,1,0:T(8,128)(2,1)S(1)} custom-call(bf16[16,224,128]{2,1,0:T(8,128)(2,1)S(1)} %all_to_all.25.q_ref, bf16[256,2560]{1,0:T(8,128)(2,1)S(1)} %copy-done.2, bf16[256,2560]{1,0:T(8,128)(2,1)S(1)} %copy-done.3), custom_call_target="tpu_custom_call" | custom-call | tf_op jit(solution)/shard_map/attend/pallas_call | solution.py:235
  56.8 27.8 %all_to_all.26.in_ref = bf16[16,240,128]{2,1,0:T(8,128)(2,1)S(1)} all-to-all(bf16[16,240,128]{2,1,0:T(8,128)(2,1)S(1)} %attend.1), channel_id=1, replica_groups=mesh['seq'=16,'head'=2] {'seq'}, dimensions={0} | all-to-all | bytes 1966080 | tf_op jit(solution)/shard_map/all_to_all | solution.py:247
  84.6 1.5 %combine.1 = bf16[16,224,128]{2,1,0:T(8,128)(2,1)S(1)} custom-call(bf16[16,240,128]{2,1,0:T(8,128)(2,1)S(1)} %all_to_all.26.in_ref), custom_call_target="tpu_custom_call" | custom-call | tf_op jit(solution)/shard_map/combine/pallas_call | solution.py:235
  86.1 0.0 copy-start
  86.1 26.7 %all_to_all.27.attn_ref = bf16[16,224,128]{2,1,0:T(8,128)(2,1)S(1)} all-to-all(bf16[16,224,128]{2,1,0:T(8,128)(2,1)S(1)} %combine.1), channel_id=1, replica_groups=mesh['seq'=16,'head'=2] {'seq'}, dimensions={0} | all-to-all | bytes 1835008 | tf_op jit(solution)/shard_map/all_to_all | solution.py:247
  112.8 0.0 copy-done
  112.8 1.3 project.1
  114.1 15.1 %all_to_all.28 = bf16[16,32,320]{2,1,0:T(8,128)(2,1)S(1)} all-to-all(bf16[16,32,320]{2,1,0:T(8,128)(2,1)S(1)} %project.1), channel_id=1, replica_groups=mesh['seq'=16,'head'=2] {'seq'}, dimensions={0} | all-to-all | bytes 655360 | tf_op jit(solution)/shard_map/all_to_all | solution.py:247
  129.2 0.0 copy-start.5
  129.2 0.0 collective-permute-start
  129.2 1.7 %collective-permute-done = bf16[16,32,320]{2,1,0:T(8,128)(2,1)S(1)} collective-permute-done((bf16[16,32,320]{2,1,0:T(8,128)(2,1)S(1)}, bf16[16,32,320]{2,1,0:T(8,128)(2,1)S(1)}, u32[]{:S(2)}, u32[]{:S(2)}) %collective-permute-start) | collective-permute-done | bytes 327712 | tf_op jit(solution)/shard_map/ppermute | solution.py:290
  130.9 0.0 copy-start.6
  130.9 0.0 copy-done.5
  130.9 0.7 copy-done.6
  131.7 4.8 %update.1 = bf16[256,2560]{1,0:T(8,128)(2,1)} custom-call(s32[1]{0:T(128)} %bitcast.half_ref, s32[1,256]{1,0:T(1,128)} %bitcast.7, bf16[1,16,32,320]{3,2,1,0:T(8,128)(2,1)} %bitcast.9, bf16[1,16,32,320]{3,2,1,0:T(8,128)(2,1)} %bitcast.10, bf16[256,2560]{1,0:T(8,128)(2,1)} %refs_3_.1, bf16[256,2560]{1,0:T(8,128)(2,1)} %refs_4_.1), custom_call_target="tpu_custom_call" | custom-call | tf_op jit(solution)/shard_map/update/pallas_call | solution.py:302
Async XLA Ops:
  0.0 1.3 copy-start.1
  1.3 0.7 copy-start.4
  3.2 46.1 %copy-start.2 = (bf16[256,2560]{1,0:T(8,128)(2,1)S(1)}, bf16[256,2560]{1,0:T(8,128)(2,1)}, u32[]{:S(2)}) copy-start(bf16[256,2560]{1,0:T(8,128)(2,1)} %k_ref.1) | copy-start | bytes 3932164
  3.2 46.1 %copy-start.3 = (bf16[256,2560]{1,0:T(8,128)(2,1)S(1)}, bf16[256,2560]{1,0:T(8,128)(2,1)}, u32[]{:S(2)}) copy-start(bf16[256,2560]{1,0:T(8,128)(2,1)} %v_ref.1) | copy-start | bytes 3932164
  3.2 19.3 %all-to-all-start = ((bf16[16,72,128]{2,1,0:T(8,128)(2,1)}), bf16[16,72,128]{2,1,0:T(8,128)(2,1)S(1)}, u32[]{:S(2)}, u32[]{:S(2)}) async-start(bf16[16,72,128]{2,1,0:T(8,128)(2,1)} %select.1), calls=%async_computation | async-start | bytes 589824 | tf_op jit(solution)/shard_map/all_to_all | solution.py:247
  86.1 26.7 %copy-start = (bf16[2560,320]{0,1:T(8,128)(2,1)S(1)}, bf16[2560,320]{0,1:T(8,128)(2,1)}, u32[]{:S(2)}) copy-start(bf16[2560,320]{0,1:T(8,128)(2,1)} %param.13) | copy-start | bytes 4915204
  129.2 1.7 %copy-start.5 = (bf16[16,32,320]{2,1,0:T(8,128)(2,1)}, bf16[16,32,320]{2,1,0:T(8,128)(2,1)S(1)}, u32[]{:S(2)}) copy-start(bf16[16,32,320]{2,1,0:T(8,128)(2,1)S(1)} %all_to_all.28) | copy-start | bytes 983044
  129.2 1.7 %collective-permute-start = (bf16[16,32,320]{2,1,0:T(8,128)(2,1)S(1)}, bf16[16,32,320]{2,1,0:T(8,128)(2,1)S(1)}, u32[]{:S(2)}, u32[]{:S(2)}) collective-permute-start(bf16[16,32,320]{2,1,0:T(8,128)(2,1)S(1)} %all_to_all.28), channel_id=1, source_target_pairs={{0,1},{1,0},{2,3},{3,2},{4,5},{5,4},{6,7},{7,6},{8,9},{9,8},{10,11... | collective-permute-start | bytes 983048 | tf_op jit(solution)/shard_map/ppermute | solution.py:290
  130.9 0.7 copy-start.6

commit v2 on v1

v2 whole, which is shorter than its diff:
```python
import functools
import math

import jax
import jax.numpy as jnp
from jax import lax
from jax.experimental import pallas as pl
from jax.experimental.pallas import tpu as pltpu
from jax.sharding import PartitionSpec as P

HD = 128
TILE = 16
QUAD = 4
LOG_LANES = 32
F32 = jnp.float32
BF16 = jnp.bfloat16
VMEM = pl.BlockSpec(memory_space=pltpu.VMEM)
SMEM = pl.BlockSpec(memory_space=pltpu.SMEM)
LANES_BOTH = (((1,), (1,)), ((), ()))
ROWS_BOTH = (((0,), (0,)), ((), ()))


def iota(shape, dim):
    return lax.broadcasted_iota(jnp.int32, shape, dim).astype(F32)


class Plan:
    def __init__(self, devices, tok_dev, features):
        assert devices % (2 * QUAD) == 0
        self.devices = devices
        self.line = devices // QUAD
        self.heads = features // HD
        self.own_heads = -(-self.heads // QUAD)
        self.cap = tok_dev // 8
        self.total = devices * tok_dev * 11 // 256
        groups = -(-self.total // TILE)
        self.tok = groups * TILE
        self.tiles = -(-self.own_heads * groups // self.line)
        self.rows = self.tiles * TILE
        self.half = self.line // 2 * self.rows
        assert self.tiles <= LOG_LANES

    def head_at(self, index, quad):
        return jnp.minimum(index * QUAD + quad, self.heads - 1)

    def head_rows(self, refs, index):
        first, last = index * self.tok, (index + 1) * self.tok
        parts = []
        for i, ref in enumerate(refs):
            low, high = max(first - i * self.half, 0), min(last - i * self.half, self.half)
            if low < high:
                parts.append(ref[low:high, :])
        return parts[0] if len(parts) == 1 else jnp.concatenate(parts, axis=0)

    def put_rows(self, refs, index, block):
        first, last = index * self.tok, (index + 1) * self.tok
        for i, ref in enumerate(refs):
            low, high = max(first, i * self.half), min(last, (i + 1) * self.half)
            if low < high:
                ref[low - i * self.half : high - i * self.half, :] = block[low - first : high - first]


def own_selection(act_ref, cap):
    tokens = act_ref.shape[1]
    act = act_ref[...].astype(F32)
    before = (iota((tokens, tokens), 0) < iota((tokens, tokens), 1)).astype(BF16)
    many = jnp.broadcast_to(act, (TILE, tokens)).astype(BF16)
    rank = jnp.dot(many, before, preferred_element_type=F32)[0:1]
    rank = jnp.where(act > 0, rank, -1.0)
    return (iota((cap, tokens), 0) == rank).astype(BF16), act


def select_kernel(plan, act_ref, q_ref, out_ref):
    chosen, act = own_selection(act_ref, plan.cap)
    count = jnp.broadcast_to(jnp.sum(act, axis=1, keepdims=True), (8, HD)).astype(BF16)
    own = jnp.dot(chosen, q_ref[...], preferred_element_type=F32).astype(BF16)
    for device in range(plan.devices):
        for i in range(plan.own_heads):
            head = min(i * QUAD + device % QUAD, plan.heads - 1)
            out_ref[device, i * plan.cap : (i + 1) * plan.cap, :] = own[:, head * HD : (head + 1) * HD]
        out_ref[device, plan.own_heads * plan.cap :, :] = count


def compact_kernel(plan, in_ref, low_ref, high_ref, info_ref):
    devices, cap = plan.devices, plan.cap
    count = jnp.max(in_ref[:, plan.own_heads * cap :, :].astype(F32), axis=1)
    earlier = (iota((devices, devices), 1) < iota((devices, devices), 0)).astype(BF16)
    offset = jnp.dot(earlier, count.astype(BF16), preferred_element_type=F32)
    info_ref[0] = count
    info_ref[1] = offset
    slots = devices * cap
    place = iota((devices, slots), 1) - iota((devices, slots), 0) * cap
    held = (place >= 0) & (place < jnp.minimum(count[:, 0:1], float(cap)))
    rank = jnp.sum(jnp.where(held, offset[:, 0:1] + place + 1.0, 0.0), axis=0, keepdims=True) - 1.0
    pick = (iota((plan.tok, slots), 0) == rank).astype(BF16)
    rest = plan.line * plan.rows - plan.own_heads * plan.tok
    if rest:
        high_ref[plan.half - rest :, :] = jnp.zeros((rest, HD), BF16)
    for i in range(plan.own_heads):
        source = in_ref[:, i * cap : (i + 1) * cap, :].reshape(slots, HD)
        packed = jnp.dot(pick, source, preferred_element_type=F32).astype(BF16)
        plan.put_rows((low_ref, high_ref), i, packed)


def pack_logs(logs):
    high = logs.astype(BF16).astype(F32)
    mid = (logs - high).astype(BF16).astype(F32)
    low = (logs - high - mid).astype(BF16).astype(F32)
    return (high + pltpu.roll(mid, LOG_LANES, 1) + pltpu.roll(low, 2 * LOG_LANES, 1)).astype(BF16)


def unpack_logs(packed):
    kept = packed.astype(F32)
    return kept + pltpu.roll(kept, HD - LOG_LANES, 1) + pltpu.roll(kept, HD - 2 * LOG_LANES, 1)


def attention_kernel(plan, step, where_ref, low_ref, high_ref, k_ref, v_ref, out_ref):
    inv_root = 1.0 / HD**0.5
    quad = (where_ref[0] & (QUAD - 1)) ^ step
    lane = lax.broadcasted_iota(jnp.int32, (TILE, HD), 1)
    laid = [jnp.zeros((TILE, HD), F32) for _ in range(plan.line)]
    rest = plan.line * plan.rows - plan.own_heads * plan.tok
    if rest:
        first = plan.own_heads * plan.tok
        for chunk in range(first // plan.rows, plan.line):
            low = max(first - chunk * plan.rows, 0)
            out_ref[chunk, low : plan.rows, :] = jnp.zeros((plan.rows - low, HD), BF16)
    for i in range(plan.own_heads):
        columns = pl.ds(pl.multiple_of(plan.head_at(i, quad) * HD, HD), HD)
        query = plan.head_rows((low_ref, high_ref), i)
        scores = (
            lax.dot_general(query, k_ref[:, columns], LANES_BOTH, preferred_element_type=F32)
            * inv_root
        )
        peak = jnp.max(scores, axis=1, keepdims=True)
        expo = jnp.exp(scores - peak)
        total = jnp.sum(expo, axis=1, keepdims=True)
        block = jnp.dot(expo.astype(BF16), v_ref[:, columns], preferred_element_type=F32)
        block = (block / total).astype(BF16)
        logs = peak + jnp.log(total)
        for tile in range(plan.tok // TILE):
            chunk, place = divmod(i * (plan.tok // TILE) + tile, plan.tiles)
            mine = slice(tile * TILE, (tile + 1) * TILE)
            out_ref[chunk, place * TILE : (place + 1) * TILE, :] = block[mine]
            laid[chunk] = jnp.where(lane == place, logs[mine], laid[chunk])
    for chunk in range(plan.line):
        out_ref[chunk, plan.rows :, :] = pack_logs(laid[chunk])


def merge(plan, parts, out_ref, keep_logs):
    rows = plan.rows
    logs = [unpack_logs(part[rows:, :]) for part in parts]
    top = functools.reduce(jnp.maximum, logs)
    weights = [jnp.exp(log - top) for log in logs]
    total = functools.reduce(jnp.add, weights)
    scale = 1.0 / total
    weights = [weight * scale for weight in weights]
    for tile in range(plan.tiles):
        mine = slice(tile * TILE, (tile + 1) * TILE)
        mixed = functools.reduce(
            jnp.add,
            [w[:, tile : tile + 1] * part[mine, :].astype(F32) for w, part in zip(weights, parts)],
        )
        out_ref[mine, :] = mixed.astype(BF16)
    if keep_logs:
        lane = lax.broadcasted_iota(jnp.int32, (TILE, HD), 1)
        out_ref[rows:, :] = pack_logs(jnp.where(lane < LOG_LANES, top + jnp.log(total), 0.0))


def quad_kernel(plan, where_ref, *refs):
    parts, outs = refs[:QUAD], refs[QUAD:]
    line = where_ref[0] // QUAD
    for step, out_ref in enumerate(outs):
        merge(plan, [part.at[line ^ step] for part in parts], out_ref, True)


def line_kernel(plan, *refs):
    merge(plan, refs[:-1], refs[-1], False)


def stack_kernel(plan, where_ref, *refs):
    *parts, low_ref, high_ref, held_ref = refs
    line = where_ref[0] // QUAD
    for step, part in enumerate(parts):
        held_ref[line ^ step] = part[...]
    for i in range(plan.line // 2):
        low_ref[i * plan.rows : (i + 1) * plan.rows, :] = held_ref[i]
        high_ref[i * plan.rows : (i + 1) * plan.rows, :] = held_ref[plan.line // 2 + i]


def project_group(plan, quad, refs, w_ref):
    sides, weights = [], []
    for i in range(plan.own_heads):
        block = plan.head_rows(refs, i)
        if plan.own_heads * QUAD != plan.heads:
            block = jnp.where(i * QUAD + quad < plan.heads, block, jnp.zeros_like(block))
        sides.append(block)
        columns = pl.ds(pl.multiple_of(plan.head_at(i, quad) * HD, HD), HD)
        weights.append(w_ref[:, columns])
    return lax.dot_general(
        jnp.concatenate(sides, axis=1),
        jnp.concatenate(weights, axis=1),
        LANES_BOTH,
        preferred_element_type=F32,
    )


def project_kernel(plan, steps, where_ref, w_ref, *refs):
    *refs, out_ref = refs
    total = None
    if len(refs) % 2:
        *refs, sum_ref = refs
        total = sum_ref[...]
    for i, step in enumerate(steps):
        quad = (where_ref[0] & (QUAD - 1)) ^ step
        term = project_group(plan, quad, refs[2 * i : 2 * i + 2], w_ref)
        total = term if total is None else total + term
    out_ref[...] = total


def place_kernel(plan, step, where_ref, w_ref, low_ref, high_ref, sum_ref, info_ref, out_ref):
    devices, cap, tok = plan.devices, plan.cap, plan.tok
    quad = (where_ref[0] & (QUAD - 1)) ^ step
    proj = sum_ref[...] + project_group(plan, quad, (low_ref, high_ref), w_ref)
    picks = []
    for device in range(devices):
        place = iota((cap, tok), 0)
        count = info_ref[0, device : device + 1, 0:1]
        offset = info_ref[1, device : device + 1, 0:1]
        picks.append(
            ((iota((cap, tok), 1) - offset == place) & (place < count)).astype(F32).astype(BF16)
        )
    pick = jnp.concatenate(picks, axis=0)
    laid = jnp.dot(pick, proj.astype(BF16), preferred_element_type=F32).astype(BF16)
    out_ref[...] = laid.reshape(devices, cap, w_ref.shape[0])


def update_kernel(cap, act_ref, *refs):
    *term_refs, hidden_ref, cached_ref, out_ref = refs
    chosen, _ = own_selection(act_ref, cap)
    mask = lax.dot_general(chosen, jnp.ones((cap, HD), BF16), ROWS_BOTH, preferred_element_type=F32)
    terms = []
    for ref in term_refs:
        for i in range(ref.shape[0]):
            wide = [ref[i, j].astype(F32) for j in range(ref.shape[1])]
            terms.append(jnp.concatenate(wide, axis=1).astype(BF16))
    many = jnp.concatenate([chosen] * len(terms), axis=0)
    summed = lax.dot_general(
        many, jnp.concatenate(terms, axis=0), ROWS_BOTH, preferred_element_type=F32
    )
    updated = (hidden_ref[...].astype(F32) + summed).astype(BF16)
    out_ref[...] = jnp.where(mask[:, 0:1] > 0, updated, cached_ref[...])


def shape(*dims, dtype=BF16):
    return jax.ShapeDtypeStruct(dims, dtype)


def call(kernel, name, out_shape, *args, cost=None, **options):
    return pl.pallas_call(
        kernel,
        name=name,
        out_shape=out_shape,
        in_specs=[SMEM if a.dtype == jnp.int32 and a.ndim == 1 else VMEM for a in args],
        out_specs=jax.tree.map(lambda _: VMEM, out_shape),
        compiler_params=pltpu.CompilerParams(vmem_limit_bytes=32 << 20),
        cost_estimate=cost,
        **options,
    )(*args)


def exchange(value):
    return lax.all_to_all(value, "seq", split_axis=0, concat_axis=0, tiled=True)


def shift(value, mask):
    pairs = [(i, i ^ mask) for i in range(lax.axis_size("seq"))]
    return lax.ppermute(value, "seq", pairs)


def quad_gather(low, high):
    x_low, y_high = shift(low, 1), shift(high, 2)
    x_high, y_low = shift(high, 1), shift(low, 2)
    return [(low, high), (x_low, x_high), (y_low, y_high), (shift(x_low, 2), shift(y_high, 1))]


def shards(queries, keys, values, hidden, cached, active, w_out):
    tok_dev, features = queries.shape
    devices, halves = lax.axis_size("seq"), lax.axis_size("head")
    plan = Plan(devices, tok_dev, features)
    cap, columns = plan.cap, w_out.shape[1]
    act = active.reshape(1, tok_dev)
    me = lax.axis_index("seq").astype(jnp.int32).reshape(1)
    halves_shape = (shape(plan.half, HD), shape(plan.half, HD))

    sent = call(
        functools.partial(select_kernel, plan), "select",
        shape(devices, plan.own_heads * cap + 8, HD), act, queries,
    )
    low, high, info = call(
        functools.partial(compact_kernel, plan), "compact",
        (*halves_shape, shape(2, devices, HD, dtype=F32)), exchange(sent),
    )
    scored = plan.own_heads * plan.tok * tok_dev
    cost = pl.CostEstimate(
        flops=4 * scored * HD, transcendentals=scored, bytes_accessed=4 * tok_dev * HD * plan.own_heads
    )
    partials = []
    for step, (a, b) in enumerate(quad_gather(low, high)):
        part = call(
            functools.partial(attention_kernel, plan, step), f"attend_{step}",
            shape(plan.line, plan.rows + TILE, HD), me, a, b, keys, values, cost=cost,
        )
        partials.append(shift(part, step) if step else part)
    sums = call(
        functools.partial(quad_kernel, plan), "merge_quad",
        tuple(shape(plan.rows + TILE, HD) for _ in range(plan.line)), me, *partials,
    )
    arrived = [shift(part, step * QUAD) if step else part for step, part in enumerate(sums)]
    chunk = call(functools.partial(line_kernel, plan), "merge_line", shape(plan.rows, HD), *arrived)
    line = [shift(chunk, step * QUAD) if step else chunk for step in range(plan.line)]
    low, high = call(
        functools.partial(stack_kernel, plan), "stack", halves_shape, me, *line,
        scratch_shapes=[pltpu.VMEM((plan.line, plan.rows, HD), BF16)],
    )
    w_rows = w_out.T
    cost = pl.CostEstimate(
        flops=2 * plan.own_heads * plan.tok * HD * columns,
        transcendentals=0,
        bytes_accessed=2 * plan.own_heads * HD * columns,
    )
    groups = quad_gather(low, high)
    proj = None
    for step in range(QUAD - 1):
        extra = () if proj is None else (proj,)
        proj = call(
            functools.partial(project_kernel, plan, (step,)), f"project_{step}",
            shape(plan.tok, columns, dtype=F32), me, w_rows, *groups[step], *extra, cost=cost,
        )
    terms = call(
        functools.partial(place_kernel, plan, QUAD - 1), "place",
        shape(devices, cap, columns), me, w_rows, *groups[QUAD - 1], proj, info,
    )
    arrived = exchange(terms)

    half = lax.axis_index("head").astype(jnp.int32).reshape(1)
    wide = math.lcm(columns, HD)
    blocks = wide // columns
    steps = features // wide
    if halves == 2:
        other = lax.ppermute(arrived, "head", [(0, 1), (1, 0)])
        term_args = [arrived[None], other[None]]
        term_spec = pl.BlockSpec((1, blocks, cap, columns), lambda i, h: (0, h[0] * steps + i, 0, 0))
    else:
        split = arrived.reshape(halves, devices // halves, cap, columns)
        term_args = [lax.all_to_all(split, "head", split_axis=0, concat_axis=0, tiled=True)]
        term_spec = pl.BlockSpec((halves, blocks, cap, columns), lambda i, h: (0, i, 0, 0))
    column_spec = pl.BlockSpec((tok_dev, wide), lambda i, h: (0, i))

    def update(half_ref, *refs):
        update_kernel(cap, *refs)

    return pl.pallas_call(
        update,
        name="update",
        out_shape=shape(tok_dev, features),
        grid_spec=pltpu.PrefetchScalarGridSpec(
            num_scalar_prefetch=1,
            grid=(steps,),
            in_specs=[
                pl.BlockSpec((1, tok_dev), lambda i, h: (0, 0)),
                *[term_spec] * len(term_args),
                column_spec,
                column_spec,
            ],
            out_specs=column_spec,
        ),
    )(half, act, *term_args, hidden, cached)


def solution(mesh):
    placed = (
        P("seq", "head"),
        P("seq", "head"),
        P("seq", "head"),
        P("seq", "head"),
        P("seq", "head"),
        P("seq"),
        P("head", "seq"),
    )
    return jax.shard_map(
        shards, mesh=mesh, in_specs=placed, out_specs=P("seq", "head"), check_vma=False
    )
```

time: 137 us -> 105 us (0.77)
  blocking collectives: 96.1 us -> 41.8 us
  starting transfers between devices: 8.61 us -> 25.5 us
  waiting for transfers between devices: 12.4 us -> 21.7 us
  Pallas kernels: 16.5 us -> 12.6 us
    all_to_all x4 -> x2, blocking collectives: 96.1 us -> 41.8 us  [exchange(): return lax.all_to_all(value, 'seq', split_axis=0, concat_axis=0, tiled=True)]
    ppermute x0 -> x21, starting transfers between devices: none -> 25.5 us  [shift(): return lax.ppermute(value, 'seq', pairs)]
    ppermute x0 -> x21, waiting for transfers between devices: none -> 20 us  [shift(): return lax.ppermute(value, 'seq', pairs)]
    all_to_all x1 -> x0, waiting for transfers between devices: 10.7 us -> none  [exchange(): return lax.all_to_all(value, 'seq', split_axis=0, concat_axis=0, tiled=True)]
    all_to_all x1 -> x0, starting transfers between devices: 8.6 us -> none  [exchange(): return lax.all_to_all(value, 'seq', split_axis=0, concat_axis=0, tiled=True)]
    pallas_call x6 -> x14, Pallas kernels: 16.5 us -> 12.6 us  [the longest x13 7.79 us: call(): pl.pallas_call(kernel, name=name, out_shape=out_shape, in_specs=[SMEM if...]
  transfers between devices with their start and end apart: 2 -> 22, of which waited for: 2 -> 16; matrix products, arithmetic and copies ran while one was open for 0% -> 0% of each run, Pallas kernels for 0% -> 4%
where the time goes in v2:
time: 105 us; the launch traced here: 104 us
  blocking collectives  41.8 us (40%)
  starting transfers between devices  25.5 us (24%)
  waiting for transfers between devices  21.7 us (21%)
  Pallas kernels  12.6 us (12%)
  local copies, waits for them, and re-layouts  2.77 us (3%)
    all_to_all x2, blocking collectives, exchange(): return lax.all_to_all(value, 'seq', split_axis=0, concat_axis=0, tiled=True)  41.8 us
    ppermute x21, starting transfers between devices, shift(): return lax.ppermute(value, 'seq', pairs)  25.5 us
    ppermute x21, waiting for transfers between devices, shift(): return lax.ppermute(value, 'seq', pairs)  20 us
    pallas_call x13, Pallas kernels, call(): pl.pallas_call(kernel, name=name, out_shape=out_shape, in_specs=[SMEM if...  7.79 us
    pallas_call x1, Pallas kernels, shards(): pl.pallas_call(update, name='update', out_shape=shape(tok_dev, features),...  4.76 us
    unnamed x14, local copies, waits for them, and re-layouts  2.77 us
  transfers between devices with their start and end apart: 22, of which 16 were waited for; matrix products, arithmetic and copies ran while one was open for 0% of the time, Pallas kernels for 4%

profile of v2, /device:TPU:0, one launch (start us, length us, event | category | flops | bytes accessed | tf_op | source)
XLA Modules:
  0.0 104.4 jit_solution(9621807221507919825)
XLA Ops:
  0.0 1.3 %copy-done.3 = bf16[256,2560]{1,0:T(8,128)(2,1)S(1)} copy-done((bf16[256,2560]{1,0:T(8,128)(2,1)S(1)}, bf16[256,2560]{1,0:T(8,128)(2,1)}, u32[]{:S(2)}) %copy-start.3) | copy-done | bytes 1310744
  1.3 0.7 copy-done.4
  2.0 0.5 select.1
  2.5 27.6 %all_to_all.10.in_ref = bf16[16,168,128]{2,1,0:T(8,128)(2,1)S(1)} all-to-all(bf16[16,168,128]{2,1,0:T(8,128)(2,1)S(1)} %select.1), channel_id=1, replica_groups=mesh['seq'=16,'head'=2] {'seq'}, dimensions={0} | all-to-all | bytes 1376256 | tf_op jit(solution)/shard_map/all_to_all | solution.py:273
  30.1 0.6 compact.1
  30.7 0.6 collective-permute-start
  31.4 0.7 collective-permute-start.4
  32.0 1.4 %collective-permute-start.3 = (bf16[448,128]{1,0:T(8,128)(2,1)S(1)}, bf16[448,128]{1,0:T(8,128)(2,1)S(1)}, u32[]{:S(2)}, u32[]{:S(2)}) collective-permute-start(bf16[448,128]{1,0:T(8,128)(2,1)S(1)} %get-tuple-element.14.low_ref), channel_id=1, source_target_pairs={{0,4},{2,6},{4,0},{6,2},{8,12},{10,14},{12,8},{14,10},{16,20},{18,... | collective-permute-start | bytes 344072 | tf_op jit(solution)/shard_map/ppermute | solution.py:278
  33.4 1.5 %collective-permute-start.1 = (bf16[448,128]{1,0:T(8,128)(2,1)S(1)}, bf16[448,128]{1,0:T(8,128)(2,1)S(1)}, u32[]{:S(2)}, u32[]{:S(2)}) collective-permute-start(bf16[448,128]{1,0:T(8,128)(2,1)S(1)} %get-tuple-element.15.high_ref), channel_id=1, source_target_pairs={{0,2},{2,0},{4,6},{6,4},{8,10},{10,8},{12,14},{14,12},{16,18},{18,... | collective-permute-start | bytes 344072 | tf_op jit(solution)/shard_map/ppermute | solution.py:278
  34.8 1.2 %collective-permute-done.low_ref = bf16[448,128]{1,0:T(8,128)(2,1)S(1)} collective-permute-done((bf16[448,128]{1,0:T(8,128)(2,1)S(1)}, bf16[448,128]{1,0:T(8,128)(2,1)S(1)}, u32[]{:S(2)}, u32[]{:S(2)}) %collective-permute-start) | collective-permute-done | bytes 114720 | tf_op jit(solution)/shard_map/ppermute | solution.py:278
  36.1 0.8 collective-permute-start.6
  36.9 1.7 %collective-permute-start.7 = (bf16[448,128]{1,0:T(8,128)(2,1)S(1)}, bf16[448,128]{1,0:T(8,128)(2,1)S(1)}, u32[]{:S(2)}, u32[]{:S(2)}) collective-permute-start(bf16[448,128]{1,0:T(8,128)(2,1)S(1)} %collective-permute-done.4.high_ref), channel_id=1, source_target_pairs={{0,2},{2,0},{4,6},{6,4},{8,10},{10,8},{12,14},{14,12},{16,18},{18,... | collective-permute-start | bytes 344072 | tf_op jit(solution)/shard_map/ppermute | solution.py:278
  38.6 0.4 collective-permute-done.3.low_ref
  39.0 0.9 attend_2.1
  39.9 0.5 collective-permute-start.5
  40.4 0.9 attend_1.1
  41.3 1.3 %collective-permute-start.2 = (bf16[4,240,128]{2,1,0:T(8,128)(2,1)S(1)}, bf16[4,240,128]{2,1,0:T(8,128)(2,1)S(1)}, u32[]{:S(2)}, u32[]{:S(2)}) collective-permute-start(bf16[4,240,128]{2,1,0:T(8,128)(2,1)S(1)} %attend_1.1), channel_id=1, source_target_pairs={{0,2},{2,0},{4,6},{6,4},{8,10},{10,8},{12,14},{14,12},{16,18},{18,... | collective-permute-start | bytes 737288 | tf_op jit(solution)/shard_map/ppermute | solution.py:278
  42.9 0.9 attend_3.1
  43.7 2.1 %collective-permute-start.8 = (bf16[4,240,128]{2,1,0:T(8,128)(2,1)S(1)}, bf16[4,240,128]{2,1,0:T(8,128)(2,1)S(1)}, u32[]{:S(2)}, u32[]{:S(2)}) collective-permute-start(bf16[4,240,128]{2,1,0:T(8,128)(2,1)S(1)} %attend_3.1), channel_id=1, source_target_pairs={{0,6},{2,4},{4,2},{6,0},{8,14},{10,12},{12,10},{14,8},{16,22},{18,... | collective-permute-start | bytes 737288 | tf_op jit(solution)/shard_map/ppermute | solution.py:278
  45.8 0.9 attend_0.1.refs_0_
  46.7 2.0 %collective-permute-done.5.refs_2_ = bf16[4,240,128]{2,1,0:T(8,128)(2,1)S(1)} collective-permute-done((bf16[4,240,128]{2,1,0:T(8,128)(2,1)S(1)}, bf16[4,240,128]{2,1,0:T(8,128)(2,1)S(1)}, u32[]{:S(2)}, u32[]{:S(2)}) %collective-permute-start.5) | collective-permute-done | bytes 245792 | tf_op jit(solution)/shard_map/ppermute | solution.py:278
  48.9 3.2 %collective-permute-done.8.refs_3_ = bf16[4,240,128]{2,1,0:T(8,128)(2,1)S(1)} collective-permute-done((bf16[4,240,128]{2,1,0:T(8,128)(2,1)S(1)}, bf16[4,240,128]{2,1,0:T(8,128)(2,1)S(1)}, u32[]{:S(2)}, u32[]{:S(2)}) %collective-permute-start.8) | collective-permute-done | bytes 245792 | tf_op jit(solution)/shard_map/ppermute | solution.py:278
  52.1 1.3 %merge_quad.1 = (bf16[240,128]{1,0:T(8,128)(2,1)S(1)}, bf16[240,128]{1,0:T(8,128)(2,1)S(1)}, bf16[240,128]{1,0:T(8,128)(2,1)S(1)}, bf16[240,128]{1,0:T(8,128)(2,1)S(1)}) custom-call(s32[1]{0:T(128)} %bitcast.2.where_ref, bf16[4,240,128]{2,1,0:T(8,128)(2,1)S(1)} %attend_0.1.refs_0_, bf16[4,240,128]{2,1,0:T(8,128)(2,1)S(1)} %collective-permute-done.2.refs_1_, ...), custom_call_target="tpu_custom_call" | custom-call | tf_op jit(solution)/shard_map/merge_quad/pallas_call | solution.py:260
  53.4 1.1 %collective-permute-start.9 = (bf16[240,128]{1,0:T(8,128)(2,1)S(1)}, bf16[240,128]{1,0:T(8,128)(2,1)S(1)}, u32[]{:S(2)}, u32[]{:S(2)}) collective-permute-start(bf16[240,128]{1,0:T(8,128)(2,1)S(1)} %get-tuple-element.17), channel_id=1, source_target_pairs={{0,8},{2,10},{4,12},{6,14},{8,0},{10,2},{12,4},{14,6},{16,24},{18,... | collective-permute-start | bytes 184328 | tf_op jit(solution)/shard_map/ppermute | solution.py:278
  54.5 2.1 %collective-permute-start.10 = (bf16[240,128]{1,0:T(8,128)(2,1)S(1)}, bf16[240,128]{1,0:T(8,128)(2,1)S(1)}, u32[]{:S(2)}, u32[]{:S(2)}) collective-permute-start(bf16[240,128]{1,0:T(8,128)(2,1)S(1)} %get-tuple-element.18), channel_id=1, source_target_pairs={{0,16},{2,18},{4,20},{6,22},{8,24},{10,26},{12,28},{14,30},{16,0},... | collective-permute-start | bytes 184328 | tf_op jit(solution)/shard_map/ppermute | solution.py:278
  56.6 1.3 %collective-permute-start.11 = (bf16[240,128]{1,0:T(8,128)(2,1)S(1)}, bf16[240,128]{1,0:T(8,128)(2,1)S(1)}, u32[]{:S(2)}, u32[]{:S(2)}) collective-permute-start(bf16[240,128]{1,0:T(8,128)(2,1)S(1)} %get-tuple-element.19), channel_id=1, source_target_pairs={{0,24},{2,26},{4,28},{6,30},{8,16},{10,18},{12,20},{14,22},{16,8},... | collective-permute-start | bytes 184328 | tf_op jit(solution)/shard_map/ppermute | solution.py:278
  57.8 0.4 collective-permute-done.9.refs_1_
  58.3 2.6 %collective-permute-done.10.refs_2_ = bf16[240,128]{1,0:T(8,128)(2,1)S(1)} collective-permute-done((bf16[240,128]{1,0:T(8,128)(2,1)S(1)}, bf16[240,128]{1,0:T(8,128)(2,1)S(1)}, u32[]{:S(2)}, u32[]{:S(2)}) %collective-permute-start.10) | collective-permute-done | bytes 61472 | tf_op jit(solution)/shard_map/ppermute | solution.py:278
  60.9 2.1 %collective-permute-done.11.refs_3_ = bf16[240,128]{1,0:T(8,128)(2,1)S(1)} collective-permute-done((bf16[240,128]{1,0:T(8,128)(2,1)S(1)}, bf16[240,128]{1,0:T(8,128)(2,1)S(1)}, u32[]{:S(2)}, u32[]{:S(2)}) %collective-permute-start.11) | collective-permute-done | bytes 61472 | tf_op jit(solution)/shard_map/ppermute | solution.py:278
  63.3 1.7 %collective-permute-start.14 = (bf16[224,128]{1,0:T(8,128)(2,1)S(1)}, bf16[224,128]{1,0:T(8,128)(2,1)S(1)}, u32[]{:S(2)}, u32[]{:S(2)}) collective-permute-start(bf16[224,128]{1,0:T(8,128)(2,1)S(1)} %merge_line.1.refs_0_), channel_id=1, source_target_pairs={{0,24},{2,26},{4,28},{6,30},{8,16},{10,18},{12,20},{14,22},{16,8},... | collective-permute-start | bytes 172040 | tf_op jit(solution)/shard_map/ppermute | solution.py:278
  65.0 0.3 collective-permute-start.13
  65.3 2.4 %collective-permute-start.12 = (bf16[224,128]{1,0:T(8,128)(2,1)S(1)}, bf16[224,128]{1,0:T(8,128)(2,1)S(1)}, u32[]{:S(2)}, u32[]{:S(2)}) collective-permute-start(bf16[224,128]{1,0:T(8,128)(2,1)S(1)} %merge_line.1.refs_0_), channel_id=1, source_target_pairs={{0,8},{2,10},{4,12},{6,14},{8,0},{10,2},{12,4},{14,6},{16,24},{18,... | collective-permute-start | bytes 172040 | tf_op jit(solution)/shard_map/ppermute | solution.py:278
  67.8 1.6 %collective-permute-done.14.refs_3_ = bf16[224,128]{1,0:T(8,128)(2,1)S(1)} collective-permute-done((bf16[224,128]{1,0:T(8,128)(2,1)S(1)}, bf16[224,128]{1,0:T(8,128)(2,1)S(1)}, u32[]{:S(2)}, u32[]{:S(2)}) %collective-permute-start.14) | collective-permute-done | bytes 57376 | tf_op jit(solution)/shard_map/ppermute | solution.py:278
  69.3 1.3 %collective-permute-done.13.refs_2_ = bf16[224,128]{1,0:T(8,128)(2,1)S(1)} collective-permute-done((bf16[224,128]{1,0:T(8,128)(2,1)S(1)}, bf16[224,128]{1,0:T(8,128)(2,1)S(1)}, u32[]{:S(2)}, u32[]{:S(2)}) %collective-permute-start.13) | collective-permute-done | bytes 57376 | tf_op jit(solution)/shard_map/ppermute | solution.py:278
  70.7 1.5 %collective-permute-start.15 = (bf16[448,128]{1,0:T(8,128)(2,1)S(1)}, bf16[448,128]{1,0:T(8,128)(2,1)S(1)}, u32[]{:S(2)}, u32[]{:S(2)}) collective-permute-start(bf16[448,128]{1,0:T(8,128)(2,1)S(1)} %get-tuple-element.20.refs_0_), channel_id=1, source_target_pairs={{0,2},{2,0},{4,6},{6,4},{8,10},{10,8},{12,14},{14,12},{16,18},{18,... | collective-permute-start | bytes 344072 | tf_op jit(solution)/shard_map/ppermute | solution.py:278
  72.3 1.1 %collective-permute-start.17 = (bf16[448,128]{1,0:T(8,128)(2,1)S(1)}, bf16[448,128]{1,0:T(8,128)(2,1)S(1)}, u32[]{:S(2)}, u32[]{:S(2)}) collective-permute-start(bf16[448,128]{1,0:T(8,128)(2,1)S(1)} %get-tuple-element.21.refs_1_), channel_id=1, source_target_pairs={{0,4},{2,6},{4,0},{6,2},{8,12},{10,14},{12,8},{14,10},{16,20},{18,... | collective-permute-start | bytes 344072 | tf_op jit(solution)/shard_map/ppermute | solution.py:278
  73.6 1.2 %collective-permute-start.19 = (bf16[448,128]{1,0:T(8,128)(2,1)S(1)}, bf16[448,128]{1,0:T(8,128)(2,1)S(1)}, u32[]{:S(2)}, u32[]{:S(2)}) collective-permute-start(bf16[448,128]{1,0:T(8,128)(2,1)S(1)} %get-tuple-element.20.refs_0_), channel_id=1, source_target_pairs={{0,4},{2,6},{4,0},{6,2},{8,12},{10,14},{12,8},{14,10},{16,20},{18,... | collective-permute-start | bytes 344072 | tf_op jit(solution)/shard_map/ppermute | solution.py:278
  74.8 0.7 collective-permute-done.15.refs_0_
  75.6 0.8 collective-permute-start.16
  76.4 0.7 collective-permute-done.17.refs_1_
  77.0 1.1 %collective-permute-start.18 = (bf16[448,128]{1,0:T(8,128)(2,1)S(1)}, bf16[448,128]{1,0:T(8,128)(2,1)S(1)}, u32[]{:S(2)}, u32[]{:S(2)}) collective-permute-start(bf16[448,128]{1,0:T(8,128)(2,1)S(1)} %collective-permute-done.17.refs_1_), channel_id=1, source_target_pairs={{0,2},{2,0},{4,6},{6,4},{8,10},{10,8},{12,14},{14,12},{16,18},{18,... | collective-permute-start | bytes 344072 | tf_op jit(solution)/shard_map/ppermute | solution.py:278
  79.2 1.4 %collective-permute-done.16.low_ref = bf16[448,128]{1,0:T(8,128)(2,1)S(1)} collective-permute-done((bf16[448,128]{1,0:T(8,128)(2,1)S(1)}, bf16[448,128]{1,0:T(8,128)(2,1)S(1)}, u32[]{:S(2)}, u32[]{:S(2)}) %collective-permute-start.16) | collective-permute-done | bytes 114720 | tf_op jit(solution)/shard_map/ppermute | solution.py:278
  80.6 1.7 %collective-permute-done.18.high_ref = bf16[448,128]{1,0:T(8,128)(2,1)S(1)} collective-permute-done((bf16[448,128]{1,0:T(8,128)(2,1)S(1)}, bf16[448,128]{1,0:T(8,128)(2,1)S(1)}, u32[]{:S(2)}, u32[]{:S(2)}) %collective-permute-start.18) | collective-permute-done | bytes 114720 | tf_op jit(solution)/shard_map/ppermute | solution.py:278
  82.4 0.7 place.1
  83.0 14.1 %all_to_all.11 = bf16[16,32,320]{2,1,0:T(8,128)(2,1)S(1)} all-to-all(bf16[16,32,320]{2,1,0:T(8,128)(2,1)S(1)} %place.1), channel_id=1, replica_groups=mesh['seq'=16,'head'=2] {'seq'}, dimensions={0} | all-to-all | bytes 655360 | tf_op jit(solution)/shard_map/all_to_all | solution.py:273
  97.2 1.7 %collective-permute-done.21 = bf16[16,32,320]{2,1,0:T(8,128)(2,1)S(1)} collective-permute-done((bf16[16,32,320]{2,1,0:T(8,128)(2,1)S(1)}, bf16[16,32,320]{2,1,0:T(8,128)(2,1)S(1)}, u32[]{:S(2)}, u32[]{:S(2)}) %collective-permute-start.21) | collective-permute-done | bytes 327712 | tf_op jit(solution)/shard_map/ppermute | solution.py:351
  98.9 0.8 copy-done.6
  99.7 4.8 %update.1 = bf16[256,2560]{1,0:T(8,128)(2,1)} custom-call(s32[1]{0:T(128)} %bitcast.half_ref, s32[1,256]{1,0:T(1,128)} %bitcast.10, bf16[1,16,32,320]{3,2,1,0:T(8,128)(2,1)} %bitcast.12, bf16[1,16,32,320]{3,2,1,0:T(8,128)(2,1)} %bitcast.13, bf16[256,2560]{1,0:T(8,128)(2,1)} %refs_3_.1, bf16[256,2560]{1,0:T(8,128)(2,1)} %refs_4_.1), custom_call_target="tpu_custom_call" | custom-call | tf_op jit(solution)/shard_map/update/pallas_call | solution.py:363
  (26 shorter events, 2.1 us)
Async XLA Ops:
  0.0 1.3 %copy-start.3 = (bf16[256,2560]{1,0:T(8,128)(2,1)S(1)}, bf16[256,2560]{1,0:T(8,128)(2,1)}, u32[]{:S(2)}) copy-start(bf16[256,2560]{1,0:T(8,128)(2,1)} %q_ref.1) | copy-start | bytes 3932164
  1.3 0.7 copy-start.4
  2.0 37.0 %copy-start.2 = (bf16[256,2560]{1,0:T(8,128)(2,1)S(1)}, bf16[256,2560]{1,0:T(8,128)(2,1)}, u32[]{:S(2)}) copy-start(bf16[256,2560]{1,0:T(8,128)(2,1)} %v_ref.7) | copy-start | bytes 3932164
  2.5 36.5 %copy-start.1 = (bf16[256,2560]{1,0:T(8,128)(2,1)S(1)}, bf16[256,2560]{1,0:T(8,128)(2,1)}, u32[]{:S(2)}) copy-start(bf16[256,2560]{1,0:T(8,128)(2,1)} %k_ref.7) | copy-start | bytes 3932164
  30.7 5.4 %collective-permute-start = (bf16[448,128]{1,0:T(8,128)(2,1)S(1)}, bf16[448,128]{1,0:T(8,128)(2,1)S(1)}, u32[]{:S(2)}, u32[]{:S(2)}) collective-permute-start(bf16[448,128]{1,0:T(8,128)(2,1)S(1)} %get-tuple-element.14.low_ref), channel_id=1, source_target_pairs={{0,2},{2,0},{4,6},{6,4},{8,10},{10,8},{12,14},{14,12},{16,18},{18,... | collective-permute-start | bytes 344072 | tf_op jit(solution)/shard_map/ppermute | solution.py:278
  31.4 5.5 %collective-permute-start.4 = (bf16[448,128]{1,0:T(8,128)(2,1)S(1)}, bf16[448,128]{1,0:T(8,128)(2,1)S(1)}, u32[]{:S(2)}, u32[]{:S(2)}) collective-permute-start(bf16[448,128]{1,0:T(8,128)(2,1)S(1)} %get-tuple-element.15.high_ref), channel_id=1, source_target_pairs={{0,4},{2,6},{4,0},{6,2},{8,12},{10,14},{12,8},{14,10},{16,20},{18,... | collective-permute-start | bytes 344072 | tf_op jit(solution)/shard_map/ppermute | solution.py:278
  32.0 7.0 %collective-permute-start.3 = (bf16[448,128]{1,0:T(8,128)(2,1)S(1)}, bf16[448,128]{1,0:T(8,128)(2,1)S(1)}, u32[]{:S(2)}, u32[]{:S(2)}) collective-permute-start(bf16[448,128]{1,0:T(8,128)(2,1)S(1)} %get-tuple-element.14.low_ref), channel_id=1, source_target_pairs={{0,4},{2,6},{4,0},{6,2},{8,12},{10,14},{12,8},{14,10},{16,20},{18,... | collective-permute-start | bytes 344072 | tf_op jit(solution)/shard_map/ppermute | solution.py:278
  33.4 7.0 %collective-permute-start.1 = (bf16[448,128]{1,0:T(8,128)(2,1)S(1)}, bf16[448,128]{1,0:T(8,128)(2,1)S(1)}, u32[]{:S(2)}, u32[]{:S(2)}) collective-permute-start(bf16[448,128]{1,0:T(8,128)(2,1)S(1)} %get-tuple-element.15.high_ref), channel_id=1, source_target_pairs={{0,2},{2,0},{4,6},{6,4},{8,10},{10,8},{12,14},{14,12},{16,18},{18,... | collective-permute-start | bytes 344072 | tf_op jit(solution)/shard_map/ppermute | solution.py:278
  36.1 6.5 %collective-permute-start.6 = (bf16[448,128]{1,0:T(8,128)(2,1)S(1)}, bf16[448,128]{1,0:T(8,128)(2,1)S(1)}, u32[]{:S(2)}, u32[]{:S(2)}) collective-permute-start(bf16[448,128]{1,0:T(8,128)(2,1)S(1)} %collective-permute-done.low_ref), channel_id=1, source_target_pairs={{0,4},{2,6},{4,0},{6,2},{8,12},{10,14},{12,8},{14,10},{16,20},{18,... | collective-permute-start | bytes 344072 | tf_op jit(solution)/shard_map/ppermute | solution.py:278
  36.9 6.0 %collective-permute-start.7 = (bf16[448,128]{1,0:T(8,128)(2,1)S(1)}, bf16[448,128]{1,0:T(8,128)(2,1)S(1)}, u32[]{:S(2)}, u32[]{:S(2)}) collective-permute-start(bf16[448,128]{1,0:T(8,128)(2,1)S(1)} %collective-permute-done.4.high_ref), channel_id=1, source_target_pairs={{0,2},{2,0},{4,6},{6,4},{8,10},{10,8},{12,14},{14,12},{16,18},{18,... | collective-permute-start | bytes 344072 | tf_op jit(solution)/shard_map/ppermute | solution.py:278
  39.9 8.9 %collective-permute-start.5 = (bf16[4,240,128]{2,1,0:T(8,128)(2,1)S(1)}, bf16[4,240,128]{2,1,0:T(8,128)(2,1)S(1)}, u32[]{:S(2)}, u32[]{:S(2)}) collective-permute-start(bf16[4,240,128]{2,1,0:T(8,128)(2,1)S(1)} %attend_2.1), channel_id=1, source_target_pairs={{0,4},{2,6},{4,0},{6,2},{8,12},{10,14},{12,8},{14,10},{16,20},{18,... | collective-permute-start | bytes 737288 | tf_op jit(solution)/shard_map/ppermute | solution.py:278
  41.3 7.7 %collective-permute-start.2 = (bf16[4,240,128]{2,1,0:T(8,128)(2,1)S(1)}, bf16[4,240,128]{2,1,0:T(8,128)(2,1)S(1)}, u32[]{:S(2)}, u32[]{:S(2)}) collective-permute-start(bf16[4,240,128]{2,1,0:T(8,128)(2,1)S(1)} %attend_1.1), channel_id=1, source_target_pairs={{0,2},{2,0},{4,6},{6,4},{8,10},{10,8},{12,14},{14,12},{16,18},{18,... | collective-permute-start | bytes 737288 | tf_op jit(solution)/shard_map/ppermute | solution.py:278
  43.7 8.4 %collective-permute-start.8 = (bf16[4,240,128]{2,1,0:T(8,128)(2,1)S(1)}, bf16[4,240,128]{2,1,0:T(8,128)(2,1)S(1)}, u32[]{:S(2)}, u32[]{:S(2)}) collective-permute-start(bf16[4,240,128]{2,1,0:T(8,128)(2,1)S(1)} %attend_3.1), channel_id=1, source_target_pairs={{0,6},{2,4},{4,2},{6,0},{8,14},{10,12},{12,10},{14,8},{16,22},{18,... | collective-permute-start | bytes 737288 | tf_op jit(solution)/shard_map/ppermute | solution.py:278
  45.8 32.3 %copy-start = (bf16[2560,320]{0,1:T(8,128)(2,1)S(1)}, bf16[2560,320]{0,1:T(8,128)(2,1)}, u32[]{:S(2)}) copy-start(bf16[2560,320]{0,1:T(8,128)(2,1)} %param.13) | copy-start | bytes 4915204
  53.4 4.9 %collective-permute-start.9 = (bf16[240,128]{1,0:T(8,128)(2,1)S(1)}, bf16[240,128]{1,0:T(8,128)(2,1)S(1)}, u32[]{:S(2)}, u32[]{:S(2)}) collective-permute-start(bf16[240,128]{1,0:T(8,128)(2,1)S(1)} %get-tuple-element.17), channel_id=1, source_target_pairs={{0,8},{2,10},{4,12},{6,14},{8,0},{10,2},{12,4},{14,6},{16,24},{18,... | collective-permute-start | bytes 184328 | tf_op jit(solution)/shard_map/ppermute | solution.py:278
  54.5 6.4 %collective-permute-start.10 = (bf16[240,128]{1,0:T(8,128)(2,1)S(1)}, bf16[240,128]{1,0:T(8,128)(2,1)S(1)}, u32[]{:S(2)}, u32[]{:S(2)}) collective-permute-start(bf16[240,128]{1,0:T(8,128)(2,1)S(1)} %get-tuple-element.18), channel_id=1, source_target_pairs={{0,16},{2,18},{4,20},{6,22},{8,24},{10,26},{12,28},{14,30},{16,0},... | collective-permute-start | bytes 184328 | tf_op jit(solution)/shard_map/ppermute | solution.py:278
  56.6 6.4 %collective-permute-start.11 = (bf16[240,128]{1,0:T(8,128)(2,1)S(1)}, bf16[240,128]{1,0:T(8,128)(2,1)S(1)}, u32[]{:S(2)}, u32[]{:S(2)}) collective-permute-start(bf16[240,128]{1,0:T(8,128)(2,1)S(1)} %get-tuple-element.19), channel_id=1, source_target_pairs={{0,24},{2,26},{4,28},{6,30},{8,16},{10,18},{12,20},{14,22},{16,8},... | collective-permute-start | bytes 184328 | tf_op jit(solution)/shard_map/ppermute | solution.py:278
  63.3 6.0 %collective-permute-start.14 = (bf16[224,128]{1,0:T(8,128)(2,1)S(1)}, bf16[224,128]{1,0:T(8,128)(2,1)S(1)}, u32[]{:S(2)}, u32[]{:S(2)}) collective-permute-start(bf16[224,128]{1,0:T(8,128)(2,1)S(1)} %merge_line.1.refs_0_), channel_id=1, source_target_pairs={{0,24},{2,26},{4,28},{6,30},{8,16},{10,18},{12,20},{14,22},{16,8},... | collective-permute-start | bytes 172040 | tf_op jit(solution)/shard_map/ppermute | solution.py:278
  65.0 5.7 %collective-permute-start.13 = (bf16[224,128]{1,0:T(8,128)(2,1)S(1)}, bf16[224,128]{1,0:T(8,128)(2,1)S(1)}, u32[]{:S(2)}, u32[]{:S(2)}) collective-permute-start(bf16[224,128]{1,0:T(8,128)(2,1)S(1)} %merge_line.1.refs_0_), channel_id=1, source_target_pairs={{0,16},{2,18},{4,20},{6,22},{8,24},{10,26},{12,28},{14,30},{16,0},... | collective-permute-start | bytes 172040 | tf_op jit(solution)/shard_map/ppermute | solution.py:278
  65.3 5.4 %collective-permute-start.12 = (bf16[224,128]{1,0:T(8,128)(2,1)S(1)}, bf16[224,128]{1,0:T(8,128)(2,1)S(1)}, u32[]{:S(2)}, u32[]{:S(2)}) collective-permute-start(bf16[224,128]{1,0:T(8,128)(2,1)S(1)} %merge_line.1.refs_0_), channel_id=1, source_target_pairs={{0,8},{2,10},{4,12},{6,14},{8,0},{10,2},{12,4},{14,6},{16,24},{18,... | collective-permute-start | bytes 172040 | tf_op jit(solution)/shard_map/ppermute | solution.py:278
  70.7 4.9 %collective-permute-start.15 = (bf16[448,128]{1,0:T(8,128)(2,1)S(1)}, bf16[448,128]{1,0:T(8,128)(2,1)S(1)}, u32[]{:S(2)}, u32[]{:S(2)}) collective-permute-start(bf16[448,128]{1,0:T(8,128)(2,1)S(1)} %get-tuple-element.20.refs_0_), channel_id=1, source_target_pairs={{0,2},{2,0},{4,6},{6,4},{8,10},{10,8},{12,14},{14,12},{16,18},{18,... | collective-permute-start | bytes 344072 | tf_op jit(solution)/shard_map/ppermute | solution.py:278
  72.3 4.8 %collective-permute-start.17 = (bf16[448,128]{1,0:T(8,128)(2,1)S(1)}, bf16[448,128]{1,0:T(8,128)(2,1)S(1)}, u32[]{:S(2)}, u32[]{:S(2)}) collective-permute-start(bf16[448,128]{1,0:T(8,128)(2,1)S(1)} %get-tuple-element.21.refs_1_), channel_id=1, source_target_pairs={{0,4},{2,6},{4,0},{6,2},{8,12},{10,14},{12,8},{14,10},{16,20},{18,... | collective-permute-start | bytes 344072 | tf_op jit(solution)/shard_map/ppermute | solution.py:278
  73.4 5.1 %collective-permute-start.20 = (bf16[448,128]{1,0:T(8,128)(2,1)S(1)}, bf16[448,128]{1,0:T(8,128)(2,1)S(1)}, u32[]{:S(2)}, u32[]{:S(2)}) collective-permute-start(bf16[448,128]{1,0:T(8,128)(2,1)S(1)} %get-tuple-element.21.refs_1_), channel_id=1, source_target_pairs={{0,2},{2,0},{4,6},{6,4},{8,10},{10,8},{12,14},{14,12},{16,18},{18,... | collective-permute-start | bytes 344072 | tf_op jit(solution)/shard_map/ppermute | solution.py:278
  73.6 5.2 %collective-permute-start.19 = (bf16[448,128]{1,0:T(8,128)(2,1)S(1)}, bf16[448,128]{1,0:T(8,128)(2,1)S(1)}, u32[]{:S(2)}, u32[]{:S(2)}) collective-permute-start(bf16[448,128]{1,0:T(8,128)(2,1)S(1)} %get-tuple-element.20.refs_0_), channel_id=1, source_target_pairs={{0,4},{2,6},{4,0},{6,2},{8,12},{10,14},{12,8},{14,10},{16,20},{18,... | collective-permute-start | bytes 344072 | tf_op jit(solution)/shard_map/ppermute | solution.py:278
  75.6 5.1 %collective-permute-start.16 = (bf16[448,128]{1,0:T(8,128)(2,1)S(1)}, bf16[448,128]{1,0:T(8,128)(2,1)S(1)}, u32[]{:S(2)}, u32[]{:S(2)}) collective-permute-start(bf16[448,128]{1,0:T(8,128)(2,1)S(1)} %collective-permute-done.15.refs_0_), channel_id=1, source_target_pairs={{0,4},{2,6},{4,0},{6,2},{8,12},{10,14},{12,8},{14,10},{16,20},{18,... | collective-permute-start | bytes 344072 | tf_op jit(solution)/shard_map/ppermute | solution.py:278
  77.0 5.3 %collective-permute-start.18 = (bf16[448,128]{1,0:T(8,128)(2,1)S(1)}, bf16[448,128]{1,0:T(8,128)(2,1)S(1)}, u32[]{:S(2)}, u32[]{:S(2)}) collective-permute-start(bf16[448,128]{1,0:T(8,128)(2,1)S(1)} %collective-permute-done.17.refs_1_), channel_id=1, source_target_pairs={{0,2},{2,0},{4,6},{6,4},{8,10},{10,8},{12,14},{14,12},{16,18},{18,... | collective-permute-start | bytes 344072 | tf_op jit(solution)/shard_map/ppermute | solution.py:278
  97.2 1.7 %copy-start.5 = (bf16[16,32,320]{2,1,0:T(8,128)(2,1)}, bf16[16,32,320]{2,1,0:T(8,128)(2,1)S(1)}, u32[]{:S(2)}) copy-start(bf16[16,32,320]{2,1,0:T(8,128)(2,1)S(1)} %all_to_all.11) | copy-start | bytes 983044
  97.2 1.7 %collective-permute-start.21 = (bf16[16,32,320]{2,1,0:T(8,128)(2,1)S(1)}, bf16[16,32,320]{2,1,0:T(8,128)(2,1)S(1)}, u32[]{:S(2)}, u32[]{:S(2)}) collective-permute-start(bf16[16,32,320]{2,1,0:T(8,128)(2,1)S(1)} %all_to_all.11), channel_id=1, source_target_pairs={{0,1},{1,0},{2,3},{3,2},{4,5},{5,4},{6,7},{7,6},{8,9},{9,8},{10,11... | collective-permute-start | bytes 983048 | tf_op jit(solution)/shard_map/ppermute | solution.py:351
  98.9 0.8 copy-start.6

commit v3 on v2

v3 whole, which is shorter than its diff:
```python
import functools
import math

import jax
import jax.numpy as jnp
from jax import lax
from jax.experimental import pallas as pl
from jax.experimental.pallas import tpu as pltpu
from jax.sharding import PartitionSpec as P


HD = 128
TILE = 16
QUAD = 4
LOG_LANES = 32
F32 = jnp.float32
BF16 = jnp.bfloat16
VMEM = pl.BlockSpec(memory_space=pltpu.VMEM)
SMEM = pl.BlockSpec(memory_space=pltpu.SMEM)
HBM = pl.BlockSpec(memory_space=pltpu.HBM)
LANES_BOTH = (((1,), (1,)), ((), ()))
ROWS_BOTH = (((0,), (0,)), ((), ()))


def iota(shape, dim):
    return lax.broadcasted_iota(jnp.int32, shape, dim).astype(F32)


class Plan:
    def __init__(self, devices, tok_dev, features):
        assert devices % (2 * QUAD) == 0
        self.devices = devices
        self.line = devices // QUAD
        self.heads = features // HD
        self.own_heads = -(-self.heads // QUAD)
        self.cap = tok_dev // 8
        self.total = devices * tok_dev * 11 // 256
        groups = -(-self.total // TILE)
        self.tok = groups * TILE
        self.tiles = -(-self.own_heads * groups // self.line)
        self.rows = self.tiles * TILE
        self.half = self.line // 2 * self.rows
        self.spans = max(
            min((self.tiles * (line + 1) - 1) // groups, self.own_heads - 1) - self.tiles * line // groups + 1
            for line in range(self.line)
        )
        assert self.tiles <= LOG_LANES

    def head_at(self, index, quad):
        return jnp.minimum(index * QUAD + quad, self.heads - 1)

    def first_head(self, line):
        return line * self.tiles * TILE // self.tok

    def sent_heads(self, device):
        first = self.first_head(device // QUAD)
        local = [min(first + i, self.own_heads - 1) for i in range(self.spans)]
        return [min(i * QUAD + device % QUAD, self.heads - 1) for i in local]

    def head_rows(self, refs, index):
        first, last = index * self.tok, (index + 1) * self.tok
        parts = []
        for i, ref in enumerate(refs):
            low, high = max(first - i * self.half, 0), min(last - i * self.half, self.half)
            if low < high:
                parts.append(ref[low:high, :])
        return parts[0] if len(parts) == 1 else jnp.concatenate(parts, axis=0)


def own_selection(act, cap):
    tokens = act.shape[1]
    before = (iota((tokens, tokens), 0) < iota((tokens, tokens), 1)).astype(BF16)
    many = jnp.broadcast_to(act, (TILE, tokens)).astype(BF16)
    rank = jnp.dot(many, before, preferred_element_type=F32)[0:1]
    rank = jnp.where(act > 0, rank, -1.0)
    return (iota((cap, tokens), 0) == rank).astype(BF16)


def prepare_kernel(plan, parts, wanted, act_hbm, q_hbm, k_hbm, v_hbm, *refs):
    out_ref, *fetched = refs[: 1 + len(wanted)]
    act_ref, q_ref, own_ref, passing, q_sems, in_sems, out_sems = refs[1 + len(wanted) :]
    me = lax.axis_index("seq")
    heads = plan.own_heads
    arriving, leaving = [], []
    for j, (source, step) in enumerate(wanted):
        quad = lax.rem(me, QUAD) ^ step
        for i in range(heads):
            columns = pl.ds(pl.multiple_of(plan.head_at(i, quad) * HD, HD), HD)
            n = j * heads + i
            taken = (k_hbm, v_hbm)[source].at[:, columns]
            target = fetched[j].at[:, i * HD : (i + 1) * HD]
            arriving.append(pltpu.make_async_copy(taken, passing.at[n], in_sems.at[n]))
            leaving.append(pltpu.make_async_copy(passing.at[n], target, out_sems.at[n]))
    wide = q_hbm.shape[1] // parts
    columns = [slice(i * wide, (i + 1) * wide) for i in range(parts)]
    queries = [
        pltpu.make_async_copy(q_hbm.at[:, c], q_ref.at[:, c], q_sems.at[i])
        for i, c in enumerate(columns)
    ]
    first = pltpu.make_async_copy(act_hbm, act_ref, q_sems.at[parts])
    early = 2 * heads
    for copy in [first, *arriving[:early], *queries, *arriving[early:]]:
        copy.start()

    def forward(low, high):
        for one, two in zip(arriving[low:high], leaving[low:high]):
            one.wait()
            two.start()

    first.wait()
    act = act_ref[...].astype(F32)
    chosen = own_selection(act, plan.cap)
    count = jnp.broadcast_to(jnp.sum(act, axis=1, keepdims=True), (8, HD)).astype(BF16)
    forward(0, early)
    for copy, c in zip(queries, columns):
        copy.wait()
        own_ref[:, c] = jnp.dot(chosen, q_ref[:, c], preferred_element_type=F32).astype(BF16)
    forward(early, len(arriving))
    for device in range(plan.devices):
        for i, head in enumerate(plan.sent_heads(device)):
            out_ref[device, i * plan.cap : (i + 1) * plan.cap, :] = own_ref[:, head * HD : (head + 1) * HD]
        out_ref[device, plan.spans * plan.cap :, :] = count
    for copy in leaving:
        copy.wait()


def compact_kernel(plan, where_ref, in_ref, out_ref, info_ref):
    devices, cap = plan.devices, plan.cap
    count = jnp.max(in_ref[:, plan.spans * cap :, :].astype(F32), axis=1)
    earlier = (iota((devices, devices), 1) < iota((devices, devices), 0)).astype(BF16)
    offset = jnp.dot(earlier, count.astype(BF16), preferred_element_type=F32)
    info_ref[0] = count
    info_ref[1] = offset
    slots = devices * cap
    place = iota((devices, slots), 1) - iota((devices, slots), 0) * cap
    held = (place >= 0) & (place < jnp.minimum(count[:, 0:1], float(cap)))
    ranks = jnp.sum(jnp.where(held, offset[:, 0:1] + place + 1.0, 0.0), axis=0, keepdims=True) - 1.0
    ranks = jnp.where(ranks < 0, -1.0e6, ranks)
    line = where_ref[0] // QUAD
    start = line * plan.rows - plan.first_head(line) * plan.tok
    packed = jnp.zeros((plan.rows, HD), F32)
    for i in range(plan.spans):
        token = iota((plan.rows, slots), 0) + (start - i * plan.tok).astype(F32)
        pick = (token == ranks).astype(BF16)
        source = in_ref[:, i * cap : (i + 1) * cap, :].reshape(slots, HD)
        packed = packed + jnp.dot(pick, source, preferred_element_type=F32)
    out_ref[...] = packed.astype(BF16)


def pack_logs(logs):
    high = logs.astype(BF16).astype(F32)
    mid = (logs - high).astype(BF16).astype(F32)
    low = (logs - high - mid).astype(BF16).astype(F32)
    return (high + pltpu.roll(mid, LOG_LANES, 1) + pltpu.roll(low, 2 * LOG_LANES, 1)).astype(BF16)


def unpack_logs(packed):
    kept = packed.astype(F32)
    return kept + pltpu.roll(kept, HD - LOG_LANES, 1) + pltpu.roll(kept, HD - 2 * LOG_LANES, 1)


def attention_kernel(plan, fetched, own, where_ref, *refs):
    *refs, out_ref, held_ref = refs
    line_refs, refs = refs[: plan.line], refs[plan.line :]
    inv_root = 1.0 / HD**0.5
    line, quad = where_ref[0] // QUAD, where_ref[0] & (QUAD - 1)
    lane = lax.broadcasted_iota(jnp.int32, (TILE, HD), 1)
    laid = [jnp.zeros((TILE, HD), F32) for _ in range(plan.line)]
    for step, ref in enumerate(line_refs):
        held_ref[pl.ds(pl.multiple_of((line ^ step) * plan.rows, TILE), plan.rows), :] = ref[...]
    first = plan.own_heads * plan.tok
    for chunk in range(first // plan.rows, plan.line):
        low = max(first - chunk * plan.rows, 0)
        if low < plan.rows:
            out_ref[chunk, low : plan.rows, :] = jnp.zeros((plan.rows - low, HD), BF16)
    for i in range(plan.own_heads):
        query = held_ref[i * plan.tok : (i + 1) * plan.tok, :]
        pairs = []
        for j in range(fetched):
            columns = slice(i * HD, (i + 1) * HD)
            pairs.append((refs[2 * j][:, columns], refs[2 * j + 1][:, columns]))
        if own:
            k_ref, v_ref = refs[2 * fetched :]
            columns = pl.ds(pl.multiple_of(plan.head_at(i, quad) * HD, HD), HD)
            pairs.append((k_ref[:, columns], v_ref[:, columns]))
        scores = [
            lax.dot_general(query, key, LANES_BOTH, preferred_element_type=F32) * inv_root
            for key, _ in pairs
        ]
        peak = functools.reduce(jnp.maximum, [jnp.max(s, axis=1, keepdims=True) for s in scores])
        expos = [jnp.exp(s - peak) for s in scores]
        total = functools.reduce(jnp.add, [jnp.sum(e, axis=1, keepdims=True) for e in expos])
        block = functools.reduce(
            jnp.add,
            [
                jnp.dot(e.astype(BF16), value, preferred_element_type=F32)
                for e, (_, value) in zip(expos, pairs)
            ],
        )
        block = (block / total).astype(BF16)
        logs = peak + jnp.log(total)
        for tile in range(plan.tok // TILE):
            chunk, place = divmod(i * (plan.tok // TILE) + tile, plan.tiles)
            mine = slice(tile * TILE, (tile + 1) * TILE)
            out_ref[chunk, place * TILE : (place + 1) * TILE, :] = block[mine]
            laid[chunk] = jnp.where(lane == place, logs[mine], laid[chunk])
    for chunk in range(plan.line):
        out_ref[chunk, plan.rows :, :] = pack_logs(laid[chunk])


def merge(plan, parts, out_ref, keep_logs):
    rows = plan.rows
    logs = [unpack_logs(part[rows:, :]) for part in parts]
    top = functools.reduce(jnp.maximum, logs)
    weights = [jnp.exp(log - top) for log in logs]
    total = functools.reduce(jnp.add, weights)
    scale = 1.0 / total
    weights = [weight * scale for weight in weights]
    for tile in range(plan.tiles):
        mine = slice(tile * TILE, (tile + 1) * TILE)
        mixed = functools.reduce(
            jnp.add,
            [w[:, tile : tile + 1] * part[mine, :].astype(F32) for w, part in zip(weights, parts)],
        )
        out_ref[mine, :] = mixed.astype(BF16)
    if keep_logs:
        lane = lax.broadcasted_iota(jnp.int32, (TILE, HD), 1)
        out_ref[rows:, :] = pack_logs(jnp.where(lane < LOG_LANES, top + jnp.log(total), 0.0))


def split_kernel(plan, where_ref, *refs):
    parts, outs = refs[: -plan.line], refs[-plan.line :]
    line = where_ref[0] // QUAD
    for step, out_ref in enumerate(outs):
        merge(plan, [part.at[line ^ step] for part in parts], out_ref, True)


def finish_kernel(plan, where_ref, near_ref, *refs):
    *refs, part_ref, held_ref = refs
    attention_kernel(plan, 2, False, where_ref, *refs[: -plan.line], part_ref, held_ref)
    split_kernel(plan, where_ref, near_ref, part_ref, *refs[-plan.line :])


def line_kernel(plan, *refs):
    merge(plan, refs[:-1], refs[-1], False)


def stack_kernel(plan, where_ref, *refs):
    *parts, low_ref, high_ref, held_ref = refs
    line = where_ref[0] // QUAD
    for step, part in enumerate(parts):
        held_ref[line ^ step] = part[...]
    for i in range(plan.line // 2):
        low_ref[i * plan.rows : (i + 1) * plan.rows, :] = held_ref[i]
        high_ref[i * plan.rows : (i + 1) * plan.rows, :] = held_ref[plan.line // 2 + i]


def project_group(plan, quad, refs, w_ref):
    sides, weights = [], []
    for i in range(plan.own_heads):
        block = plan.head_rows(refs, i)
        if plan.own_heads * QUAD != plan.heads:
            block = jnp.where(i * QUAD + quad < plan.heads, block, jnp.zeros_like(block))
        sides.append(block)
        columns = pl.ds(pl.multiple_of(plan.head_at(i, quad) * HD, HD), HD)
        weights.append(w_ref[:, columns])
    return lax.dot_general(
        jnp.concatenate(sides, axis=1),
        jnp.concatenate(weights, axis=1),
        LANES_BOTH,
        preferred_element_type=F32,
    )


def project_kernel(plan, steps, where_ref, w_ref, *refs):
    *refs, out_ref = refs
    total = None
    if len(refs) % 2:
        *refs, sum_ref = refs
        total = sum_ref[...]
    for i, step in enumerate(steps):
        quad = (where_ref[0] & (QUAD - 1)) ^ step
        term = project_group(plan, quad, refs[2 * i : 2 * i + 2], w_ref)
        total = term if total is None else total + term
    out_ref[...] = total


def place_kernel(plan, step, where_ref, w_ref, low_ref, high_ref, sum_ref, info_ref, out_ref):
    devices, cap, tok = plan.devices, plan.cap, plan.tok
    quad = (where_ref[0] & (QUAD - 1)) ^ step
    proj = sum_ref[...] + project_group(plan, quad, (low_ref, high_ref), w_ref)
    picks = []
    for device in range(devices):
        place = iota((cap, tok), 0)
        count = info_ref[0, device : device + 1, 0:1]
        offset = info_ref[1, device : device + 1, 0:1]
        picks.append(
            ((iota((cap, tok), 1) - offset == place) & (place < count)).astype(F32).astype(BF16)
        )
    pick = jnp.concatenate(picks, axis=0)
    laid = jnp.dot(pick, proj.astype(BF16), preferred_element_type=F32).astype(BF16)
    out_ref[...] = laid.reshape(devices, cap, w_ref.shape[0])


def update_kernel(plan, halves, half_ref, act_ref, *refs):
    *term_refs, hidden_ref, cached_ref, out_hbm, held_ref, sems = refs
    cap, width = plan.cap, term_refs[0].shape[-1]
    wide = math.lcm(width, HD)
    blocks, steps = wide // width, hidden_ref.shape[1] // wide
    chosen = own_selection(act_ref[...].astype(F32), cap)
    mask = lax.dot_general(chosen, jnp.ones((cap, HD), BF16), ROWS_BOTH, preferred_element_type=F32)
    active = mask[:, 0:1] > 0
    copies = []
    for step in range(steps):
        terms = []
        for ref in term_refs:
            if ref.ndim == 3:
                first = half_ref[0] * (plan.devices // halves) + step * blocks
                sides = [[ref[first + j] for j in range(blocks)]]
            else:
                sides = [[ref[i, step * blocks + j] for j in range(blocks)] for i in range(halves)]
            for side in sides:
                terms.append(jnp.concatenate([b.astype(F32) for b in side], axis=1).astype(BF16))
        summed = lax.dot_general(
            jnp.concatenate([chosen] * len(terms), axis=0),
            jnp.concatenate(terms, axis=0),
            ROWS_BOTH,
            preferred_element_type=F32,
        )
        columns = slice(step * wide, (step + 1) * wide)
        updated = (hidden_ref[:, columns].astype(F32) + summed).astype(BF16)
        held_ref[:, columns] = jnp.where(active, updated, cached_ref[:, columns])
        copy = pltpu.make_async_copy(held_ref.at[:, columns], out_hbm.at[:, columns], sems.at[step])
        copy.start()
        copies.append(copy)
    for copy in copies:
        copy.wait()


def shape(*dims, dtype=BF16):
    return jax.ShapeDtypeStruct(dims, dtype)


def call(kernel, out_shape, *args, cost=None, hbm=(), out_hbm=(), grant=32, **options):
    def spec(i, arg):
        if i in hbm:
            return HBM
        return SMEM if arg.dtype == jnp.int32 and arg.ndim == 1 else VMEM

    return pl.pallas_call(
        kernel,
        out_shape=out_shape,
        in_specs=[spec(i, arg) for i, arg in enumerate(args)],
        out_specs=jax.tree.unflatten(
            jax.tree.structure(out_shape),
            [HBM if i in out_hbm else VMEM for i in range(len(jax.tree.leaves(out_shape)))],
        ),
        compiler_params=pltpu.CompilerParams(vmem_limit_bytes=grant << 20),
        cost_estimate=cost,
        **options,
    )(*args)


def exchange(value):
    return lax.all_to_all(value, "seq", split_axis=0, concat_axis=0, tiled=True)


def shift(value, mask):
    pairs = [(i, i ^ mask) for i in range(lax.axis_size("seq"))]
    return lax.ppermute(value, "seq", pairs)


def line_gather(plan, chunk):
    return [shift(chunk, step * QUAD) if step else chunk for step in range(plan.line)]


def quad_gather(low, high):
    x_low, y_high = shift(low, 1), shift(high, 2)
    x_high, y_low = shift(high, 1), shift(low, 2)
    return [(low, high), (x_low, x_high), (y_low, y_high), (shift(x_low, 2), shift(y_high, 1))]


def shards(queries, keys, values, hidden, cached, active, w_out):
    tok_dev, features = queries.shape
    devices, halves = lax.axis_size("seq"), lax.axis_size("head")
    plan = Plan(devices, tok_dev, features)
    cap, columns = plan.cap, w_out.shape[1]
    act = active.reshape(1, tok_dev)
    me = lax.axis_index("seq").astype(jnp.int32).reshape(1)
    dma = pltpu.SemaphoreType.DMA
    partial = functools.partial

    parts = math.gcd(features // HD, 5)
    wanted = ((0, 1), (0, 2), (1, 1), (1, 2), (0, 3), (1, 3))
    blocks = plan.own_heads * len(wanted)
    sent, *near_k, x_v, y_v, far_k, far_v = call(
        partial(prepare_kernel, plan, parts, wanted),
        (
            shape(devices, plan.spans * cap + 8, HD),
            *[shape(tok_dev, plan.own_heads * HD) for _ in wanted],
        ),
        act, queries, keys, values, hbm=range(4), out_hbm=range(1, 1 + len(wanted)), grant=56,
        scratch_shapes=[
            pltpu.VMEM((1, tok_dev), jnp.int32),
            pltpu.VMEM((tok_dev, features), BF16),
            pltpu.VMEM((cap, features), BF16),
            pltpu.VMEM((blocks, tok_dev, HD), BF16),
            dma((parts + 1,)), dma((blocks,)), dma((blocks,)),
        ],
    )
    near_k = [shift(part, i + 1) for i, part in enumerate(near_k)]
    spread = exchange(sent)
    near_v = [shift(x_v, 1), shift(y_v, 2)]
    far = [shift(far_k, 3), shift(far_v, 3)]
    near, far = [near_k[0], near_v[0]], [near_k[1], near_v[1], *far]
    chunk, info = call(
        partial(compact_kernel, plan),
        (shape(plan.rows, HD), shape(2, devices, HD, dtype=F32)), me, spread,
    )
    line = line_gather(plan, chunk)
    scored = plan.own_heads * plan.tok * tok_dev

    def attend(kernel, count, out, *args, **options):
        cost = pl.CostEstimate(
            flops=4 * count * scored * HD,
            transcendentals=count * scored,
            bytes_accessed=4 * count * tok_dev * HD * plan.own_heads,
        )
        held = pltpu.VMEM((plan.line * plan.rows, HD), BF16)
        scratch = [*options.get("scratch", ()), held]
        return call(kernel, out, me, *args, cost=cost, scratch_shapes=scratch)

    scored_shape = (plan.line, plan.rows + TILE, HD)
    part = attend(
        partial(attention_kernel, plan, 1, True), 2,
        shape(*scored_shape), *line, *near, keys, values,
    )
    sums = attend(
        partial(finish_kernel, plan), 2,
        tuple(shape(plan.rows + TILE, HD) for _ in range(plan.line)),
        part, *line, *far, scratch=[pltpu.VMEM(scored_shape, BF16)],
    )
    arrived = [shift(part, step * QUAD) if step else part for step, part in enumerate(sums)]
    chunk = call(partial(line_kernel, plan), shape(plan.rows, HD), *arrived)
    low, high = call(
        partial(stack_kernel, plan), (shape(plan.half, HD), shape(plan.half, HD)),
        me, *line_gather(plan, chunk),
        scratch_shapes=[pltpu.VMEM((plan.line, plan.rows, HD), BF16)],
    )
    w_rows = w_out.T
    cost = pl.CostEstimate(
        flops=2 * plan.own_heads * plan.tok * HD * columns,
        transcendentals=0,
        bytes_accessed=2 * plan.own_heads * HD * columns,
    )
    groups = quad_gather(low, high)
    proj = None
    for step in range(QUAD - 1):
        extra = () if proj is None else (proj,)
        proj = call(
            partial(project_kernel, plan, (step,)),
            shape(plan.tok, columns, dtype=F32), me, w_rows, *groups[step], *extra, cost=cost,
        )
    terms = call(
        partial(place_kernel, plan, QUAD - 1),
        shape(devices, cap, columns), me, w_rows, *groups[QUAD - 1], proj, info,
    )
    arrived = exchange(terms)

    half = lax.axis_index("head").astype(jnp.int32).reshape(1)
    if halves == 2:
        term_args = [arrived, lax.ppermute(arrived, "head", [(0, 1), (1, 0)])]
    else:
        split = arrived.reshape(halves, devices // halves, cap, columns)
        term_args = [lax.all_to_all(split, "head", split_axis=0, concat_axis=0, tiled=True)]
    return call(
        partial(update_kernel, plan, halves),
        shape(tok_dev, features), half, act, *term_args, hidden, cached, out_hbm=(0,),
        scratch_shapes=[
            pltpu.VMEM((tok_dev, features), BF16),
            dma((features // math.lcm(columns, HD),)),
        ],
    )


def solution(mesh):
    placed = (
        P("seq", "head"),
        P("seq", "head"),
        P("seq", "head"),
        P("seq", "head"),
        P("seq", "head"),
        P("seq"),
        P("head", "seq"),
    )


    return jax.shard_map(
        shards, mesh=mesh, in_specs=placed, out_specs=P("seq", "head"), check_vma=False
    )
```

time: 105 us -> 105 us (level)
  blocking collectives: 41.8 us -> 14.1 us
  waiting for transfers between devices: 21.7 us -> 37.9 us
  starting transfers between devices: 25.5 us -> 35.3 us
  Pallas kernels: 12.6 us -> 15.1 us
  local copies, waits for them, and re-layouts: 2.77 us -> 1.72 us
    all_to_all x2 -> x1, blocking collectives: 41.8 us -> 14.1 us  [exchange(): return lax.all_to_all(value, 'seq', split_axis=0, concat_axis=0, tiled=True)]
    ppermute x21, waiting for transfers between devices: 20 us -> 36.1 us  [shift(): return lax.ppermute(value, 'seq', pairs)]
    all_to_all x0 -> x1, starting transfers between devices: none -> 8.35 us  [exchange(): return lax.all_to_all(value, 'seq', split_axis=0, concat_axis=0, tiled=True)]
    pallas_call x14 -> x11, Pallas kernels: 12.6 us -> 15.1 us  [call(): pl.pallas_call(kernel, out_shape=out_shape, in_specs=[spec(i, arg) for i,...]
    ppermute x21, starting transfers between devices: 25.5 us -> 27 us  [shift(): return lax.ppermute(value, 'seq', pairs)]
    unnamed x14 -> x16, local copies, waits for them, and re-layouts: 2.77 us -> 1.72 us
  transfers between devices with their start and end apart: 22 -> 23, of which waited for: 16 -> 14; matrix products, arithmetic and copies ran while one was open for 0% -> 0% of each run, Pallas kernels for 4% -> 4%
where the time goes in v3:
time: 105 us; the launch traced here: 104 us
  waiting for transfers between devices  37.9 us (36%)
  starting transfers between devices  35.3 us (34%)
  Pallas kernels  15.1 us (14%)
  blocking collectives  14.1 us (13%)
  local copies, waits for them, and re-layouts  1.72 us (2%)
    ppermute x21, waiting for transfers between devices, shift(): return lax.ppermute(value, 'seq', pairs)  36.1 us
    ppermute x21, starting transfers between devices, shift(): return lax.ppermute(value, 'seq', pairs)  27 us
    pallas_call x11, Pallas kernels, call(): pl.pallas_call(kernel, out_shape=out_shape, in_specs=[spec(i, arg) for i,...  15.1 us
    all_to_all x1, blocking collectives, exchange(): return lax.all_to_all(value, 'seq', split_axis=0, concat_axis=0, tiled=True)  14.1 us
    all_to_all x1, starting transfers between devices, exchange(): return lax.all_to_all(value, 'seq', split_axis=0, concat_axis=0, tiled=True)  8.35 us
  transfers between devices with their start and end apart: 23, of which 14 were waited for; matrix products, arithmetic and copies ran while one was open for 0% of the time, Pallas kernels for 4%

profile of v3, /device:TPU:0, one launch (start us, length us, event | category | flops | bytes accessed | tf_op | source)
XLA Modules:
  0.0 104.2 jit_solution(6328821114784845155)
XLA Ops:
  0.0 4.9 %shard_map.73 = (bf16[16,72,128]{2,1,0:T(8,128)(2,1)}, bf16[256,640]{1,0:T(8,128)(2,1)}, bf16[256,640]{1,0:T(8,128)(2,1)}, bf16[256,640]{1,0:T(8,128)(2,1)}, bf1...) custom-call(s32[1,256]{1,0:T(1,128)} %bitcast.8, bf16[256,2560]{1,0:T(8,128)(2,1)} %q_hbm.1, ...), custom_call_target="tpu_custom_call" | custom-call | tf_op jit(solution)/shard_map/pallas_call | solution.py:350
  5.0 8.4 %all-to-all-start = ((bf16[16,72,128]{2,1,0:T(8,128)(2,1)}), bf16[16,72,128]{2,1,0:T(8,128)(2,1)S(1)}, u32[]{:S(2)}, u32[]{:S(2)}) async-start(bf16[16,72,128]{2,1,0:T(8,128)(2,1)} %get-tuple-element.20), calls=%async_computation | async-start | bytes 589824 | tf_op jit(solution)/shard_map/all_to_all | solution.py:365
  13.3 1.9 %collective-permute-start.3 = (bf16[256,640]{1,0:T(8,128)(2,1)}, bf16[256,640]{1,0:T(8,128)(2,1)S(1)}, u32[]{:S(2)}, u32[]{:S(2)}) collective-permute-start(bf16[256,640]{1,0:T(8,128)(2,1)} %get-tuple-element.22), channel_id=1, source_target_pairs={{0,2},{2,0},{4,6},{6,4},{8,10},{10,8},{12,14},{14,12},{16,18},{18,... | collective-permute-start | bytes 983048 | tf_op jit(solution)/shard_map/ppermute | solution.py:370
  15.2 0.2 collective-permute-start.4
  15.4 1.9 %collective-permute-start.5 = (bf16[256,640]{1,0:T(8,128)(2,1)}, bf16[256,640]{1,0:T(8,128)(2,1)S(1)}, u32[]{:S(2)}, u32[]{:S(2)}) collective-permute-start(bf16[256,640]{1,0:T(8,128)(2,1)} %get-tuple-element.24), channel_id=1, source_target_pairs={{0,4},{2,6},{4,0},{6,2},{8,12},{10,14},{12,8},{14,10},{16,20},{18,... | collective-permute-start | bytes 983048 | tf_op jit(solution)/shard_map/ppermute | solution.py:370
  17.3 0.2 collective-permute-start.6
  17.4 2.8 %collective-permute-start.7 = (bf16[256,640]{1,0:T(8,128)(2,1)}, bf16[256,640]{1,0:T(8,128)(2,1)}, u32[]{:S(2)}, u32[]{:S(2)}) collective-permute-start(bf16[256,640]{1,0:T(8,128)(2,1)} %get-tuple-element.26), channel_id=1, source_target_pairs={{0,6},{2,4},{4,2},{6,0},{8,14},{10,12},{12,10},{14,8},{16,22},{18,... | collective-permute-start | bytes 983048 | tf_op jit(solution)/shard_map/ppermute | solution.py:370
  20.2 6.9 %collective-permute-done.3.refs_4_ = bf16[256,640]{1,0:T(8,128)(2,1)S(1)} collective-permute-done((bf16[256,640]{1,0:T(8,128)(2,1)}, bf16[256,640]{1,0:T(8,128)(2,1)S(1)}, u32[]{:S(2)}, u32[]{:S(2)}) %collective-permute-start.3) | collective-permute-done | bytes 327712 | tf_op jit(solution)/shard_map/ppermute | solution.py:370
  27.1 0.7 copy-done.5
  27.9 1.6 %collective-permute-start.8 = (bf16[256,640]{1,0:T(8,128)(2,1)}, bf16[256,640]{1,0:T(8,128)(2,1)}, u32[]{:S(2)}, u32[]{:S(2)}) collective-permute-start(bf16[256,640]{1,0:T(8,128)(2,1)} %get-tuple-element.27), channel_id=1, source_target_pairs={{0,6},{2,4},{4,2},{6,0},{8,14},{10,12},{12,10},{14,8},{16,22},{18,... | collective-permute-start | bytes 983048 | tf_op jit(solution)/shard_map/ppermute | solution.py:370
  29.5 0.5 shard_map.74
  30.0 4.3 %collective-permute-done.4.refs_5_ = bf16[256,640]{1,0:T(8,128)(2,1)} collective-permute-done((bf16[256,640]{1,0:T(8,128)(2,1)}, bf16[256,640]{1,0:T(8,128)(2,1)}, u32[]{:S(2)}, u32[]{:S(2)}) %collective-permute-start.4) | collective-permute-done | bytes 327712 | tf_op jit(solution)/shard_map/ppermute | solution.py:370
  34.3 2.9 %collective-permute-start.2 = (bf16[224,128]{1,0:T(8,128)(2,1)S(1)}, bf16[224,128]{1,0:T(8,128)(2,1)S(1)}, u32[]{:S(2)}, u32[]{:S(2)}) collective-permute-start(bf16[224,128]{1,0:T(8,128)(2,1)S(1)} %get-tuple-element.21.refs_0_), channel_id=1, source_target_pairs={{0,24},{2,26},{4,28},{6,30},{8,16},{10,18},{12,20},{14,22},{16,8},... | collective-permute-start | bytes 172040 | tf_op jit(solution)/shard_map/ppermute | solution.py:370
  37.2 3.1 %collective-permute-done.2.refs_3_ = bf16[224,128]{1,0:T(8,128)(2,1)S(1)} collective-permute-done((bf16[224,128]{1,0:T(8,128)(2,1)S(1)}, bf16[224,128]{1,0:T(8,128)(2,1)S(1)}, u32[]{:S(2)}, u32[]{:S(2)}) %collective-permute-start.2) | collective-permute-done | bytes 57376 | tf_op jit(solution)/shard_map/ppermute | solution.py:370
  40.3 0.6 collective-permute-start.1
  40.8 5.1 %collective-permute-done.1.refs_2_ = bf16[224,128]{1,0:T(8,128)(2,1)S(1)} collective-permute-done((bf16[224,128]{1,0:T(8,128)(2,1)S(1)}, bf16[224,128]{1,0:T(8,128)(2,1)S(1)}, u32[]{:S(2)}, u32[]{:S(2)}) %collective-permute-start.1) | collective-permute-done | bytes 57376 | tf_op jit(solution)/shard_map/ppermute | solution.py:370
  45.9 0.0 collective-permute-start
  45.9 4.2 %collective-permute-done.refs_1_ = bf16[224,128]{1,0:T(8,128)(2,1)S(1)} collective-permute-done((bf16[224,128]{1,0:T(8,128)(2,1)S(1)}, bf16[224,128]{1,0:T(8,128)(2,1)S(1)}, u32[]{:S(2)}, u32[]{:S(2)}) %collective-permute-start) | collective-permute-done | bytes 57376 | tf_op jit(solution)/shard_map/ppermute | solution.py:370
  50.1 1.0 copy-done.6
  51.1 2.6 %shard_map.75.near_ref = bf16[4,240,128]{2,1,0:T(8,128)(2,1)S(1)} custom-call(s32[1]{0:T(128)} %bitcast.2.where_ref, bf16[224,128]{1,0:T(8,128)(2,1)S(1)} %get-tuple-element.21.refs_0_, bf16[224,128]{1,0:T(8,128)(2,1)S(1)} %collective-permute-done.refs_1_, bf16[224,128]{1,0:T(8,128)(2,1)S(1)} %collective-permute-done.1.refs_2_, ...), custom_call_target="tpu_custom_call" | custom-call | flops 230686720 | bytes 1310720 | tf_op jit(solution)/shard_map/pallas_call | solution.py:350
  53.7 3.4 %shard_map.76 = (bf16[240,128]{1,0:T(8,128)(2,1)S(1)}, bf16[240,128]{1,0:T(8,128)(2,1)S(1)}, bf16[240,128]{1,0:T(8,128)(2,1)S(1)}, bf16[240,128]{1,0:T(8,128)(2,1)S(1)}) custom-call(s32[1]{0:T(128)} %bitcast.2.where_ref, bf16[4,240,128]{2,1,0:T(8,128)(2,1)S(1)} %shard_map.75.near_ref, bf16[224,128]{1,0:T(8,128)(2,1)S(1)} %get-tuple-element.21.refs_0_, ...), custom_call_target="tpu_custom_call" | custom-call | flops 230686720 | bytes 1310720 | tf_op jit(solution)/shard_map/pallas_call | solution.py:350
  57.1 0.1 collective-permute-start.9
  57.2 2.9 %collective-permute-start.10 = (bf16[240,128]{1,0:T(8,128)(2,1)S(1)}, bf16[240,128]{1,0:T(8,128)(2,1)S(1)}, u32[]{:S(2)}, u32[]{:S(2)}) collective-permute-start(bf16[240,128]{1,0:T(8,128)(2,1)S(1)} %get-tuple-element.30), channel_id=1, source_target_pairs={{0,16},{2,18},{4,20},{6,22},{8,24},{10,26},{12,28},{14,30},{16,0},... | collective-permute-start | bytes 184328 | tf_op jit(solution)/shard_map/ppermute | solution.py:370
  60.1 1.5 %collective-permute-start.11 = (bf16[240,128]{1,0:T(8,128)(2,1)S(1)}, bf16[240,128]{1,0:T(8,128)(2,1)S(1)}, u32[]{:S(2)}, u32[]{:S(2)}) collective-permute-start(bf16[240,128]{1,0:T(8,128)(2,1)S(1)} %get-tuple-element.31), channel_id=1, source_target_pairs={{0,24},{2,26},{4,28},{6,30},{8,16},{10,18},{12,20},{14,22},{16,8},... | collective-permute-start | bytes 184328 | tf_op jit(solution)/shard_map/ppermute | solution.py:370
  61.6 1.0 collective-permute-done.10.refs_2_
  62.6 4.2 %collective-permute-done.11.refs_3_ = bf16[240,128]{1,0:T(8,128)(2,1)S(1)} collective-permute-done((bf16[240,128]{1,0:T(8,128)(2,1)S(1)}, bf16[240,128]{1,0:T(8,128)(2,1)S(1)}, u32[]{:S(2)}, u32[]{:S(2)}) %collective-permute-start.11) | collective-permute-done | bytes 61472 | tf_op jit(solution)/shard_map/ppermute | solution.py:370
  66.8 0.3 shard_map.77.refs_0_
  67.1 1.4 %collective-permute-start.14 = (bf16[224,128]{1,0:T(8,128)(2,1)S(1)}, bf16[224,128]{1,0:T(8,128)(2,1)S(1)}, u32[]{:S(2)}, u32[]{:S(2)}) collective-permute-start(bf16[224,128]{1,0:T(8,128)(2,1)S(1)} %shard_map.77.refs_0_), channel_id=1, source_target_pairs={{0,24},{2,26},{4,28},{6,30},{8,16},{10,18},{12,20},{14,22},{16,8},... | collective-permute-start | bytes 172040 | tf_op jit(solution)/shard_map/ppermute | solution.py:370
  68.5 3.1 %collective-permute-start.12 = (bf16[224,128]{1,0:T(8,128)(2,1)S(1)}, bf16[224,128]{1,0:T(8,128)(2,1)S(1)}, u32[]{:S(2)}, u32[]{:S(2)}) collective-permute-start(bf16[224,128]{1,0:T(8,128)(2,1)S(1)} %shard_map.77.refs_0_), channel_id=1, source_target_pairs={{0,8},{2,10},{4,12},{6,14},{8,0},{10,2},{12,4},{14,6},{16,24},{18,... | collective-permute-start | bytes 172040 | tf_op jit(solution)/shard_map/ppermute | solution.py:370
  71.5 1.6 %collective-permute-done.14.refs_3_ = bf16[224,128]{1,0:T(8,128)(2,1)S(1)} collective-permute-done((bf16[224,128]{1,0:T(8,128)(2,1)S(1)}, bf16[224,128]{1,0:T(8,128)(2,1)S(1)}, u32[]{:S(2)}, u32[]{:S(2)}) %collective-permute-start.14) | collective-permute-done | bytes 57376 | tf_op jit(solution)/shard_map/ppermute | solution.py:370
  73.2 1.2 %collective-permute-done.13.refs_2_ = bf16[224,128]{1,0:T(8,128)(2,1)S(1)} collective-permute-done((bf16[224,128]{1,0:T(8,128)(2,1)S(1)}, bf16[224,128]{1,0:T(8,128)(2,1)S(1)}, u32[]{:S(2)}, u32[]{:S(2)}) %collective-permute-start.13) | collective-permute-done | bytes 57376 | tf_op jit(solution)/shard_map/ppermute | solution.py:370
  74.4 1.2 %collective-permute-start.15 = (bf16[448,128]{1,0:T(8,128)(2,1)S(1)}, bf16[448,128]{1,0:T(8,128)(2,1)S(1)}, u32[]{:S(2)}, u32[]{:S(2)}) collective-permute-start(bf16[448,128]{1,0:T(8,128)(2,1)S(1)} %get-tuple-element.32.refs_0_), channel_id=1, source_target_pairs={{0,2},{2,0},{4,6},{6,4},{8,10},{10,8},{12,14},{14,12},{16,18},{18,... | collective-permute-start | bytes 344072 | tf_op jit(solution)/shard_map/ppermute | solution.py:370
  75.6 0.5 collective-permute-start.17
  76.1 1.9 %collective-permute-start.20 = (bf16[448,128]{1,0:T(8,128)(2,1)S(1)}, bf16[448,128]{1,0:T(8,128)(2,1)S(1)}, u32[]{:S(2)}, u32[]{:S(2)}) collective-permute-start(bf16[448,128]{1,0:T(8,128)(2,1)S(1)} %get-tuple-element.33.refs_1_), channel_id=1, source_target_pairs={{0,2},{2,0},{4,6},{6,4},{8,10},{10,8},{12,14},{14,12},{16,18},{18,... | collective-permute-start | bytes 344072 | tf_op jit(solution)/shard_map/ppermute | solution.py:370
  78.0 0.5 collective-permute-start.19
  78.5 0.7 collective-permute-done.15.refs_0_
  79.3 1.5 %collective-permute-start.16 = (bf16[448,128]{1,0:T(8,128)(2,1)S(1)}, bf16[448,128]{1,0:T(8,128)(2,1)S(1)}, u32[]{:S(2)}, u32[]{:S(2)}) collective-permute-start(bf16[448,128]{1,0:T(8,128)(2,1)S(1)} %collective-permute-done.15.refs_0_), channel_id=1, source_target_pairs={{0,4},{2,6},{4,0},{6,2},{8,12},{10,14},{12,8},{14,10},{16,20},{18,... | collective-permute-start | bytes 344072 | tf_op jit(solution)/shard_map/ppermute | solution.py:370
  80.8 0.5 collective-permute-start.18
  81.3 0.3 shard_map.79.refs_2_
  81.6 0.3 shard_map.80.refs_2_
  82.0 0.8 collective-permute-done.19.refs_0_
  82.8 0.3 shard_map.81.sum_ref
  83.1 1.7 %collective-permute-done.16.low_ref = bf16[448,128]{1,0:T(8,128)(2,1)S(1)} collective-permute-done((bf16[448,128]{1,0:T(8,128)(2,1)S(1)}, bf16[448,128]{1,0:T(8,128)(2,1)S(1)}, u32[]{:S(2)}, u32[]{:S(2)}) %collective-permute-start.16) | collective-permute-done | bytes 114720 | tf_op jit(solution)/shard_map/ppermute | solution.py:370
  84.9 1.2 %collective-permute-done.18.high_ref = bf16[448,128]{1,0:T(8,128)(2,1)S(1)} collective-permute-done((bf16[448,128]{1,0:T(8,128)(2,1)S(1)}, bf16[448,128]{1,0:T(8,128)(2,1)S(1)}, u32[]{:S(2)}, u32[]{:S(2)}) %collective-permute-start.18) | collective-permute-done | bytes 114720 | tf_op jit(solution)/shard_map/ppermute | solution.py:370
  86.1 0.7 shard_map.82
  86.8 14.1 %all_to_all.10.refs_0_ = bf16[16,32,320]{2,1,0:T(8,128)(2,1)S(1)} all-to-all(bf16[16,32,320]{2,1,0:T(8,128)(2,1)S(1)} %shard_map.82), channel_id=1, replica_groups=mesh['seq'=16,'head'=2] {'seq'}, dimensions={0} | all-to-all | bytes 655360 | tf_op jit(solution)/shard_map/all_to_all | solution.py:365
  100.8 1.7 %collective-permute-done.21.refs_1_ = bf16[16,32,320]{2,1,0:T(8,128)(2,1)S(1)} collective-permute-done((bf16[16,32,320]{2,1,0:T(8,128)(2,1)S(1)}, bf16[16,32,320]{2,1,0:T(8,128)(2,1)S(1)}, u32[]{:S(2)}, u32[]{:S(2)}) %collective-permute-start.21) | collective-permute-done | bytes 327712 | tf_op jit(solution)/shard_map/ppermute | solution.py:472
  102.6 1.6 %shard_map.83 = bf16[256,2560]{1,0:T(8,128)(2,1)} custom-call(s32[1]{0:T(128)} %bitcast.half_ref, s32[1,256]{1,0:T(1,128)S(1)} %bitcast.9, bf16[16,32,320]{2,1,0:T(8,128)(2,1)S(1)} %all_to_all.10.refs_0_, bf16[16,32,320]{2,1,0:T(8,128)(2,1)S(1)} %collective-permute-done.21.refs_1_, bf16[256,2560]{1,0:T(8,128)(2,1)S(1)} %copy-done.3, ...), custom_call_target="tpu_custom_call" | custom-call | tf_op jit(solution)/shard_map/pallas_call | solution.py:350
  (26 shorter events, 0.1 us)
Async XLA Ops:
  0.0 50.1 %copy-start.1 = (bf16[256,2560]{1,0:T(8,128)(2,1)S(1)}, bf16[256,2560]{1,0:T(8,128)(2,1)}, u32[]{:S(2)}) copy-start(bf16[256,2560]{1,0:T(8,128)(2,1)} %refs_6_.1) | copy-start | bytes 3932164
  0.0 50.1 %copy-start.2 = (bf16[256,2560]{1,0:T(8,128)(2,1)S(1)}, bf16[256,2560]{1,0:T(8,128)(2,1)}, u32[]{:S(2)}) copy-start(bf16[256,2560]{1,0:T(8,128)(2,1)} %refs_7_.1) | copy-start | bytes 3932164
  5.0 24.5 %all-to-all-start = ((bf16[16,72,128]{2,1,0:T(8,128)(2,1)}), bf16[16,72,128]{2,1,0:T(8,128)(2,1)S(1)}, u32[]{:S(2)}, u32[]{:S(2)}) async-start(bf16[16,72,128]{2,1,0:T(8,128)(2,1)} %get-tuple-element.20), calls=%async_computation | async-start | bytes 589824 | tf_op jit(solution)/shard_map/all_to_all | solution.py:365
  13.3 13.8 %collective-permute-start.3 = (bf16[256,640]{1,0:T(8,128)(2,1)}, bf16[256,640]{1,0:T(8,128)(2,1)S(1)}, u32[]{:S(2)}, u32[]{:S(2)}) collective-permute-start(bf16[256,640]{1,0:T(8,128)(2,1)} %get-tuple-element.22), channel_id=1, source_target_pairs={{0,2},{2,0},{4,6},{6,4},{8,10},{10,8},{12,14},{14,12},{16,18},{18,... | collective-permute-start | bytes 983048 | tf_op jit(solution)/shard_map/ppermute | solution.py:370
  15.2 19.0 %collective-permute-start.4 = (bf16[256,640]{1,0:T(8,128)(2,1)}, bf16[256,640]{1,0:T(8,128)(2,1)}, u32[]{:S(2)}, u32[]{:S(2)}) collective-permute-start(bf16[256,640]{1,0:T(8,128)(2,1)} %get-tuple-element.23), channel_id=1, source_target_pairs={{0,2},{2,0},{4,6},{6,4},{8,10},{10,8},{12,14},{14,12},{16,18},{18,... | collective-permute-start | bytes 983048 | tf_op jit(solution)/shard_map/ppermute | solution.py:370
  15.4 38.3 %collective-permute-start.5 = (bf16[256,640]{1,0:T(8,128)(2,1)}, bf16[256,640]{1,0:T(8,128)(2,1)S(1)}, u32[]{:S(2)}, u32[]{:S(2)}) collective-permute-start(bf16[256,640]{1,0:T(8,128)(2,1)} %get-tuple-element.24), channel_id=1, source_target_pairs={{0,4},{2,6},{4,0},{6,2},{8,12},{10,14},{12,8},{14,10},{16,20},{18,... | collective-permute-start | bytes 983048 | tf_op jit(solution)/shard_map/ppermute | solution.py:370
  17.3 36.4 %collective-permute-start.6 = (bf16[256,640]{1,0:T(8,128)(2,1)}, bf16[256,640]{1,0:T(8,128)(2,1)}, u32[]{:S(2)}, u32[]{:S(2)}) collective-permute-start(bf16[256,640]{1,0:T(8,128)(2,1)} %get-tuple-element.25), channel_id=1, source_target_pairs={{0,4},{2,6},{4,0},{6,2},{8,12},{10,14},{12,8},{14,10},{16,20},{18,... | collective-permute-start | bytes 983048 | tf_op jit(solution)/shard_map/ppermute | solution.py:370
  17.4 36.3 %collective-permute-start.7 = (bf16[256,640]{1,0:T(8,128)(2,1)}, bf16[256,640]{1,0:T(8,128)(2,1)}, u32[]{:S(2)}, u32[]{:S(2)}) collective-permute-start(bf16[256,640]{1,0:T(8,128)(2,1)} %get-tuple-element.26), channel_id=1, source_target_pairs={{0,6},{2,4},{4,2},{6,0},{8,14},{10,12},{12,10},{14,8},{16,22},{18,... | collective-permute-start | bytes 983048 | tf_op jit(solution)/shard_map/ppermute | solution.py:370
  27.1 0.7 copy-start.5
  27.9 25.8 %collective-permute-start.8 = (bf16[256,640]{1,0:T(8,128)(2,1)}, bf16[256,640]{1,0:T(8,128)(2,1)}, u32[]{:S(2)}, u32[]{:S(2)}) collective-permute-start(bf16[256,640]{1,0:T(8,128)(2,1)} %get-tuple-element.27), channel_id=1, source_target_pairs={{0,6},{2,4},{4,2},{6,0},{8,14},{10,12},{12,10},{14,8},{16,22},{18,... | collective-permute-start | bytes 983048 | tf_op jit(solution)/shard_map/ppermute | solution.py:370
  34.3 6.0 %collective-permute-start.2 = (bf16[224,128]{1,0:T(8,128)(2,1)S(1)}, bf16[224,128]{1,0:T(8,128)(2,1)S(1)}, u32[]{:S(2)}, u32[]{:S(2)}) collective-permute-start(bf16[224,128]{1,0:T(8,128)(2,1)S(1)} %get-tuple-element.21.refs_0_), channel_id=1, source_target_pairs={{0,24},{2,26},{4,28},{6,30},{8,16},{10,18},{12,20},{14,22},{16,8},... | collective-permute-start | bytes 172040 | tf_op jit(solution)/shard_map/ppermute | solution.py:370
  40.3 5.6 %collective-permute-start.1 = (bf16[224,128]{1,0:T(8,128)(2,1)S(1)}, bf16[224,128]{1,0:T(8,128)(2,1)S(1)}, u32[]{:S(2)}, u32[]{:S(2)}) collective-permute-start(bf16[224,128]{1,0:T(8,128)(2,1)S(1)} %get-tuple-element.21.refs_0_), channel_id=1, source_target_pairs={{0,16},{2,18},{4,20},{6,22},{8,24},{10,26},{12,28},{14,30},{16,0},... | collective-permute-start | bytes 172040 | tf_op jit(solution)/shard_map/ppermute | solution.py:370
  45.9 4.2 %collective-permute-start = (bf16[224,128]{1,0:T(8,128)(2,1)S(1)}, bf16[224,128]{1,0:T(8,128)(2,1)S(1)}, u32[]{:S(2)}, u32[]{:S(2)}) collective-permute-start(bf16[224,128]{1,0:T(8,128)(2,1)S(1)} %get-tuple-element.21.refs_0_), channel_id=1, source_target_pairs={{0,8},{2,10},{4,12},{6,14},{8,0},{10,2},{12,4},{14,6},{16,24},{18,... | collective-permute-start | bytes 172040 | tf_op jit(solution)/shard_map/ppermute | solution.py:370
  50.1 1.0 copy-start.6
  53.7 27.6 %copy-start = (bf16[2560,320]{0,1:T(8,128)(2,1)S(1)}, bf16[2560,320]{0,1:T(8,128)(2,1)}, u32[]{:S(2)}) copy-start(bf16[2560,320]{0,1:T(8,128)(2,1)} %param.13) | copy-start | bytes 4915204
  57.1 4.5 %collective-permute-start.9 = (bf16[240,128]{1,0:T(8,128)(2,1)S(1)}, bf16[240,128]{1,0:T(8,128)(2,1)S(1)}, u32[]{:S(2)}, u32[]{:S(2)}) collective-permute-start(bf16[240,128]{1,0:T(8,128)(2,1)S(1)} %get-tuple-element.29), channel_id=1, source_target_pairs={{0,8},{2,10},{4,12},{6,14},{8,0},{10,2},{12,4},{14,6},{16,24},{18,... | collective-permute-start | bytes 184328 | tf_op jit(solution)/shard_map/ppermute | solution.py:370
  57.2 5.3 %collective-permute-start.10 = (bf16[240,128]{1,0:T(8,128)(2,1)S(1)}, bf16[240,128]{1,0:T(8,128)(2,1)S(1)}, u32[]{:S(2)}, u32[]{:S(2)}) collective-permute-start(bf16[240,128]{1,0:T(8,128)(2,1)S(1)} %get-tuple-element.30), channel_id=1, source_target_pairs={{0,16},{2,18},{4,20},{6,22},{8,24},{10,26},{12,28},{14,30},{16,0},... | collective-permute-start | bytes 184328 | tf_op jit(solution)/shard_map/ppermute | solution.py:370
  60.1 6.7 %collective-permute-start.11 = (bf16[240,128]{1,0:T(8,128)(2,1)S(1)}, bf16[240,128]{1,0:T(8,128)(2,1)S(1)}, u32[]{:S(2)}, u32[]{:S(2)}) collective-permute-start(bf16[240,128]{1,0:T(8,128)(2,1)S(1)} %get-tuple-element.31), channel_id=1, source_target_pairs={{0,24},{2,26},{4,28},{6,30},{8,16},{10,18},{12,20},{14,22},{16,8},... | collective-permute-start | bytes 184328 | tf_op jit(solution)/shard_map/ppermute | solution.py:370
  67.1 6.1 %collective-permute-start.14 = (bf16[224,128]{1,0:T(8,128)(2,1)S(1)}, bf16[224,128]{1,0:T(8,128)(2,1)S(1)}, u32[]{:S(2)}, u32[]{:S(2)}) collective-permute-start(bf16[224,128]{1,0:T(8,128)(2,1)S(1)} %shard_map.77.refs_0_), channel_id=1, source_target_pairs={{0,24},{2,26},{4,28},{6,30},{8,16},{10,18},{12,20},{14,22},{16,8},... | collective-permute-start | bytes 172040 | tf_op jit(solution)/shard_map/ppermute | solution.py:370
  68.4 5.9 %collective-permute-start.13 = (bf16[224,128]{1,0:T(8,128)(2,1)S(1)}, bf16[224,128]{1,0:T(8,128)(2,1)S(1)}, u32[]{:S(2)}, u32[]{:S(2)}) collective-permute-start(bf16[224,128]{1,0:T(8,128)(2,1)S(1)} %shard_map.77.refs_0_), channel_id=1, source_target_pairs={{0,16},{2,18},{4,20},{6,22},{8,24},{10,26},{12,28},{14,30},{16,0},... | collective-permute-start | bytes 172040 | tf_op jit(solution)/shard_map/ppermute | solution.py:370
  68.5 5.9 %collective-permute-start.12 = (bf16[224,128]{1,0:T(8,128)(2,1)S(1)}, bf16[224,128]{1,0:T(8,128)(2,1)S(1)}, u32[]{:S(2)}, u32[]{:S(2)}) collective-permute-start(bf16[224,128]{1,0:T(8,128)(2,1)S(1)} %shard_map.77.refs_0_), channel_id=1, source_target_pairs={{0,8},{2,10},{4,12},{6,14},{8,0},{10,2},{12,4},{14,6},{16,24},{18,... | collective-permute-start | bytes 172040 | tf_op jit(solution)/shard_map/ppermute | solution.py:370
  74.4 4.9 %collective-permute-start.15 = (bf16[448,128]{1,0:T(8,128)(2,1)S(1)}, bf16[448,128]{1,0:T(8,128)(2,1)S(1)}, u32[]{:S(2)}, u32[]{:S(2)}) collective-permute-start(bf16[448,128]{1,0:T(8,128)(2,1)S(1)} %get-tuple-element.32.refs_0_), channel_id=1, source_target_pairs={{0,2},{2,0},{4,6},{6,4},{8,10},{10,8},{12,14},{14,12},{16,18},{18,... | collective-permute-start | bytes 344072 | tf_op jit(solution)/shard_map/ppermute | solution.py:370
  75.6 5.2 %collective-permute-start.17 = (bf16[448,128]{1,0:T(8,128)(2,1)S(1)}, bf16[448,128]{1,0:T(8,128)(2,1)S(1)}, u32[]{:S(2)}, u32[]{:S(2)}) collective-permute-start(bf16[448,128]{1,0:T(8,128)(2,1)S(1)} %get-tuple-element.33.refs_1_), channel_id=1, source_target_pairs={{0,4},{2,6},{4,0},{6,2},{8,12},{10,14},{12,8},{14,10},{16,20},{18,... | collective-permute-start | bytes 344072 | tf_op jit(solution)/shard_map/ppermute | solution.py:370
  76.1 5.6 %collective-permute-start.20 = (bf16[448,128]{1,0:T(8,128)(2,1)S(1)}, bf16[448,128]{1,0:T(8,128)(2,1)S(1)}, u32[]{:S(2)}, u32[]{:S(2)}) collective-permute-start(bf16[448,128]{1,0:T(8,128)(2,1)S(1)} %get-tuple-element.33.refs_1_), channel_id=1, source_target_pairs={{0,2},{2,0},{4,6},{6,4},{8,10},{10,8},{12,14},{14,12},{16,18},{18,... | collective-permute-start | bytes 344072 | tf_op jit(solution)/shard_map/ppermute | solution.py:370
  78.0 4.8 %collective-permute-start.19 = (bf16[448,128]{1,0:T(8,128)(2,1)S(1)}, bf16[448,128]{1,0:T(8,128)(2,1)S(1)}, u32[]{:S(2)}, u32[]{:S(2)}) collective-permute-start(bf16[448,128]{1,0:T(8,128)(2,1)S(1)} %get-tuple-element.32.refs_0_), channel_id=1, source_target_pairs={{0,4},{2,6},{4,0},{6,2},{8,12},{10,14},{12,8},{14,10},{16,20},{18,... | collective-permute-start | bytes 344072 | tf_op jit(solution)/shard_map/ppermute | solution.py:370
  79.3 5.6 %collective-permute-start.16 = (bf16[448,128]{1,0:T(8,128)(2,1)S(1)}, bf16[448,128]{1,0:T(8,128)(2,1)S(1)}, u32[]{:S(2)}, u32[]{:S(2)}) collective-permute-start(bf16[448,128]{1,0:T(8,128)(2,1)S(1)} %collective-permute-done.15.refs_0_), channel_id=1, source_target_pairs={{0,4},{2,6},{4,0},{6,2},{8,12},{10,14},{12,8},{14,10},{16,20},{18,... | collective-permute-start | bytes 344072 | tf_op jit(solution)/shard_map/ppermute | solution.py:370
  80.8 5.3 %collective-permute-start.18 = (bf16[448,128]{1,0:T(8,128)(2,1)S(1)}, bf16[448,128]{1,0:T(8,128)(2,1)S(1)}, u32[]{:S(2)}, u32[]{:S(2)}) collective-permute-start(bf16[448,128]{1,0:T(8,128)(2,1)S(1)} %collective-permute-done.17.refs_1_), channel_id=1, source_target_pairs={{0,2},{2,0},{4,6},{6,4},{8,10},{10,8},{12,14},{14,12},{16,18},{18,... | collective-permute-start | bytes 344072 | tf_op jit(solution)/shard_map/ppermute | solution.py:370
  86.1 16.5 %copy-start.3 = (bf16[256,2560]{1,0:T(8,128)(2,1)S(1)}, bf16[256,2560]{1,0:T(8,128)(2,1)}, u32[]{:S(2)}) copy-start(bf16[256,2560]{1,0:T(8,128)(2,1)} %refs_2_.1) | copy-start | bytes 3932164
  86.1 16.5 %copy-start.4 = (bf16[256,2560]{1,0:T(8,128)(2,1)S(1)}, bf16[256,2560]{1,0:T(8,128)(2,1)}, u32[]{:S(2)}) copy-start(bf16[256,2560]{1,0:T(8,128)(2,1)} %refs_3_.1) | copy-start | bytes 3932164
  86.1 16.5 %copy-start.7 = (s32[256]{0:T(256)S(1)}, s32[256]{0:T(256)}, u32[]{:S(2)}) copy-start(s32[256]{0:T(256)} %param.12) | copy-start | bytes 3076
  100.8 1.7 %collective-permute-start.21 = (bf16[16,32,320]{2,1,0:T(8,128)(2,1)S(1)}, bf16[16,32,320]{2,1,0:T(8,128)(2,1)S(1)}, u32[]{:S(2)}, u32[]{:S(2)}) collective-permute-start(bf16[16,32,320]{2,1,0:T(8,128)(2,1)S(1)} %all_to_all.10.refs_0_), channel_id=1, source_target_pairs={{0,1},{1,0},{2,3},{3,2},{4,5},{5,4},{6,7},{7,6},{8,9},{9,8},{10,11... | collective-permute-start | bytes 983048 | tf_op jit(solution)/shard_map/ppermute | solution.py:472

commit v4 on v3

--- a/solution.py
+++ b/solution.py
@@ -298,13 +298,15 @@
             ((iota((cap, tok), 1) - offset == place) & (place < count)).astype(F32).astype(BF16)
         )
     pick = jnp.concatenate(picks, axis=0)
-    laid = jnp.dot(pick, proj.astype(BF16), preferred_element_type=F32).astype(BF16)
-    out_ref[...] = laid.reshape(devices, cap, w_ref.shape[0])
+    laid = jnp.dot(pick, proj.astype(BF16), preferred_element_type=F32)
+    for device in range(devices):
+        rows = laid[device * cap : (device + 1) * cap]
+        out_ref[device] = pack_rows(rows, cap, w_ref.shape[0]).astype(BF16)
 
 
 def update_kernel(plan, halves, half_ref, act_ref, *refs):
     *term_refs, hidden_ref, cached_ref, out_hbm, held_ref, sems = refs
-    cap, width = plan.cap, term_refs[0].shape[-1]
+    cap, width = plan.cap, hidden_ref.shape[1] * halves // plan.devices
     wide = math.lcm(width, HD)
     blocks, steps = wide // width, hidden_ref.shape[1] // wide
     chosen = own_selection(act_ref[...].astype(F32), cap)
@@ -320,7 +322,8 @@
             else:
                 sides = [[ref[i, step * blocks + j] for j in range(blocks)] for i in range(halves)]
             for side in sides:
-                terms.append(jnp.concatenate([b.astype(F32) for b in side], axis=1).astype(BF16))
+                wide_rows = [c for b in side for c in unpack_rows(b.astype(F32), cap, width)]
+                terms.append(jnp.concatenate(wide_rows, axis=1).astype(BF16))
         summed = lax.dot_general(
             jnp.concatenate([chosen] * len(terms), axis=0),
             jnp.concatenate(terms, axis=0),
@@ -335,6 +338,40 @@
         copies.append(copy)
     for copy in copies:
         copy.wait()
+
+
+def packing(cap, width):
+    whole, rest = divmod(width, HD)
+    blocks = [(i * cap, 0, cap, i * HD, 0, HD) for i in range(whole)]
+    if rest and HD % rest == 0 and cap % (HD // rest * TILE) == 0:
+        fold = cap * rest // HD
+        blocks += [(whole * cap, i * fold, fold, whole * HD, i * rest, rest) for i in range(HD // rest)]
+        return whole * cap + fold, blocks
+    if rest:
+        blocks.append((whole * cap, 0, cap, whole * HD, 0, rest))
+    return (whole + (1 if rest else 0)) * cap, blocks
+
+
+def pack_rows(rows, cap, width):
+    _, blocks = packing(cap, width)
+    pieces = {}
+    for first, row, count, column, lane, columns in blocks:
+        pieces.setdefault(first, []).append(rows[row : row + count, column : column + columns])
+    joined = []
+    for first in sorted(pieces):
+        side = jnp.concatenate(pieces[first], axis=1) if len(pieces[first]) > 1 else pieces[first][0]
+        if side.shape[1] < HD:
+            side = jnp.concatenate([side, jnp.zeros((side.shape[0], HD - side.shape[1]), side.dtype)], axis=1)
+        joined.append(side)
+    return jnp.concatenate(joined, axis=0)
+
+
+def unpack_rows(packed, cap, width):
+    _, blocks = packing(cap, width)
+    columns = {}
+    for first, row, count, column, lane, wide in blocks:
+        columns.setdefault(column, []).append(packed[first : first + count, lane : lane + wide])
+    return [jnp.concatenate(columns[c], axis=0) for c in sorted(columns)]
 
 
 def shape(*dims, dtype=BF16):
@@ -463,7 +500,7 @@
         )
     terms = call(
         partial(place_kernel, plan, QUAD - 1),
-        shape(devices, cap, columns), me, w_rows, *groups[QUAD - 1], proj, info,
+        shape(devices, packing(cap, columns)[0], HD), me, w_rows, *groups[QUAD - 1], proj, info,
     )
     arrived = exchange(terms)
 
@@ -471,7 +508,7 @@
     if halves == 2:
         term_args = [arrived, lax.ppermute(arrived, "head", [(0, 1), (1, 0)])]
     else:
-        split = arrived.reshape(halves, devices // halves, cap, columns)
+        split = arrived.reshape(halves, devices // halves, *arrived.shape[1:])
         term_args = [lax.all_to_all(split, "head", split_axis=0, concat_axis=0, tiled=True)]
     return call(
         partial(update_kernel, plan, halves),

time: 105 us -> 104 us (level)
  no operation moved by 1% of the time
where the time goes in v4:
time: 104 us
  waiting for transfers between devices  37.8 us (36%)
  starting transfers between devices  35.3 us (34%)
  Pallas kernels  15.3 us (15%)
  blocking collectives  13.2 us (13%)
  local copies, waits for them, and re-layouts  1.72 us (2%)
    ppermute x21, waiting for transfers between devices, shift(): return lax.ppermute(value, 'seq', pairs)  36.2 us
    ppermute x21, starting transfers between devices, shift(): return lax.ppermute(value, 'seq', pairs)  27 us
    pallas_call x11, Pallas kernels, call(): pl.pallas_call(kernel, out_shape=out_shape, in_specs=[spec(i, arg) for i,...  15.3 us
    all_to_all x1, blocking collectives, exchange(): return lax.all_to_all(value, 'seq', split_axis=0, concat_axis=0, tiled=True)  13.2 us
    all_to_all x1, starting transfers between devices, exchange(): return lax.all_to_all(value, 'seq', split_axis=0, concat_axis=0, tiled=True)  8.35 us
  transfers between devices with their start and end apart: 23, of which 14 were waited for; matrix products, arithmetic and copies ran while one was open for 0% of the time, Pallas kernels for 4%

profile of v4, /device:TPU:0, one launch (start us, length us, event | category | flops | bytes accessed | tf_op | source)
XLA Modules:
  0.0 103.5 jit_solution(6227130708268557944)
XLA Ops:
  0.0 4.9 %shard_map.73 = (bf16[16,72,128]{2,1,0:T(8,128)(2,1)}, bf16[256,640]{1,0:T(8,128)(2,1)}, bf16[256,640]{1,0:T(8,128)(2,1)}, bf16[256,640]{1,0:T(8,128)(2,1)}, bf1...) custom-call(s32[1,256]{1,0:T(1,128)} %bitcast.8, bf16[256,2560]{1,0:T(8,128)(2,1)} %q_hbm.1, ...), custom_call_target="tpu_custom_call" | custom-call | tf_op jit(solution)/shard_map/pallas_call | solution.py:387
  5.0 8.4 %all-to-all-start = ((bf16[16,72,128]{2,1,0:T(8,128)(2,1)}), bf16[16,72,128]{2,1,0:T(8,128)(2,1)S(1)}, u32[]{:S(2)}, u32[]{:S(2)}) async-start(bf16[16,72,128]{2,1,0:T(8,128)(2,1)} %get-tuple-element.20), calls=%async_computation | async-start | bytes 589824 | tf_op jit(solution)/shard_map/all_to_all | solution.py:402
  13.3 1.9 %collective-permute-start.3 = (bf16[256,640]{1,0:T(8,128)(2,1)}, bf16[256,640]{1,0:T(8,128)(2,1)S(1)}, u32[]{:S(2)}, u32[]{:S(2)}) collective-permute-start(bf16[256,640]{1,0:T(8,128)(2,1)} %get-tuple-element.22), channel_id=1, source_target_pairs={{0,2},{2,0},{4,6},{6,4},{8,10},{10,8},{12,14},{14,12},{16,18},{18,... | collective-permute-start | bytes 983048 | tf_op jit(solution)/shard_map/ppermute | solution.py:407
  15.2 0.2 collective-permute-start.4
  15.4 1.9 %collective-permute-start.5 = (bf16[256,640]{1,0:T(8,128)(2,1)}, bf16[256,640]{1,0:T(8,128)(2,1)S(1)}, u32[]{:S(2)}, u32[]{:S(2)}) collective-permute-start(bf16[256,640]{1,0:T(8,128)(2,1)} %get-tuple-element.24), channel_id=1, source_target_pairs={{0,4},{2,6},{4,0},{6,2},{8,12},{10,14},{12,8},{14,10},{16,20},{18,... | collective-permute-start | bytes 983048 | tf_op jit(solution)/shard_map/ppermute | solution.py:407
  17.3 0.2 collective-permute-start.6
  17.4 2.8 %collective-permute-start.7 = (bf16[256,640]{1,0:T(8,128)(2,1)}, bf16[256,640]{1,0:T(8,128)(2,1)}, u32[]{:S(2)}, u32[]{:S(2)}) collective-permute-start(bf16[256,640]{1,0:T(8,128)(2,1)} %get-tuple-element.26), channel_id=1, source_target_pairs={{0,6},{2,4},{4,2},{6,0},{8,14},{10,12},{12,10},{14,8},{16,22},{18,... | collective-permute-start | bytes 983048 | tf_op jit(solution)/shard_map/ppermute | solution.py:407
  20.2 6.9 %collective-permute-done.3.refs_4_ = bf16[256,640]{1,0:T(8,128)(2,1)S(1)} collective-permute-done((bf16[256,640]{1,0:T(8,128)(2,1)}, bf16[256,640]{1,0:T(8,128)(2,1)S(1)}, u32[]{:S(2)}, u32[]{:S(2)}) %collective-permute-start.3) | collective-permute-done | bytes 327712 | tf_op jit(solution)/shard_map/ppermute | solution.py:407
  27.1 0.7 copy-done.5
  27.9 1.6 %collective-permute-start.8 = (bf16[256,640]{1,0:T(8,128)(2,1)}, bf16[256,640]{1,0:T(8,128)(2,1)}, u32[]{:S(2)}, u32[]{:S(2)}) collective-permute-start(bf16[256,640]{1,0:T(8,128)(2,1)} %get-tuple-element.27), channel_id=1, source_target_pairs={{0,6},{2,4},{4,2},{6,0},{8,14},{10,12},{12,10},{14,8},{16,22},{18,... | collective-permute-start | bytes 983048 | tf_op jit(solution)/shard_map/ppermute | solution.py:407
  29.5 0.5 shard_map.74
  30.0 4.3 %collective-permute-done.4.refs_5_ = bf16[256,640]{1,0:T(8,128)(2,1)} collective-permute-done((bf16[256,640]{1,0:T(8,128)(2,1)}, bf16[256,640]{1,0:T(8,128)(2,1)}, u32[]{:S(2)}, u32[]{:S(2)}) %collective-permute-start.4) | collective-permute-done | bytes 327712 | tf_op jit(solution)/shard_map/ppermute | solution.py:407
  34.3 2.9 %collective-permute-start.2 = (bf16[224,128]{1,0:T(8,128)(2,1)S(1)}, bf16[224,128]{1,0:T(8,128)(2,1)S(1)}, u32[]{:S(2)}, u32[]{:S(2)}) collective-permute-start(bf16[224,128]{1,0:T(8,128)(2,1)S(1)} %get-tuple-element.21.refs_0_), channel_id=1, source_target_pairs={{0,24},{2,26},{4,28},{6,30},{8,16},{10,18},{12,20},{14,22},{16,8},... | collective-permute-start | bytes 172040 | tf_op jit(solution)/shard_map/ppermute | solution.py:407
  37.2 3.1 %collective-permute-done.2.refs_3_ = bf16[224,128]{1,0:T(8,128)(2,1)S(1)} collective-permute-done((bf16[224,128]{1,0:T(8,128)(2,1)S(1)}, bf16[224,128]{1,0:T(8,128)(2,1)S(1)}, u32[]{:S(2)}, u32[]{:S(2)}) %collective-permute-start.2) | collective-permute-done | bytes 57376 | tf_op jit(solution)/shard_map/ppermute | solution.py:407
  40.3 0.6 collective-permute-start.1
  40.8 5.1 %collective-permute-done.1.refs_2_ = bf16[224,128]{1,0:T(8,128)(2,1)S(1)} collective-permute-done((bf16[224,128]{1,0:T(8,128)(2,1)S(1)}, bf16[224,128]{1,0:T(8,128)(2,1)S(1)}, u32[]{:S(2)}, u32[]{:S(2)}) %collective-permute-start.1) | collective-permute-done | bytes 57376 | tf_op jit(solution)/shard_map/ppermute | solution.py:407
  45.9 0.0 collective-permute-start
  45.9 4.2 %collective-permute-done.refs_1_ = bf16[224,128]{1,0:T(8,128)(2,1)S(1)} collective-permute-done((bf16[224,128]{1,0:T(8,128)(2,1)S(1)}, bf16[224,128]{1,0:T(8,128)(2,1)S(1)}, u32[]{:S(2)}, u32[]{:S(2)}) %collective-permute-start) | collective-permute-done | bytes 57376 | tf_op jit(solution)/shard_map/ppermute | solution.py:407
  50.1 1.0 copy-done.6
  51.1 2.6 %shard_map.75.near_ref = bf16[4,240,128]{2,1,0:T(8,128)(2,1)S(1)} custom-call(s32[1]{0:T(128)} %bitcast.2.where_ref, bf16[224,128]{1,0:T(8,128)(2,1)S(1)} %get-tuple-element.21.refs_0_, bf16[224,128]{1,0:T(8,128)(2,1)S(1)} %collective-permute-done.refs_1_, bf16[224,128]{1,0:T(8,128)(2,1)S(1)} %collective-permute-done.1.refs_2_, ...), custom_call_target="tpu_custom_call" | custom-call | flops 230686720 | bytes 1310720 | tf_op jit(solution)/shard_map/pallas_call | solution.py:387
  53.7 3.4 %shard_map.76 = (bf16[240,128]{1,0:T(8,128)(2,1)S(1)}, bf16[240,128]{1,0:T(8,128)(2,1)S(1)}, bf16[240,128]{1,0:T(8,128)(2,1)S(1)}, bf16[240,128]{1,0:T(8,128)(2,1)S(1)}) custom-call(s32[1]{0:T(128)} %bitcast.2.where_ref, bf16[4,240,128]{2,1,0:T(8,128)(2,1)S(1)} %shard_map.75.near_ref, bf16[224,128]{1,0:T(8,128)(2,1)S(1)} %get-tuple-element.21.refs_0_, ...), custom_call_target="tpu_custom_call" | custom-call | flops 230686720 | bytes 1310720 | tf_op jit(solution)/shard_map/pallas_call | solution.py:387
  57.1 0.1 collective-permute-start.9
  57.2 2.9 %collective-permute-start.10 = (bf16[240,128]{1,0:T(8,128)(2,1)S(1)}, bf16[240,128]{1,0:T(8,128)(2,1)S(1)}, u32[]{:S(2)}, u32[]{:S(2)}) collective-permute-start(bf16[240,128]{1,0:T(8,128)(2,1)S(1)} %get-tuple-element.30), channel_id=1, source_target_pairs={{0,16},{2,18},{4,20},{6,22},{8,24},{10,26},{12,28},{14,30},{16,0},... | collective-permute-start | bytes 184328 | tf_op jit(solution)/shard_map/ppermute | solution.py:407
  60.1 1.5 %collective-permute-start.11 = (bf16[240,128]{1,0:T(8,128)(2,1)S(1)}, bf16[240,128]{1,0:T(8,128)(2,1)S(1)}, u32[]{:S(2)}, u32[]{:S(2)}) collective-permute-start(bf16[240,128]{1,0:T(8,128)(2,1)S(1)} %get-tuple-element.31), channel_id=1, source_target_pairs={{0,24},{2,26},{4,28},{6,30},{8,16},{10,18},{12,20},{14,22},{16,8},... | collective-permute-start | bytes 184328 | tf_op jit(solution)/shard_map/ppermute | solution.py:407
  61.6 1.0 collective-permute-done.10.refs_2_
  62.6 4.2 %collective-permute-done.11.refs_3_ = bf16[240,128]{1,0:T(8,128)(2,1)S(1)} collective-permute-done((bf16[240,128]{1,0:T(8,128)(2,1)S(1)}, bf16[240,128]{1,0:T(8,128)(2,1)S(1)}, u32[]{:S(2)}, u32[]{:S(2)}) %collective-permute-start.11) | collective-permute-done | bytes 61472 | tf_op jit(solution)/shard_map/ppermute | solution.py:407
  66.8 0.3 shard_map.77.refs_0_
  67.1 1.4 %collective-permute-start.14 = (bf16[224,128]{1,0:T(8,128)(2,1)S(1)}, bf16[224,128]{1,0:T(8,128)(2,1)S(1)}, u32[]{:S(2)}, u32[]{:S(2)}) collective-permute-start(bf16[224,128]{1,0:T(8,128)(2,1)S(1)} %shard_map.77.refs_0_), channel_id=1, source_target_pairs={{0,24},{2,26},{4,28},{6,30},{8,16},{10,18},{12,20},{14,22},{16,8},... | collective-permute-start | bytes 172040 | tf_op jit(solution)/shard_map/ppermute | solution.py:407
  68.5 3.1 %collective-permute-start.12 = (bf16[224,128]{1,0:T(8,128)(2,1)S(1)}, bf16[224,128]{1,0:T(8,128)(2,1)S(1)}, u32[]{:S(2)}, u32[]{:S(2)}) collective-permute-start(bf16[224,128]{1,0:T(8,128)(2,1)S(1)} %shard_map.77.refs_0_), channel_id=1, source_target_pairs={{0,8},{2,10},{4,12},{6,14},{8,0},{10,2},{12,4},{14,6},{16,24},{18,... | collective-permute-start | bytes 172040 | tf_op jit(solution)/shard_map/ppermute | solution.py:407
  71.5 1.6 %collective-permute-done.14.refs_3_ = bf16[224,128]{1,0:T(8,128)(2,1)S(1)} collective-permute-done((bf16[224,128]{1,0:T(8,128)(2,1)S(1)}, bf16[224,128]{1,0:T(8,128)(2,1)S(1)}, u32[]{:S(2)}, u32[]{:S(2)}) %collective-permute-start.14) | collective-permute-done | bytes 57376 | tf_op jit(solution)/shard_map/ppermute | solution.py:407
  73.2 1.2 %collective-permute-done.13.refs_2_ = bf16[224,128]{1,0:T(8,128)(2,1)S(1)} collective-permute-done((bf16[224,128]{1,0:T(8,128)(2,1)S(1)}, bf16[224,128]{1,0:T(8,128)(2,1)S(1)}, u32[]{:S(2)}, u32[]{:S(2)}) %collective-permute-start.13) | collective-permute-done | bytes 57376 | tf_op jit(solution)/shard_map/ppermute | solution.py:407
  74.4 1.2 %collective-permute-start.15 = (bf16[448,128]{1,0:T(8,128)(2,1)S(1)}, bf16[448,128]{1,0:T(8,128)(2,1)S(1)}, u32[]{:S(2)}, u32[]{:S(2)}) collective-permute-start(bf16[448,128]{1,0:T(8,128)(2,1)S(1)} %get-tuple-element.32.refs_0_), channel_id=1, source_target_pairs={{0,2},{2,0},{4,6},{6,4},{8,10},{10,8},{12,14},{14,12},{16,18},{18,... | collective-permute-start | bytes 344072 | tf_op jit(solution)/shard_map/ppermute | solution.py:407
  75.6 0.5 collective-permute-start.17
  76.1 1.9 %collective-permute-start.20 = (bf16[448,128]{1,0:T(8,128)(2,1)S(1)}, bf16[448,128]{1,0:T(8,128)(2,1)S(1)}, u32[]{:S(2)}, u32[]{:S(2)}) collective-permute-start(bf16[448,128]{1,0:T(8,128)(2,1)S(1)} %get-tuple-element.33.refs_1_), channel_id=1, source_target_pairs={{0,2},{2,0},{4,6},{6,4},{8,10},{10,8},{12,14},{14,12},{16,18},{18,... | collective-permute-start | bytes 344072 | tf_op jit(solution)/shard_map/ppermute | solution.py:407
  78.0 0.5 collective-permute-start.19
  78.5 0.7 collective-permute-done.15.refs_0_
  79.3 1.5 %collective-permute-start.16 = (bf16[448,128]{1,0:T(8,128)(2,1)S(1)}, bf16[448,128]{1,0:T(8,128)(2,1)S(1)}, u32[]{:S(2)}, u32[]{:S(2)}) collective-permute-start(bf16[448,128]{1,0:T(8,128)(2,1)S(1)} %collective-permute-done.15.refs_0_), channel_id=1, source_target_pairs={{0,4},{2,6},{4,0},{6,2},{8,12},{10,14},{12,8},{14,10},{16,20},{18,... | collective-permute-start | bytes 344072 | tf_op jit(solution)/shard_map/ppermute | solution.py:407
  80.8 0.5 collective-permute-start.18
  81.3 0.3 shard_map.79.refs_2_
  81.6 0.3 shard_map.80.refs_2_
  82.0 0.8 collective-permute-done.19.refs_0_
  82.8 0.3 shard_map.81.sum_ref
  83.1 1.6 %collective-permute-done.16.low_ref = bf16[448,128]{1,0:T(8,128)(2,1)S(1)} collective-permute-done((bf16[448,128]{1,0:T(8,128)(2,1)S(1)}, bf16[448,128]{1,0:T(8,128)(2,1)S(1)}, u32[]{:S(2)}, u32[]{:S(2)}) %collective-permute-start.16) | collective-permute-done | bytes 114720 | tf_op jit(solution)/shard_map/ppermute | solution.py:407
  84.7 1.4 %collective-permute-done.18.high_ref = bf16[448,128]{1,0:T(8,128)(2,1)S(1)} collective-permute-done((bf16[448,128]{1,0:T(8,128)(2,1)S(1)}, bf16[448,128]{1,0:T(8,128)(2,1)S(1)}, u32[]{:S(2)}, u32[]{:S(2)}) %collective-permute-start.18) | collective-permute-done | bytes 114720 | tf_op jit(solution)/shard_map/ppermute | solution.py:407
  86.1 0.7 shard_map.82
  86.9 13.2 %all_to_all.10.refs_0_ = bf16[16,80,128]{2,1,0:T(8,128)(2,1)S(1)} all-to-all(bf16[16,80,128]{2,1,0:T(8,128)(2,1)S(1)} %shard_map.82), channel_id=1, replica_groups=mesh['seq'=16,'head'=2] {'seq'}, dimensions={0} | all-to-all | bytes 655360 | tf_op jit(solution)/shard_map/all_to_all | solution.py:402
  100.1 1.6 %collective-permute-done.21.refs_1_ = bf16[16,80,128]{2,1,0:T(8,128)(2,1)S(1)} collective-permute-done((bf16[16,80,128]{2,1,0:T(8,128)(2,1)S(1)}, bf16[16,80,128]{2,1,0:T(8,128)(2,1)S(1)}, u32[]{:S(2)}, u32[]{:S(2)}) %collective-permute-start.21) | collective-permute-done | bytes 327712 | tf_op jit(solution)/shard_map/ppermute | solution.py:509
  101.7 1.8 %shard_map.83 = bf16[256,2560]{1,0:T(8,128)(2,1)} custom-call(s32[1]{0:T(128)} %bitcast.half_ref, s32[1,256]{1,0:T(1,128)S(1)} %bitcast.9, bf16[16,80,128]{2,1,0:T(8,128)(2,1)S(1)} %all_to_all.10.refs_0_, bf16[16,80,128]{2,1,0:T(8,128)(2,1)S(1)} %collective-permute-done.21.refs_1_, bf16[256,2560]{1,0:T(8,128)(2,1)S(1)} %copy-done.3, ...), custom_call_target="tpu_custom_call" | custom-call | tf_op jit(solution)/shard_map/pallas_call | solution.py:387
  (26 shorter events, 0.1 us)
Async XLA Ops:
  0.0 50.1 %copy-start.1 = (bf16[256,2560]{1,0:T(8,128)(2,1)S(1)}, bf16[256,2560]{1,0:T(8,128)(2,1)}, u32[]{:S(2)}) copy-start(bf16[256,2560]{1,0:T(8,128)(2,1)} %refs_6_.1) | copy-start | bytes 3932164
  0.0 50.1 %copy-start.2 = (bf16[256,2560]{1,0:T(8,128)(2,1)S(1)}, bf16[256,2560]{1,0:T(8,128)(2,1)}, u32[]{:S(2)}) copy-start(bf16[256,2560]{1,0:T(8,128)(2,1)} %refs_7_.1) | copy-start | bytes 3932164
  5.0 24.5 %all-to-all-start = ((bf16[16,72,128]{2,1,0:T(8,128)(2,1)}), bf16[16,72,128]{2,1,0:T(8,128)(2,1)S(1)}, u32[]{:S(2)}, u32[]{:S(2)}) async-start(bf16[16,72,128]{2,1,0:T(8,128)(2,1)} %get-tuple-element.20), calls=%async_computation | async-start | bytes 589824 | tf_op jit(solution)/shard_map/all_to_all | solution.py:402
  13.3 13.8 %collective-permute-start.3 = (bf16[256,640]{1,0:T(8,128)(2,1)}, bf16[256,640]{1,0:T(8,128)(2,1)S(1)}, u32[]{:S(2)}, u32[]{:S(2)}) collective-permute-start(bf16[256,640]{1,0:T(8,128)(2,1)} %get-tuple-element.22), channel_id=1, source_target_pairs={{0,2},{2,0},{4,6},{6,4},{8,10},{10,8},{12,14},{14,12},{16,18},{18,... | collective-permute-start | bytes 983048 | tf_op jit(solution)/shard_map/ppermute | solution.py:407
  15.2 19.0 %collective-permute-start.4 = (bf16[256,640]{1,0:T(8,128)(2,1)}, bf16[256,640]{1,0:T(8,128)(2,1)}, u32[]{:S(2)}, u32[]{:S(2)}) collective-permute-start(bf16[256,640]{1,0:T(8,128)(2,1)} %get-tuple-element.23), channel_id=1, source_target_pairs={{0,2},{2,0},{4,6},{6,4},{8,10},{10,8},{12,14},{14,12},{16,18},{18,... | collective-permute-start | bytes 983048 | tf_op jit(solution)/shard_map/ppermute | solution.py:407
  15.4 38.3 %collective-permute-start.5 = (bf16[256,640]{1,0:T(8,128)(2,1)}, bf16[256,640]{1,0:T(8,128)(2,1)S(1)}, u32[]{:S(2)}, u32[]{:S(2)}) collective-permute-start(bf16[256,640]{1,0:T(8,128)(2,1)} %get-tuple-element.24), channel_id=1, source_target_pairs={{0,4},{2,6},{4,0},{6,2},{8,12},{10,14},{12,8},{14,10},{16,20},{18,... | collective-permute-start | bytes 983048 | tf_op jit(solution)/shard_map/ppermute | solution.py:407
  17.3 36.4 %collective-permute-start.6 = (bf16[256,640]{1,0:T(8,128)(2,1)}, bf16[256,640]{1,0:T(8,128)(2,1)}, u32[]{:S(2)}, u32[]{:S(2)}) collective-permute-start(bf16[256,640]{1,0:T(8,128)(2,1)} %get-tuple-element.25), channel_id=1, source_target_pairs={{0,4},{2,6},{4,0},{6,2},{8,12},{10,14},{12,8},{14,10},{16,20},{18,... | collective-permute-start | bytes 983048 | tf_op jit(solution)/shard_map/ppermute | solution.py:407
  17.4 36.3 %collective-permute-start.7 = (bf16[256,640]{1,0:T(8,128)(2,1)}, bf16[256,640]{1,0:T(8,128)(2,1)}, u32[]{:S(2)}, u32[]{:S(2)}) collective-permute-start(bf16[256,640]{1,0:T(8,128)(2,1)} %get-tuple-element.26), channel_id=1, source_target_pairs={{0,6},{2,4},{4,2},{6,0},{8,14},{10,12},{12,10},{14,8},{16,22},{18,... | collective-permute-start | bytes 983048 | tf_op jit(solution)/shard_map/ppermute | solution.py:407
  27.1 0.7 copy-start.5
  27.9 25.8 %collective-permute-start.8 = (bf16[256,640]{1,0:T(8,128)(2,1)}, bf16[256,640]{1,0:T(8,128)(2,1)}, u32[]{:S(2)}, u32[]{:S(2)}) collective-permute-start(bf16[256,640]{1,0:T(8,128)(2,1)} %get-tuple-element.27), channel_id=1, source_target_pairs={{0,6},{2,4},{4,2},{6,0},{8,14},{10,12},{12,10},{14,8},{16,22},{18,... | collective-permute-start | bytes 983048 | tf_op jit(solution)/shard_map/ppermute | solution.py:407
  34.3 6.0 %collective-permute-start.2 = (bf16[224,128]{1,0:T(8,128)(2,1)S(1)}, bf16[224,128]{1,0:T(8,128)(2,1)S(1)}, u32[]{:S(2)}, u32[]{:S(2)}) collective-permute-start(bf16[224,128]{1,0:T(8,128)(2,1)S(1)} %get-tuple-element.21.refs_0_), channel_id=1, source_target_pairs={{0,24},{2,26},{4,28},{6,30},{8,16},{10,18},{12,20},{14,22},{16,8},... | collective-permute-start | bytes 172040 | tf_op jit(solution)/shard_map/ppermute | solution.py:407
  40.3 5.6 %collective-permute-start.1 = (bf16[224,128]{1,0:T(8,128)(2,1)S(1)}, bf16[224,128]{1,0:T(8,128)(2,1)S(1)}, u32[]{:S(2)}, u32[]{:S(2)}) collective-permute-start(bf16[224,128]{1,0:T(8,128)(2,1)S(1)} %get-tuple-element.21.refs_0_), channel_id=1, source_target_pairs={{0,16},{2,18},{4,20},{6,22},{8,24},{10,26},{12,28},{14,30},{16,0},... | collective-permute-start | bytes 172040 | tf_op jit(solution)/shard_map/ppermute | solution.py:407
  45.9 4.2 %collective-permute-start = (bf16[224,128]{1,0:T(8,128)(2,1)S(1)}, bf16[224,128]{1,0:T(8,128)(2,1)S(1)}, u32[]{:S(2)}, u32[]{:S(2)}) collective-permute-start(bf16[224,128]{1,0:T(8,128)(2,1)S(1)} %get-tuple-element.21.refs_0_), channel_id=1, source_target_pairs={{0,8},{2,10},{4,12},{6,14},{8,0},{10,2},{12,4},{14,6},{16,24},{18,... | collective-permute-start | bytes 172040 | tf_op jit(solution)/shard_map/ppermute | solution.py:407
  50.1 1.0 copy-start.6
  53.7 27.6 %copy-start = (bf16[2560,320]{0,1:T(8,128)(2,1)S(1)}, bf16[2560,320]{0,1:T(8,128)(2,1)}, u32[]{:S(2)}) copy-start(bf16[2560,320]{0,1:T(8,128)(2,1)} %param.13) | copy-start | bytes 4915204
  57.1 4.5 %collective-permute-start.9 = (bf16[240,128]{1,0:T(8,128)(2,1)S(1)}, bf16[240,128]{1,0:T(8,128)(2,1)S(1)}, u32[]{:S(2)}, u32[]{:S(2)}) collective-permute-start(bf16[240,128]{1,0:T(8,128)(2,1)S(1)} %get-tuple-element.29), channel_id=1, source_target_pairs={{0,8},{2,10},{4,12},{6,14},{8,0},{10,2},{12,4},{14,6},{16,24},{18,... | collective-permute-start | bytes 184328 | tf_op jit(solution)/shard_map/ppermute | solution.py:407
  57.2 5.3 %collective-permute-start.10 = (bf16[240,128]{1,0:T(8,128)(2,1)S(1)}, bf16[240,128]{1,0:T(8,128)(2,1)S(1)}, u32[]{:S(2)}, u32[]{:S(2)}) collective-permute-start(bf16[240,128]{1,0:T(8,128)(2,1)S(1)} %get-tuple-element.30), channel_id=1, source_target_pairs={{0,16},{2,18},{4,20},{6,22},{8,24},{10,26},{12,28},{14,30},{16,0},... | collective-permute-start | bytes 184328 | tf_op jit(solution)/shard_map/ppermute | solution.py:407
  60.1 6.7 %collective-permute-start.11 = (bf16[240,128]{1,0:T(8,128)(2,1)S(1)}, bf16[240,128]{1,0:T(8,128)(2,1)S(1)}, u32[]{:S(2)}, u32[]{:S(2)}) collective-permute-start(bf16[240,128]{1,0:T(8,128)(2,1)S(1)} %get-tuple-element.31), channel_id=1, source_target_pairs={{0,24},{2,26},{4,28},{6,30},{8,16},{10,18},{12,20},{14,22},{16,8},... | collective-permute-start | bytes 184328 | tf_op jit(solution)/shard_map/ppermute | solution.py:407
  67.1 6.1 %collective-permute-start.14 = (bf16[224,128]{1,0:T(8,128)(2,1)S(1)}, bf16[224,128]{1,0:T(8,128)(2,1)S(1)}, u32[]{:S(2)}, u32[]{:S(2)}) collective-permute-start(bf16[224,128]{1,0:T(8,128)(2,1)S(1)} %shard_map.77.refs_0_), channel_id=1, source_target_pairs={{0,24},{2,26},{4,28},{6,30},{8,16},{10,18},{12,20},{14,22},{16,8},... | collective-permute-start | bytes 172040 | tf_op jit(solution)/shard_map/ppermute | solution.py:407
  68.4 5.9 %collective-permute-start.13 = (bf16[224,128]{1,0:T(8,128)(2,1)S(1)}, bf16[224,128]{1,0:T(8,128)(2,1)S(1)}, u32[]{:S(2)}, u32[]{:S(2)}) collective-permute-start(bf16[224,128]{1,0:T(8,128)(2,1)S(1)} %shard_map.77.refs_0_), channel_id=1, source_target_pairs={{0,16},{2,18},{4,20},{6,22},{8,24},{10,26},{12,28},{14,30},{16,0},... | collective-permute-start | bytes 172040 | tf_op jit(solution)/shard_map/ppermute | solution.py:407
  68.5 5.9 %collective-permute-start.12 = (bf16[224,128]{1,0:T(8,128)(2,1)S(1)}, bf16[224,128]{1,0:T(8,128)(2,1)S(1)}, u32[]{:S(2)}, u32[]{:S(2)}) collective-permute-start(bf16[224,128]{1,0:T(8,128)(2,1)S(1)} %shard_map.77.refs_0_), channel_id=1, source_target_pairs={{0,8},{2,10},{4,12},{6,14},{8,0},{10,2},{12,4},{14,6},{16,24},{18,... | collective-permute-start | bytes 172040 | tf_op jit(solution)/shard_map/ppermute | solution.py:407
  74.4 4.9 %collective-permute-start.15 = (bf16[448,128]{1,0:T(8,128)(2,1)S(1)}, bf16[448,128]{1,0:T(8,128)(2,1)S(1)}, u32[]{:S(2)}, u32[]{:S(2)}) collective-permute-start(bf16[448,128]{1,0:T(8,128)(2,1)S(1)} %get-tuple-element.32.refs_0_), channel_id=1, source_target_pairs={{0,2},{2,0},{4,6},{6,4},{8,10},{10,8},{12,14},{14,12},{16,18},{18,... | collective-permute-start | bytes 344072 | tf_op jit(solution)/shard_map/ppermute | solution.py:407
  75.6 5.2 %collective-permute-start.17 = (bf16[448,128]{1,0:T(8,128)(2,1)S(1)}, bf16[448,128]{1,0:T(8,128)(2,1)S(1)}, u32[]{:S(2)}, u32[]{:S(2)}) collective-permute-start(bf16[448,128]{1,0:T(8,128)(2,1)S(1)} %get-tuple-element.33.refs_1_), channel_id=1, source_target_pairs={{0,4},{2,6},{4,0},{6,2},{8,12},{10,14},{12,8},{14,10},{16,20},{18,... | collective-permute-start | bytes 344072 | tf_op jit(solution)/shard_map/ppermute | solution.py:407
  76.1 5.6 %collective-permute-start.20 = (bf16[448,128]{1,0:T(8,128)(2,1)S(1)}, bf16[448,128]{1,0:T(8,128)(2,1)S(1)}, u32[]{:S(2)}, u32[]{:S(2)}) collective-permute-start(bf16[448,128]{1,0:T(8,128)(2,1)S(1)} %get-tuple-element.33.refs_1_), channel_id=1, source_target_pairs={{0,2},{2,0},{4,6},{6,4},{8,10},{10,8},{12,14},{14,12},{16,18},{18,... | collective-permute-start | bytes 344072 | tf_op jit(solution)/shard_map/ppermute | solution.py:407
  78.0 4.8 %collective-permute-start.19 = (bf16[448,128]{1,0:T(8,128)(2,1)S(1)}, bf16[448,128]{1,0:T(8,128)(2,1)S(1)}, u32[]{:S(2)}, u32[]{:S(2)}) collective-permute-start(bf16[448,128]{1,0:T(8,128)(2,1)S(1)} %get-tuple-element.32.refs_0_), channel_id=1, source_target_pairs={{0,4},{2,6},{4,0},{6,2},{8,12},{10,14},{12,8},{14,10},{16,20},{18,... | collective-permute-start | bytes 344072 | tf_op jit(solution)/shard_map/ppermute | solution.py:407
  79.3 5.5 %collective-permute-start.16 = (bf16[448,128]{1,0:T(8,128)(2,1)S(1)}, bf16[448,128]{1,0:T(8,128)(2,1)S(1)}, u32[]{:S(2)}, u32[]{:S(2)}) collective-permute-start(bf16[448,128]{1,0:T(8,128)(2,1)S(1)} %collective-permute-done.15.refs_0_), channel_id=1, source_target_pairs={{0,4},{2,6},{4,0},{6,2},{8,12},{10,14},{12,8},{14,10},{16,20},{18,... | collective-permute-start | bytes 344072 | tf_op jit(solution)/shard_map/ppermute | solution.py:407
  80.8 5.4 %collective-permute-start.18 = (bf16[448,128]{1,0:T(8,128)(2,1)S(1)}, bf16[448,128]{1,0:T(8,128)(2,1)S(1)}, u32[]{:S(2)}, u32[]{:S(2)}) collective-permute-start(bf16[448,128]{1,0:T(8,128)(2,1)S(1)} %collective-permute-done.17.refs_1_), channel_id=1, source_target_pairs={{0,2},{2,0},{4,6},{6,4},{8,10},{10,8},{12,14},{14,12},{16,18},{18,... | collective-permute-start | bytes 344072 | tf_op jit(solution)/shard_map/ppermute | solution.py:407
  86.1 15.6 %copy-start.3 = (bf16[256,2560]{1,0:T(8,128)(2,1)S(1)}, bf16[256,2560]{1,0:T(8,128)(2,1)}, u32[]{:S(2)}) copy-start(bf16[256,2560]{1,0:T(8,128)(2,1)} %refs_2_.1) | copy-start | bytes 3932164
  86.1 15.6 %copy-start.4 = (bf16[256,2560]{1,0:T(8,128)(2,1)S(1)}, bf16[256,2560]{1,0:T(8,128)(2,1)}, u32[]{:S(2)}) copy-start(bf16[256,2560]{1,0:T(8,128)(2,1)} %refs_3_.1) | copy-start | bytes 3932164
  86.1 15.6 %copy-start.7 = (s32[256]{0:T(256)S(1)}, s32[256]{0:T(256)}, u32[]{:S(2)}) copy-start(s32[256]{0:T(256)} %param.12) | copy-start | bytes 3076
  100.1 1.6 %collective-permute-start.21 = (bf16[16,80,128]{2,1,0:T(8,128)(2,1)S(1)}, bf16[16,80,128]{2,1,0:T(8,128)(2,1)S(1)}, u32[]{:S(2)}, u32[]{:S(2)}) collective-permute-start(bf16[16,80,128]{2,1,0:T(8,128)(2,1)S(1)} %all_to_all.10.refs_0_), channel_id=1, source_target_pairs={{0,1},{1,0},{2,3},{3,2},{4,5},{5,4},{6,7},{7,6},{8,9},{9,8},{10,11... | collective-permute-start | bytes 983048 | tf_op jit(solution)/shard_map/ppermute | solution.py:509

commit v5 on v4

--- a/solution.py
+++ b/solution.py
@@ -78,19 +78,17 @@
 
 def prepare_kernel(plan, parts, wanted, act_hbm, q_hbm, k_hbm, v_hbm, *refs):
     out_ref, *fetched = refs[: 1 + len(wanted)]
-    act_ref, q_ref, own_ref, passing, q_sems, in_sems, out_sems = refs[1 + len(wanted) :]
+    act_ref, q_ref, own_ref, q_sems, in_sems = refs[1 + len(wanted) :]
     me = lax.axis_index("seq")
     heads = plan.own_heads
-    arriving, leaving = [], []
-    for j, (source, step) in enumerate(wanted):
+    arriving = []
+    for (source, step), ref in zip(wanted, fetched):
         quad = lax.rem(me, QUAD) ^ step
         for i in range(heads):
             columns = pl.ds(pl.multiple_of(plan.head_at(i, quad) * HD, HD), HD)
-            n = j * heads + i
             taken = (k_hbm, v_hbm)[source].at[:, columns]
-            target = fetched[j].at[:, i * HD : (i + 1) * HD]
-            arriving.append(pltpu.make_async_copy(taken, passing.at[n], in_sems.at[n]))
-            leaving.append(pltpu.make_async_copy(passing.at[n], target, out_sems.at[n]))
+            target = ref.at[:, i * HD : (i + 1) * HD]
+            arriving.append(pltpu.make_async_copy(taken, target, in_sems.at[len(arriving)]))
     wide = q_hbm.shape[1] // parts
     columns = [slice(i * wide, (i + 1) * wide) for i in range(parts)]
     queries = [
@@ -102,25 +100,18 @@
     for copy in [first, *arriving[:early], *queries, *arriving[early:]]:
         copy.start()
 
-    def forward(low, high):
-        for one, two in zip(arriving[low:high], leaving[low:high]):
-            one.wait()
-            two.start()
-
     first.wait()
     act = act_ref[...].astype(F32)
     chosen = own_selection(act, plan.cap)
     count = jnp.broadcast_to(jnp.sum(act, axis=1, keepdims=True), (8, HD)).astype(BF16)
-    forward(0, early)
     for copy, c in zip(queries, columns):
         copy.wait()
         own_ref[:, c] = jnp.dot(chosen, q_ref[:, c], preferred_element_type=F32).astype(BF16)
-    forward(early, len(arriving))
     for device in range(plan.devices):
         for i, head in enumerate(plan.sent_heads(device)):
             out_ref[device, i * plan.cap : (i + 1) * plan.cap, :] = own_ref[:, head * HD : (head + 1) * HD]
         out_ref[device, plan.spans * plan.cap :, :] = count
-    for copy in leaving:
+    for copy in arriving:
         copy.wait()
 
 
@@ -436,13 +427,12 @@
             shape(devices, plan.spans * cap + 8, HD),
             *[shape(tok_dev, plan.own_heads * HD) for _ in wanted],
         ),
-        act, queries, keys, values, hbm=range(4), out_hbm=range(1, 1 + len(wanted)), grant=56,
+        act, queries, keys, values, hbm=range(4), grant=56,
         scratch_shapes=[
             pltpu.VMEM((1, tok_dev), jnp.int32),
             pltpu.VMEM((tok_dev, features), BF16),
             pltpu.VMEM((cap, features), BF16),
-            pltpu.VMEM((blocks, tok_dev, HD), BF16),
-            dma((parts + 1,)), dma((blocks,)), dma((blocks,)),
+            dma((parts + 1,)), dma((blocks,)),
         ],
     )
     near_k = [shift(part, i + 1) for i, part in enumerate(near_k)]

time: 104 us -> 103 us (level)
  no operation moved by 1% of the time
where the time goes in v5:
time: 103 us
  waiting for transfers between devices  37.8 us (37%)
  starting transfers between devices  35.3 us (34%)
  Pallas kernels  14.7 us (14%)
  blocking collectives  13.2 us (13%)
  local copies, waits for them, and re-layouts  1.72 us (2%)
    ppermute x21, waiting for transfers between devices, shift(): return lax.ppermute(value, 'seq', pairs)  36.2 us
    ppermute x21, starting transfers between devices, shift(): return lax.ppermute(value, 'seq', pairs)  27 us
    pallas_call x11, Pallas kernels, call(): pl.pallas_call(kernel, out_shape=out_shape, in_specs=[spec(i, arg) for i,...  14.7 us
    all_to_all x1, blocking collectives, exchange(): return lax.all_to_all(value, 'seq', split_axis=0, concat_axis=0, tiled=True)  13.2 us
    all_to_all x1, starting transfers between devices, exchange(): return lax.all_to_all(value, 'seq', split_axis=0, concat_axis=0, tiled=True)  8.36 us
  transfers between devices with their start and end apart: 23, of which 14 were waited for; matrix products, arithmetic and copies ran while one was open for 0% of the time, Pallas kernels for 4%

profile of v5, /device:TPU:0, one launch (start us, length us, event | category | flops | bytes accessed | tf_op | source)
XLA Modules:
  0.0 102.9 jit_solution(6686016852853207759)
XLA Ops:
  0.0 4.3 %shard_map.73 = (bf16[16,72,128]{2,1,0:T(8,128)(2,1)}, bf16[256,640]{1,0:T(8,128)(2,1)}, bf16[256,640]{1,0:T(8,128)(2,1)}, bf16[256,640]{1,0:T(8,128)(2,1)}, bf1...) custom-call(s32[1,256]{1,0:T(1,128)} %bitcast.8, bf16[256,2560]{1,0:T(8,128)(2,1)} %q_hbm.1, ...), custom_call_target="tpu_custom_call" | custom-call | tf_op jit(solution)/shard_map/pallas_call | solution.py:378
  4.3 8.4 %all-to-all-start = ((bf16[16,72,128]{2,1,0:T(8,128)(2,1)}), bf16[16,72,128]{2,1,0:T(8,128)(2,1)S(1)}, u32[]{:S(2)}, u32[]{:S(2)}) async-start(bf16[16,72,128]{2,1,0:T(8,128)(2,1)} %get-tuple-element.20), calls=%async_computation | async-start | bytes 589824 | tf_op jit(solution)/shard_map/all_to_all | solution.py:393
  12.7 1.9 %collective-permute-start.3 = (bf16[256,640]{1,0:T(8,128)(2,1)}, bf16[256,640]{1,0:T(8,128)(2,1)S(1)}, u32[]{:S(2)}, u32[]{:S(2)}) collective-permute-start(bf16[256,640]{1,0:T(8,128)(2,1)} %get-tuple-element.22), channel_id=1, source_target_pairs={{0,2},{2,0},{4,6},{6,4},{8,10},{10,8},{12,14},{14,12},{16,18},{18,... | collective-permute-start | bytes 983048 | tf_op jit(solution)/shard_map/ppermute | solution.py:398
  14.6 0.2 collective-permute-start.4
  14.8 1.9 %collective-permute-start.5 = (bf16[256,640]{1,0:T(8,128)(2,1)}, bf16[256,640]{1,0:T(8,128)(2,1)S(1)}, u32[]{:S(2)}, u32[]{:S(2)}) collective-permute-start(bf16[256,640]{1,0:T(8,128)(2,1)} %get-tuple-element.24), channel_id=1, source_target_pairs={{0,4},{2,6},{4,0},{6,2},{8,12},{10,14},{12,8},{14,10},{16,20},{18,... | collective-permute-start | bytes 983048 | tf_op jit(solution)/shard_map/ppermute | solution.py:398
  16.7 0.2 collective-permute-start.6
  16.8 2.8 %collective-permute-start.7 = (bf16[256,640]{1,0:T(8,128)(2,1)}, bf16[256,640]{1,0:T(8,128)(2,1)}, u32[]{:S(2)}, u32[]{:S(2)}) collective-permute-start(bf16[256,640]{1,0:T(8,128)(2,1)} %get-tuple-element.26), channel_id=1, source_target_pairs={{0,6},{2,4},{4,2},{6,0},{8,14},{10,12},{12,10},{14,8},{16,22},{18,... | collective-permute-start | bytes 983048 | tf_op jit(solution)/shard_map/ppermute | solution.py:398
  19.6 6.9 %collective-permute-done.3.refs_4_ = bf16[256,640]{1,0:T(8,128)(2,1)S(1)} collective-permute-done((bf16[256,640]{1,0:T(8,128)(2,1)}, bf16[256,640]{1,0:T(8,128)(2,1)S(1)}, u32[]{:S(2)}, u32[]{:S(2)}) %collective-permute-start.3) | collective-permute-done | bytes 327712 | tf_op jit(solution)/shard_map/ppermute | solution.py:398
  26.5 0.7 copy-done.5
  27.3 1.6 %collective-permute-start.8 = (bf16[256,640]{1,0:T(8,128)(2,1)}, bf16[256,640]{1,0:T(8,128)(2,1)}, u32[]{:S(2)}, u32[]{:S(2)}) collective-permute-start(bf16[256,640]{1,0:T(8,128)(2,1)} %get-tuple-element.27), channel_id=1, source_target_pairs={{0,6},{2,4},{4,2},{6,0},{8,14},{10,12},{12,10},{14,8},{16,22},{18,... | collective-permute-start | bytes 983048 | tf_op jit(solution)/shard_map/ppermute | solution.py:398
  28.9 0.5 shard_map.74
  29.4 4.3 %collective-permute-done.4.refs_5_ = bf16[256,640]{1,0:T(8,128)(2,1)} collective-permute-done((bf16[256,640]{1,0:T(8,128)(2,1)}, bf16[256,640]{1,0:T(8,128)(2,1)}, u32[]{:S(2)}, u32[]{:S(2)}) %collective-permute-start.4) | collective-permute-done | bytes 327712 | tf_op jit(solution)/shard_map/ppermute | solution.py:398
  33.7 2.9 %collective-permute-start.2 = (bf16[224,128]{1,0:T(8,128)(2,1)S(1)}, bf16[224,128]{1,0:T(8,128)(2,1)S(1)}, u32[]{:S(2)}, u32[]{:S(2)}) collective-permute-start(bf16[224,128]{1,0:T(8,128)(2,1)S(1)} %get-tuple-element.21.refs_0_), channel_id=1, source_target_pairs={{0,24},{2,26},{4,28},{6,30},{8,16},{10,18},{12,20},{14,22},{16,8},... | collective-permute-start | bytes 172040 | tf_op jit(solution)/shard_map/ppermute | solution.py:398
  36.6 3.1 %collective-permute-done.2.refs_3_ = bf16[224,128]{1,0:T(8,128)(2,1)S(1)} collective-permute-done((bf16[224,128]{1,0:T(8,128)(2,1)S(1)}, bf16[224,128]{1,0:T(8,128)(2,1)S(1)}, u32[]{:S(2)}, u32[]{:S(2)}) %collective-permute-start.2) | collective-permute-done | bytes 57376 | tf_op jit(solution)/shard_map/ppermute | solution.py:398
  39.7 0.6 collective-permute-start.1
  40.2 5.1 %collective-permute-done.1.refs_2_ = bf16[224,128]{1,0:T(8,128)(2,1)S(1)} collective-permute-done((bf16[224,128]{1,0:T(8,128)(2,1)S(1)}, bf16[224,128]{1,0:T(8,128)(2,1)S(1)}, u32[]{:S(2)}, u32[]{:S(2)}) %collective-permute-start.1) | collective-permute-done | bytes 57376 | tf_op jit(solution)/shard_map/ppermute | solution.py:398
  45.3 0.0 collective-permute-start
  45.3 4.2 %collective-permute-done.refs_1_ = bf16[224,128]{1,0:T(8,128)(2,1)S(1)} collective-permute-done((bf16[224,128]{1,0:T(8,128)(2,1)S(1)}, bf16[224,128]{1,0:T(8,128)(2,1)S(1)}, u32[]{:S(2)}, u32[]{:S(2)}) %collective-permute-start) | collective-permute-done | bytes 57376 | tf_op jit(solution)/shard_map/ppermute | solution.py:398
  49.5 1.0 copy-done.6
  50.5 2.6 %shard_map.75.near_ref = bf16[4,240,128]{2,1,0:T(8,128)(2,1)S(1)} custom-call(s32[1]{0:T(128)} %bitcast.2.where_ref, bf16[224,128]{1,0:T(8,128)(2,1)S(1)} %get-tuple-element.21.refs_0_, bf16[224,128]{1,0:T(8,128)(2,1)S(1)} %collective-permute-done.refs_1_, bf16[224,128]{1,0:T(8,128)(2,1)S(1)} %collective-permute-done.1.refs_2_, ...), custom_call_target="tpu_custom_call" | custom-call | flops 230686720 | bytes 1310720 | tf_op jit(solution)/shard_map/pallas_call | solution.py:378
  53.1 3.4 %shard_map.76 = (bf16[240,128]{1,0:T(8,128)(2,1)S(1)}, bf16[240,128]{1,0:T(8,128)(2,1)S(1)}, bf16[240,128]{1,0:T(8,128)(2,1)S(1)}, bf16[240,128]{1,0:T(8,128)(2,1)S(1)}) custom-call(s32[1]{0:T(128)} %bitcast.2.where_ref, bf16[4,240,128]{2,1,0:T(8,128)(2,1)S(1)} %shard_map.75.near_ref, bf16[224,128]{1,0:T(8,128)(2,1)S(1)} %get-tuple-element.21.refs_0_, ...), custom_call_target="tpu_custom_call" | custom-call | flops 230686720 | bytes 1310720 | tf_op jit(solution)/shard_map/pallas_call | solution.py:378
  56.5 0.1 collective-permute-start.9
  56.6 2.9 %collective-permute-start.10 = (bf16[240,128]{1,0:T(8,128)(2,1)S(1)}, bf16[240,128]{1,0:T(8,128)(2,1)S(1)}, u32[]{:S(2)}, u32[]{:S(2)}) collective-permute-start(bf16[240,128]{1,0:T(8,128)(2,1)S(1)} %get-tuple-element.30), channel_id=1, source_target_pairs={{0,16},{2,18},{4,20},{6,22},{8,24},{10,26},{12,28},{14,30},{16,0},... | collective-permute-start | bytes 184328 | tf_op jit(solution)/shard_map/ppermute | solution.py:398
  59.5 1.5 %collective-permute-start.11 = (bf16[240,128]{1,0:T(8,128)(2,1)S(1)}, bf16[240,128]{1,0:T(8,128)(2,1)S(1)}, u32[]{:S(2)}, u32[]{:S(2)}) collective-permute-start(bf16[240,128]{1,0:T(8,128)(2,1)S(1)} %get-tuple-element.31), channel_id=1, source_target_pairs={{0,24},{2,26},{4,28},{6,30},{8,16},{10,18},{12,20},{14,22},{16,8},... | collective-permute-start | bytes 184328 | tf_op jit(solution)/shard_map/ppermute | solution.py:398
  61.0 1.0 collective-permute-done.10.refs_2_
  62.0 4.2 %collective-permute-done.11.refs_3_ = bf16[240,128]{1,0:T(8,128)(2,1)S(1)} collective-permute-done((bf16[240,128]{1,0:T(8,128)(2,1)S(1)}, bf16[240,128]{1,0:T(8,128)(2,1)S(1)}, u32[]{:S(2)}, u32[]{:S(2)}) %collective-permute-start.11) | collective-permute-done | bytes 61472 | tf_op jit(solution)/shard_map/ppermute | solution.py:398
  66.2 0.3 shard_map.77.refs_0_
  66.5 1.3 %collective-permute-start.14 = (bf16[224,128]{1,0:T(8,128)(2,1)S(1)}, bf16[224,128]{1,0:T(8,128)(2,1)S(1)}, u32[]{:S(2)}, u32[]{:S(2)}) collective-permute-start(bf16[224,128]{1,0:T(8,128)(2,1)S(1)} %shard_map.77.refs_0_), channel_id=1, source_target_pairs={{0,24},{2,26},{4,28},{6,30},{8,16},{10,18},{12,20},{14,22},{16,8},... | collective-permute-start | bytes 172040 | tf_op jit(solution)/shard_map/ppermute | solution.py:398
  67.9 3.1 %collective-permute-start.12 = (bf16[224,128]{1,0:T(8,128)(2,1)S(1)}, bf16[224,128]{1,0:T(8,128)(2,1)S(1)}, u32[]{:S(2)}, u32[]{:S(2)}) collective-permute-start(bf16[224,128]{1,0:T(8,128)(2,1)S(1)} %shard_map.77.refs_0_), channel_id=1, source_target_pairs={{0,8},{2,10},{4,12},{6,14},{8,0},{10,2},{12,4},{14,6},{16,24},{18,... | collective-permute-start | bytes 172040 | tf_op jit(solution)/shard_map/ppermute | solution.py:398
  71.0 1.6 %collective-permute-done.14.refs_3_ = bf16[224,128]{1,0:T(8,128)(2,1)S(1)} collective-permute-done((bf16[224,128]{1,0:T(8,128)(2,1)S(1)}, bf16[224,128]{1,0:T(8,128)(2,1)S(1)}, u32[]{:S(2)}, u32[]{:S(2)}) %collective-permute-start.14) | collective-permute-done | bytes 57376 | tf_op jit(solution)/shard_map/ppermute | solution.py:398
  72.6 1.2 %collective-permute-done.13.refs_2_ = bf16[224,128]{1,0:T(8,128)(2,1)S(1)} collective-permute-done((bf16[224,128]{1,0:T(8,128)(2,1)S(1)}, bf16[224,128]{1,0:T(8,128)(2,1)S(1)}, u32[]{:S(2)}, u32[]{:S(2)}) %collective-permute-start.13) | collective-permute-done | bytes 57376 | tf_op jit(solution)/shard_map/ppermute | solution.py:398
  73.8 1.2 %collective-permute-start.15 = (bf16[448,128]{1,0:T(8,128)(2,1)S(1)}, bf16[448,128]{1,0:T(8,128)(2,1)S(1)}, u32[]{:S(2)}, u32[]{:S(2)}) collective-permute-start(bf16[448,128]{1,0:T(8,128)(2,1)S(1)} %get-tuple-element.32.refs_0_), channel_id=1, source_target_pairs={{0,2},{2,0},{4,6},{6,4},{8,10},{10,8},{12,14},{14,12},{16,18},{18,... | collective-permute-start | bytes 344072 | tf_op jit(solution)/shard_map/ppermute | solution.py:398
  75.0 0.5 collective-permute-start.17
  75.5 1.9 %collective-permute-start.20 = (bf16[448,128]{1,0:T(8,128)(2,1)S(1)}, bf16[448,128]{1,0:T(8,128)(2,1)S(1)}, u32[]{:S(2)}, u32[]{:S(2)}) collective-permute-start(bf16[448,128]{1,0:T(8,128)(2,1)S(1)} %get-tuple-element.33.refs_1_), channel_id=1, source_target_pairs={{0,2},{2,0},{4,6},{6,4},{8,10},{10,8},{12,14},{14,12},{16,18},{18,... | collective-permute-start | bytes 344072 | tf_op jit(solution)/shard_map/ppermute | solution.py:398
  77.4 0.6 collective-permute-start.19
  77.9 0.7 collective-permute-done.15.refs_0_
  78.7 1.5 %collective-permute-start.16 = (bf16[448,128]{1,0:T(8,128)(2,1)S(1)}, bf16[448,128]{1,0:T(8,128)(2,1)S(1)}, u32[]{:S(2)}, u32[]{:S(2)}) collective-permute-start(bf16[448,128]{1,0:T(8,128)(2,1)S(1)} %collective-permute-done.15.refs_0_), channel_id=1, source_target_pairs={{0,4},{2,6},{4,0},{6,2},{8,12},{10,14},{12,8},{14,10},{16,20},{18,... | collective-permute-start | bytes 344072 | tf_op jit(solution)/shard_map/ppermute | solution.py:398
  80.2 0.6 collective-permute-start.18
  80.7 0.3 shard_map.79.refs_2_
  81.1 0.3 shard_map.80.refs_2_
  81.4 0.8 collective-permute-done.19.refs_0_
  82.2 0.3 shard_map.81.sum_ref
  82.5 1.6 %collective-permute-done.16.low_ref = bf16[448,128]{1,0:T(8,128)(2,1)S(1)} collective-permute-done((bf16[448,128]{1,0:T(8,128)(2,1)S(1)}, bf16[448,128]{1,0:T(8,128)(2,1)S(1)}, u32[]{:S(2)}, u32[]{:S(2)}) %collective-permute-start.16) | collective-permute-done | bytes 114720 | tf_op jit(solution)/shard_map/ppermute | solution.py:398
  84.1 1.4 %collective-permute-done.18.high_ref = bf16[448,128]{1,0:T(8,128)(2,1)S(1)} collective-permute-done((bf16[448,128]{1,0:T(8,128)(2,1)S(1)}, bf16[448,128]{1,0:T(8,128)(2,1)S(1)}, u32[]{:S(2)}, u32[]{:S(2)}) %collective-permute-start.18) | collective-permute-done | bytes 114720 | tf_op jit(solution)/shard_map/ppermute | solution.py:398
  85.5 0.7 shard_map.82
  86.3 13.2 %all_to_all.10.refs_0_ = bf16[16,80,128]{2,1,0:T(8,128)(2,1)S(1)} all-to-all(bf16[16,80,128]{2,1,0:T(8,128)(2,1)S(1)} %shard_map.82), channel_id=1, replica_groups=mesh['seq'=16,'head'=2] {'seq'}, dimensions={0} | all-to-all | bytes 655360 | tf_op jit(solution)/shard_map/all_to_all | solution.py:393
  99.5 1.6 %collective-permute-done.21.refs_1_ = bf16[16,80,128]{2,1,0:T(8,128)(2,1)S(1)} collective-permute-done((bf16[16,80,128]{2,1,0:T(8,128)(2,1)S(1)}, bf16[16,80,128]{2,1,0:T(8,128)(2,1)S(1)}, u32[]{:S(2)}, u32[]{:S(2)}) %collective-permute-start.21) | collective-permute-done | bytes 327712 | tf_op jit(solution)/shard_map/ppermute | solution.py:499
  101.1 1.8 %shard_map.83 = bf16[256,2560]{1,0:T(8,128)(2,1)} custom-call(s32[1]{0:T(128)} %bitcast.half_ref, s32[1,256]{1,0:T(1,128)S(1)} %bitcast.9, bf16[16,80,128]{2,1,0:T(8,128)(2,1)S(1)} %all_to_all.10.refs_0_, bf16[16,80,128]{2,1,0:T(8,128)(2,1)S(1)} %collective-permute-done.21.refs_1_, bf16[256,2560]{1,0:T(8,128)(2,1)S(1)} %copy-done.3, ...), custom_call_target="tpu_custom_call" | custom-call | tf_op jit(solution)/shard_map/pallas_call | solution.py:378
  (26 shorter events, 0.1 us)
Async XLA Ops:
  0.0 49.5 %copy-start.1 = (bf16[256,2560]{1,0:T(8,128)(2,1)S(1)}, bf16[256,2560]{1,0:T(8,128)(2,1)}, u32[]{:S(2)}) copy-start(bf16[256,2560]{1,0:T(8,128)(2,1)} %refs_6_.1) | copy-start | bytes 3932164
  0.0 49.5 %copy-start.2 = (bf16[256,2560]{1,0:T(8,128)(2,1)S(1)}, bf16[256,2560]{1,0:T(8,128)(2,1)}, u32[]{:S(2)}) copy-start(bf16[256,2560]{1,0:T(8,128)(2,1)} %refs_7_.1) | copy-start | bytes 3932164
  4.3 24.5 %all-to-all-start = ((bf16[16,72,128]{2,1,0:T(8,128)(2,1)}), bf16[16,72,128]{2,1,0:T(8,128)(2,1)S(1)}, u32[]{:S(2)}, u32[]{:S(2)}) async-start(bf16[16,72,128]{2,1,0:T(8,128)(2,1)} %get-tuple-element.20), calls=%async_computation | async-start | bytes 589824 | tf_op jit(solution)/shard_map/all_to_all | solution.py:393
  12.7 13.8 %collective-permute-start.3 = (bf16[256,640]{1,0:T(8,128)(2,1)}, bf16[256,640]{1,0:T(8,128)(2,1)S(1)}, u32[]{:S(2)}, u32[]{:S(2)}) collective-permute-start(bf16[256,640]{1,0:T(8,128)(2,1)} %get-tuple-element.22), channel_id=1, source_target_pairs={{0,2},{2,0},{4,6},{6,4},{8,10},{10,8},{12,14},{14,12},{16,18},{18,... | collective-permute-start | bytes 983048 | tf_op jit(solution)/shard_map/ppermute | solution.py:398
  14.6 19.0 %collective-permute-start.4 = (bf16[256,640]{1,0:T(8,128)(2,1)}, bf16[256,640]{1,0:T(8,128)(2,1)}, u32[]{:S(2)}, u32[]{:S(2)}) collective-permute-start(bf16[256,640]{1,0:T(8,128)(2,1)} %get-tuple-element.23), channel_id=1, source_target_pairs={{0,2},{2,0},{4,6},{6,4},{8,10},{10,8},{12,14},{14,12},{16,18},{18,... | collective-permute-start | bytes 983048 | tf_op jit(solution)/shard_map/ppermute | solution.py:398
  14.8 38.3 %collective-permute-start.5 = (bf16[256,640]{1,0:T(8,128)(2,1)}, bf16[256,640]{1,0:T(8,128)(2,1)S(1)}, u32[]{:S(2)}, u32[]{:S(2)}) collective-permute-start(bf16[256,640]{1,0:T(8,128)(2,1)} %get-tuple-element.24), channel_id=1, source_target_pairs={{0,4},{2,6},{4,0},{6,2},{8,12},{10,14},{12,8},{14,10},{16,20},{18,... | collective-permute-start | bytes 983048 | tf_op jit(solution)/shard_map/ppermute | solution.py:398
  16.7 36.4 %collective-permute-start.6 = (bf16[256,640]{1,0:T(8,128)(2,1)}, bf16[256,640]{1,0:T(8,128)(2,1)}, u32[]{:S(2)}, u32[]{:S(2)}) collective-permute-start(bf16[256,640]{1,0:T(8,128)(2,1)} %get-tuple-element.25), channel_id=1, source_target_pairs={{0,4},{2,6},{4,0},{6,2},{8,12},{10,14},{12,8},{14,10},{16,20},{18,... | collective-permute-start | bytes 983048 | tf_op jit(solution)/shard_map/ppermute | solution.py:398
  16.8 36.2 %collective-permute-start.7 = (bf16[256,640]{1,0:T(8,128)(2,1)}, bf16[256,640]{1,0:T(8,128)(2,1)}, u32[]{:S(2)}, u32[]{:S(2)}) collective-permute-start(bf16[256,640]{1,0:T(8,128)(2,1)} %get-tuple-element.26), channel_id=1, source_target_pairs={{0,6},{2,4},{4,2},{6,0},{8,14},{10,12},{12,10},{14,8},{16,22},{18,... | collective-permute-start | bytes 983048 | tf_op jit(solution)/shard_map/ppermute | solution.py:398
  26.5 0.7 copy-start.5
  27.3 25.8 %collective-permute-start.8 = (bf16[256,640]{1,0:T(8,128)(2,1)}, bf16[256,640]{1,0:T(8,128)(2,1)}, u32[]{:S(2)}, u32[]{:S(2)}) collective-permute-start(bf16[256,640]{1,0:T(8,128)(2,1)} %get-tuple-element.27), channel_id=1, source_target_pairs={{0,6},{2,4},{4,2},{6,0},{8,14},{10,12},{12,10},{14,8},{16,22},{18,... | collective-permute-start | bytes 983048 | tf_op jit(solution)/shard_map/ppermute | solution.py:398
  33.7 6.0 %collective-permute-start.2 = (bf16[224,128]{1,0:T(8,128)(2,1)S(1)}, bf16[224,128]{1,0:T(8,128)(2,1)S(1)}, u32[]{:S(2)}, u32[]{:S(2)}) collective-permute-start(bf16[224,128]{1,0:T(8,128)(2,1)S(1)} %get-tuple-element.21.refs_0_), channel_id=1, source_target_pairs={{0,24},{2,26},{4,28},{6,30},{8,16},{10,18},{12,20},{14,22},{16,8},... | collective-permute-start | bytes 172040 | tf_op jit(solution)/shard_map/ppermute | solution.py:398
  39.7 5.6 %collective-permute-start.1 = (bf16[224,128]{1,0:T(8,128)(2,1)S(1)}, bf16[224,128]{1,0:T(8,128)(2,1)S(1)}, u32[]{:S(2)}, u32[]{:S(2)}) collective-permute-start(bf16[224,128]{1,0:T(8,128)(2,1)S(1)} %get-tuple-element.21.refs_0_), channel_id=1, source_target_pairs={{0,16},{2,18},{4,20},{6,22},{8,24},{10,26},{12,28},{14,30},{16,0},... | collective-permute-start | bytes 172040 | tf_op jit(solution)/shard_map/ppermute | solution.py:398
  45.3 4.2 %collective-permute-start = (bf16[224,128]{1,0:T(8,128)(2,1)S(1)}, bf16[224,128]{1,0:T(8,128)(2,1)S(1)}, u32[]{:S(2)}, u32[]{:S(2)}) collective-permute-start(bf16[224,128]{1,0:T(8,128)(2,1)S(1)} %get-tuple-element.21.refs_0_), channel_id=1, source_target_pairs={{0,8},{2,10},{4,12},{6,14},{8,0},{10,2},{12,4},{14,6},{16,24},{18,... | collective-permute-start | bytes 172040 | tf_op jit(solution)/shard_map/ppermute | solution.py:398
  49.5 1.0 copy-start.6
  53.1 27.6 %copy-start = (bf16[2560,320]{0,1:T(8,128)(2,1)S(1)}, bf16[2560,320]{0,1:T(8,128)(2,1)}, u32[]{:S(2)}) copy-start(bf16[2560,320]{0,1:T(8,128)(2,1)} %param.13) | copy-start | bytes 4915204
  56.5 4.5 %collective-permute-start.9 = (bf16[240,128]{1,0:T(8,128)(2,1)S(1)}, bf16[240,128]{1,0:T(8,128)(2,1)S(1)}, u32[]{:S(2)}, u32[]{:S(2)}) collective-permute-start(bf16[240,128]{1,0:T(8,128)(2,1)S(1)} %get-tuple-element.29), channel_id=1, source_target_pairs={{0,8},{2,10},{4,12},{6,14},{8,0},{10,2},{12,4},{14,6},{16,24},{18,... | collective-permute-start | bytes 184328 | tf_op jit(solution)/shard_map/ppermute | solution.py:398
  56.6 5.4 %collective-permute-start.10 = (bf16[240,128]{1,0:T(8,128)(2,1)S(1)}, bf16[240,128]{1,0:T(8,128)(2,1)S(1)}, u32[]{:S(2)}, u32[]{:S(2)}) collective-permute-start(bf16[240,128]{1,0:T(8,128)(2,1)S(1)} %get-tuple-element.30), channel_id=1, source_target_pairs={{0,16},{2,18},{4,20},{6,22},{8,24},{10,26},{12,28},{14,30},{16,0},... | collective-permute-start | bytes 184328 | tf_op jit(solution)/shard_map/ppermute | solution.py:398
  59.5 6.7 %collective-permute-start.11 = (bf16[240,128]{1,0:T(8,128)(2,1)S(1)}, bf16[240,128]{1,0:T(8,128)(2,1)S(1)}, u32[]{:S(2)}, u32[]{:S(2)}) collective-permute-start(bf16[240,128]{1,0:T(8,128)(2,1)S(1)} %get-tuple-element.31), channel_id=1, source_target_pairs={{0,24},{2,26},{4,28},{6,30},{8,16},{10,18},{12,20},{14,22},{16,8},... | collective-permute-start | bytes 184328 | tf_op jit(solution)/shard_map/ppermute | solution.py:398
  66.5 6.1 %collective-permute-start.14 = (bf16[224,128]{1,0:T(8,128)(2,1)S(1)}, bf16[224,128]{1,0:T(8,128)(2,1)S(1)}, u32[]{:S(2)}, u32[]{:S(2)}) collective-permute-start(bf16[224,128]{1,0:T(8,128)(2,1)S(1)} %shard_map.77.refs_0_), channel_id=1, source_target_pairs={{0,24},{2,26},{4,28},{6,30},{8,16},{10,18},{12,20},{14,22},{16,8},... | collective-permute-start | bytes 172040 | tf_op jit(solution)/shard_map/ppermute | solution.py:398
  67.9 5.9 %collective-permute-start.13 = (bf16[224,128]{1,0:T(8,128)(2,1)S(1)}, bf16[224,128]{1,0:T(8,128)(2,1)S(1)}, u32[]{:S(2)}, u32[]{:S(2)}) collective-permute-start(bf16[224,128]{1,0:T(8,128)(2,1)S(1)} %shard_map.77.refs_0_), channel_id=1, source_target_pairs={{0,16},{2,18},{4,20},{6,22},{8,24},{10,26},{12,28},{14,30},{16,0},... | collective-permute-start | bytes 172040 | tf_op jit(solution)/shard_map/ppermute | solution.py:398
  67.9 5.9 %collective-permute-start.12 = (bf16[224,128]{1,0:T(8,128)(2,1)S(1)}, bf16[224,128]{1,0:T(8,128)(2,1)S(1)}, u32[]{:S(2)}, u32[]{:S(2)}) collective-permute-start(bf16[224,128]{1,0:T(8,128)(2,1)S(1)} %shard_map.77.refs_0_), channel_id=1, source_target_pairs={{0,8},{2,10},{4,12},{6,14},{8,0},{10,2},{12,4},{14,6},{16,24},{18,... | collective-permute-start | bytes 172040 | tf_op jit(solution)/shard_map/ppermute | solution.py:398
  73.8 4.9 %collective-permute-start.15 = (bf16[448,128]{1,0:T(8,128)(2,1)S(1)}, bf16[448,128]{1,0:T(8,128)(2,1)S(1)}, u32[]{:S(2)}, u32[]{:S(2)}) collective-permute-start(bf16[448,128]{1,0:T(8,128)(2,1)S(1)} %get-tuple-element.32.refs_0_), channel_id=1, source_target_pairs={{0,2},{2,0},{4,6},{6,4},{8,10},{10,8},{12,14},{14,12},{16,18},{18,... | collective-permute-start | bytes 344072 | tf_op jit(solution)/shard_map/ppermute | solution.py:398
  75.0 5.2 %collective-permute-start.17 = (bf16[448,128]{1,0:T(8,128)(2,1)S(1)}, bf16[448,128]{1,0:T(8,128)(2,1)S(1)}, u32[]{:S(2)}, u32[]{:S(2)}) collective-permute-start(bf16[448,128]{1,0:T(8,128)(2,1)S(1)} %get-tuple-element.33.refs_1_), channel_id=1, source_target_pairs={{0,4},{2,6},{4,0},{6,2},{8,12},{10,14},{12,8},{14,10},{16,20},{18,... | collective-permute-start | bytes 344072 | tf_op jit(solution)/shard_map/ppermute | solution.py:398
  75.5 5.6 %collective-permute-start.20 = (bf16[448,128]{1,0:T(8,128)(2,1)S(1)}, bf16[448,128]{1,0:T(8,128)(2,1)S(1)}, u32[]{:S(2)}, u32[]{:S(2)}) collective-permute-start(bf16[448,128]{1,0:T(8,128)(2,1)S(1)} %get-tuple-element.33.refs_1_), channel_id=1, source_target_pairs={{0,2},{2,0},{4,6},{6,4},{8,10},{10,8},{12,14},{14,12},{16,18},{18,... | collective-permute-start | bytes 344072 | tf_op jit(solution)/shard_map/ppermute | solution.py:398
  77.4 4.8 %collective-permute-start.19 = (bf16[448,128]{1,0:T(8,128)(2,1)S(1)}, bf16[448,128]{1,0:T(8,128)(2,1)S(1)}, u32[]{:S(2)}, u32[]{:S(2)}) collective-permute-start(bf16[448,128]{1,0:T(8,128)(2,1)S(1)} %get-tuple-element.32.refs_0_), channel_id=1, source_target_pairs={{0,4},{2,6},{4,0},{6,2},{8,12},{10,14},{12,8},{14,10},{16,20},{18,... | collective-permute-start | bytes 344072 | tf_op jit(solution)/shard_map/ppermute | solution.py:398
  78.7 5.5 %collective-permute-start.16 = (bf16[448,128]{1,0:T(8,128)(2,1)S(1)}, bf16[448,128]{1,0:T(8,128)(2,1)S(1)}, u32[]{:S(2)}, u32[]{:S(2)}) collective-permute-start(bf16[448,128]{1,0:T(8,128)(2,1)S(1)} %collective-permute-done.15.refs_0_), channel_id=1, source_target_pairs={{0,4},{2,6},{4,0},{6,2},{8,12},{10,14},{12,8},{14,10},{16,20},{18,... | collective-permute-start | bytes 344072 | tf_op jit(solution)/shard_map/ppermute | solution.py:398
  80.2 5.4 %collective-permute-start.18 = (bf16[448,128]{1,0:T(8,128)(2,1)S(1)}, bf16[448,128]{1,0:T(8,128)(2,1)S(1)}, u32[]{:S(2)}, u32[]{:S(2)}) collective-permute-start(bf16[448,128]{1,0:T(8,128)(2,1)S(1)} %collective-permute-done.17.refs_1_), channel_id=1, source_target_pairs={{0,2},{2,0},{4,6},{6,4},{8,10},{10,8},{12,14},{14,12},{16,18},{18,... | collective-permute-start | bytes 344072 | tf_op jit(solution)/shard_map/ppermute | solution.py:398
  85.5 15.6 %copy-start.3 = (bf16[256,2560]{1,0:T(8,128)(2,1)S(1)}, bf16[256,2560]{1,0:T(8,128)(2,1)}, u32[]{:S(2)}) copy-start(bf16[256,2560]{1,0:T(8,128)(2,1)} %refs_2_.1) | copy-start | bytes 3932164
  85.5 15.6 %copy-start.4 = (bf16[256,2560]{1,0:T(8,128)(2,1)S(1)}, bf16[256,2560]{1,0:T(8,128)(2,1)}, u32[]{:S(2)}) copy-start(bf16[256,2560]{1,0:T(8,128)(2,1)} %refs_3_.1) | copy-start | bytes 3932164
  85.5 15.6 %copy-start.7 = (s32[256]{0:T(256)S(1)}, s32[256]{0:T(256)}, u32[]{:S(2)}) copy-start(s32[256]{0:T(256)} %param.12) | copy-start | bytes 3076
  99.5 1.6 %collective-permute-start.21 = (bf16[16,80,128]{2,1,0:T(8,128)(2,1)S(1)}, bf16[16,80,128]{2,1,0:T(8,128)(2,1)S(1)}, u32[]{:S(2)}, u32[]{:S(2)}) collective-permute-start(bf16[16,80,128]{2,1,0:T(8,128)(2,1)S(1)} %all_to_all.10.refs_0_), channel_id=1, source_target_pairs={{0,1},{1,0},{2,3},{3,2},{4,5},{5,4},{6,7},{7,6},{8,9},{9,8},{10,11... | collective-permute-start | bytes 983048 | tf_op jit(solution)/shard_map/ppermute | solution.py:499

commit v6 on v5

--- a/solution.py
+++ b/solution.py
@@ -398,8 +398,15 @@
     return lax.ppermute(value, "seq", pairs)
 
 
+def line_shift(parts):
+    out = [parts[0]]
+    for step in range(1, len(parts)):
+        out.append(shift(parts[step], step * QUAD))
+    return out
+
+
 def line_gather(plan, chunk):
-    return [shift(chunk, step * QUAD) if step else chunk for step in range(plan.line)]
+    return line_shift([chunk] * plan.line)
 
 
 def quad_gather(low, high):
@@ -467,7 +474,7 @@
         tuple(shape(plan.rows + TILE, HD) for _ in range(plan.line)),
         part, *line, *far, scratch=[pltpu.VMEM(scored_shape, BF16)],
     )
-    arrived = [shift(part, step * QUAD) if step else part for step, part in enumerate(sums)]
+    arrived = line_shift(sums)
     chunk = call(partial(line_kernel, plan), shape(plan.rows, HD), *arrived)
     low, high = call(
         partial(stack_kernel, plan), (shape(plan.half, HD), shape(plan.half, HD)),

time: 103 us -> 103 us (level)
  no operation moved by 1% of the time
where the time goes in v6:
time: 103 us
  waiting for transfers between devices  37.8 us (37%)
  starting transfers between devices  35.3 us (34%)
  Pallas kernels  14.7 us (14%)
  blocking collectives  13.2 us (13%)
  local copies, waits for them, and re-layouts  1.72 us (2%)
    ppermute x21, waiting for transfers between devices, shift(): return lax.ppermute(value, 'seq', pairs)  36.2 us
    ppermute x21, starting transfers between devices, shift(): return lax.ppermute(value, 'seq', pairs)  27 us
    pallas_call x11, Pallas kernels, call(): pl.pallas_call(kernel, out_shape=out_shape, in_specs=[spec(i, arg) for i,...  14.7 us
    all_to_all x1, blocking collectives, exchange(): return lax.all_to_all(value, 'seq', split_axis=0, concat_axis=0, tiled=True)  13.2 us
    all_to_all x1, starting transfers between devices, exchange(): return lax.all_to_all(value, 'seq', split_axis=0, concat_axis=0, tiled=True)  8.36 us
  transfers between devices with their start and end apart: 23, of which 14 were waited for; matrix products, arithmetic and copies ran while one was open for 0% of the time, Pallas kernels for 4%

profile of v6, /device:TPU:0, one launch (start us, length us, event | category | flops | bytes accessed | tf_op | source)
XLA Modules:
  0.0 102.9 jit_solution(6686016852853207759)
XLA Ops:
  0.0 4.3 %shard_map.73 = (bf16[16,72,128]{2,1,0:T(8,128)(2,1)}, bf16[256,640]{1,0:T(8,128)(2,1)}, bf16[256,640]{1,0:T(8,128)(2,1)}, bf16[256,640]{1,0:T(8,128)(2,1)}, bf1...) custom-call(s32[1,256]{1,0:T(1,128)} %bitcast.8, bf16[256,2560]{1,0:T(8,128)(2,1)} %q_hbm.1, ...), custom_call_target="tpu_custom_call" | custom-call | tf_op jit(solution)/shard_map/pallas_call | solution.py:378
  4.3 8.4 %all-to-all-start = ((bf16[16,72,128]{2,1,0:T(8,128)(2,1)}), bf16[16,72,128]{2,1,0:T(8,128)(2,1)S(1)}, u32[]{:S(2)}, u32[]{:S(2)}) async-start(bf16[16,72,128]{2,1,0:T(8,128)(2,1)} %get-tuple-element.20), calls=%async_computation | async-start | bytes 589824 | tf_op jit(solution)/shard_map/all_to_all | solution.py:393
  12.7 1.9 %collective-permute-start.3 = (bf16[256,640]{1,0:T(8,128)(2,1)}, bf16[256,640]{1,0:T(8,128)(2,1)S(1)}, u32[]{:S(2)}, u32[]{:S(2)}) collective-permute-start(bf16[256,640]{1,0:T(8,128)(2,1)} %get-tuple-element.22), channel_id=1, source_target_pairs={{0,2},{2,0},{4,6},{6,4},{8,10},{10,8},{12,14},{14,12},{16,18},{18,... | collective-permute-start | bytes 983048 | tf_op jit(solution)/shard_map/ppermute | solution.py:398
  14.6 0.2 collective-permute-start.4
  14.8 1.9 %collective-permute-start.5 = (bf16[256,640]{1,0:T(8,128)(2,1)}, bf16[256,640]{1,0:T(8,128)(2,1)S(1)}, u32[]{:S(2)}, u32[]{:S(2)}) collective-permute-start(bf16[256,640]{1,0:T(8,128)(2,1)} %get-tuple-element.24), channel_id=1, source_target_pairs={{0,4},{2,6},{4,0},{6,2},{8,12},{10,14},{12,8},{14,10},{16,20},{18,... | collective-permute-start | bytes 983048 | tf_op jit(solution)/shard_map/ppermute | solution.py:398
  16.7 0.2 collective-permute-start.6
  16.8 2.8 %collective-permute-start.7 = (bf16[256,640]{1,0:T(8,128)(2,1)}, bf16[256,640]{1,0:T(8,128)(2,1)}, u32[]{:S(2)}, u32[]{:S(2)}) collective-permute-start(bf16[256,640]{1,0:T(8,128)(2,1)} %get-tuple-element.26), channel_id=1, source_target_pairs={{0,6},{2,4},{4,2},{6,0},{8,14},{10,12},{12,10},{14,8},{16,22},{18,... | collective-permute-start | bytes 983048 | tf_op jit(solution)/shard_map/ppermute | solution.py:398
  19.6 6.9 %collective-permute-done.3.refs_4_ = bf16[256,640]{1,0:T(8,128)(2,1)S(1)} collective-permute-done((bf16[256,640]{1,0:T(8,128)(2,1)}, bf16[256,640]{1,0:T(8,128)(2,1)S(1)}, u32[]{:S(2)}, u32[]{:S(2)}) %collective-permute-start.3) | collective-permute-done | bytes 327712 | tf_op jit(solution)/shard_map/ppermute | solution.py:398
  26.5 0.7 copy-done.5
  27.3 1.6 %collective-permute-start.8 = (bf16[256,640]{1,0:T(8,128)(2,1)}, bf16[256,640]{1,0:T(8,128)(2,1)}, u32[]{:S(2)}, u32[]{:S(2)}) collective-permute-start(bf16[256,640]{1,0:T(8,128)(2,1)} %get-tuple-element.27), channel_id=1, source_target_pairs={{0,6},{2,4},{4,2},{6,0},{8,14},{10,12},{12,10},{14,8},{16,22},{18,... | collective-permute-start | bytes 983048 | tf_op jit(solution)/shard_map/ppermute | solution.py:398
  28.9 0.5 shard_map.74
  29.4 4.3 %collective-permute-done.4.refs_5_ = bf16[256,640]{1,0:T(8,128)(2,1)} collective-permute-done((bf16[256,640]{1,0:T(8,128)(2,1)}, bf16[256,640]{1,0:T(8,128)(2,1)}, u32[]{:S(2)}, u32[]{:S(2)}) %collective-permute-start.4) | collective-permute-done | bytes 327712 | tf_op jit(solution)/shard_map/ppermute | solution.py:398
  33.7 2.9 %collective-permute-start.2 = (bf16[224,128]{1,0:T(8,128)(2,1)S(1)}, bf16[224,128]{1,0:T(8,128)(2,1)S(1)}, u32[]{:S(2)}, u32[]{:S(2)}) collective-permute-start(bf16[224,128]{1,0:T(8,128)(2,1)S(1)} %get-tuple-element.21.refs_0_), channel_id=1, source_target_pairs={{0,24},{2,26},{4,28},{6,30},{8,16},{10,18},{12,20},{14,22},{16,8},... | collective-permute-start | bytes 172040 | tf_op jit(solution)/shard_map/ppermute | solution.py:398
  36.6 3.1 %collective-permute-done.2.refs_3_ = bf16[224,128]{1,0:T(8,128)(2,1)S(1)} collective-permute-done((bf16[224,128]{1,0:T(8,128)(2,1)S(1)}, bf16[224,128]{1,0:T(8,128)(2,1)S(1)}, u32[]{:S(2)}, u32[]{:S(2)}) %collective-permute-start.2) | collective-permute-done | bytes 57376 | tf_op jit(solution)/shard_map/ppermute | solution.py:398
  39.7 0.6 collective-permute-start.1
  40.2 5.1 %collective-permute-done.1.refs_2_ = bf16[224,128]{1,0:T(8,128)(2,1)S(1)} collective-permute-done((bf16[224,128]{1,0:T(8,128)(2,1)S(1)}, bf16[224,128]{1,0:T(8,128)(2,1)S(1)}, u32[]{:S(2)}, u32[]{:S(2)}) %collective-permute-start.1) | collective-permute-done | bytes 57376 | tf_op jit(solution)/shard_map/ppermute | solution.py:398
  45.3 0.0 collective-permute-start
  45.3 4.2 %collective-permute-done.refs_1_ = bf16[224,128]{1,0:T(8,128)(2,1)S(1)} collective-permute-done((bf16[224,128]{1,0:T(8,128)(2,1)S(1)}, bf16[224,128]{1,0:T(8,128)(2,1)S(1)}, u32[]{:S(2)}, u32[]{:S(2)}) %collective-permute-start) | collective-permute-done | bytes 57376 | tf_op jit(solution)/shard_map/ppermute | solution.py:398
  49.5 1.0 copy-done.6
  50.5 2.6 %shard_map.75.near_ref = bf16[4,240,128]{2,1,0:T(8,128)(2,1)S(1)} custom-call(s32[1]{0:T(128)} %bitcast.2.where_ref, bf16[224,128]{1,0:T(8,128)(2,1)S(1)} %get-tuple-element.21.refs_0_, bf16[224,128]{1,0:T(8,128)(2,1)S(1)} %collective-permute-done.refs_1_, bf16[224,128]{1,0:T(8,128)(2,1)S(1)} %collective-permute-done.1.refs_2_, ...), custom_call_target="tpu_custom_call" | custom-call | flops 230686720 | bytes 1310720 | tf_op jit(solution)/shard_map/pallas_call | solution.py:378
  53.1 3.4 %shard_map.76 = (bf16[240,128]{1,0:T(8,128)(2,1)S(1)}, bf16[240,128]{1,0:T(8,128)(2,1)S(1)}, bf16[240,128]{1,0:T(8,128)(2,1)S(1)}, bf16[240,128]{1,0:T(8,128)(2,1)S(1)}) custom-call(s32[1]{0:T(128)} %bitcast.2.where_ref, bf16[4,240,128]{2,1,0:T(8,128)(2,1)S(1)} %shard_map.75.near_ref, bf16[224,128]{1,0:T(8,128)(2,1)S(1)} %get-tuple-element.21.refs_0_, ...), custom_call_target="tpu_custom_call" | custom-call | flops 230686720 | bytes 1310720 | tf_op jit(solution)/shard_map/pallas_call | solution.py:378
  56.5 0.1 collective-permute-start.9
  56.6 2.9 %collective-permute-start.10 = (bf16[240,128]{1,0:T(8,128)(2,1)S(1)}, bf16[240,128]{1,0:T(8,128)(2,1)S(1)}, u32[]{:S(2)}, u32[]{:S(2)}) collective-permute-start(bf16[240,128]{1,0:T(8,128)(2,1)S(1)} %get-tuple-element.30), channel_id=1, source_target_pairs={{0,16},{2,18},{4,20},{6,22},{8,24},{10,26},{12,28},{14,30},{16,0},... | collective-permute-start | bytes 184328 | tf_op jit(solution)/shard_map/ppermute | solution.py:398
  59.5 1.5 %collective-permute-start.11 = (bf16[240,128]{1,0:T(8,128)(2,1)S(1)}, bf16[240,128]{1,0:T(8,128)(2,1)S(1)}, u32[]{:S(2)}, u32[]{:S(2)}) collective-permute-start(bf16[240,128]{1,0:T(8,128)(2,1)S(1)} %get-tuple-element.31), channel_id=1, source_target_pairs={{0,24},{2,26},{4,28},{6,30},{8,16},{10,18},{12,20},{14,22},{16,8},... | collective-permute-start | bytes 184328 | tf_op jit(solution)/shard_map/ppermute | solution.py:398
  61.0 1.0 collective-permute-done.10.refs_2_
  62.0 4.2 %collective-permute-done.11.refs_3_ = bf16[240,128]{1,0:T(8,128)(2,1)S(1)} collective-permute-done((bf16[240,128]{1,0:T(8,128)(2,1)S(1)}, bf16[240,128]{1,0:T(8,128)(2,1)S(1)}, u32[]{:S(2)}, u32[]{:S(2)}) %collective-permute-start.11) | collective-permute-done | bytes 61472 | tf_op jit(solution)/shard_map/ppermute | solution.py:398
  66.2 0.3 shard_map.77.refs_0_
  66.5 1.3 %collective-permute-start.14 = (bf16[224,128]{1,0:T(8,128)(2,1)S(1)}, bf16[224,128]{1,0:T(8,128)(2,1)S(1)}, u32[]{:S(2)}, u32[]{:S(2)}) collective-permute-start(bf16[224,128]{1,0:T(8,128)(2,1)S(1)} %shard_map.77.refs_0_), channel_id=1, source_target_pairs={{0,24},{2,26},{4,28},{6,30},{8,16},{10,18},{12,20},{14,22},{16,8},... | collective-permute-start | bytes 172040 | tf_op jit(solution)/shard_map/ppermute | solution.py:398
  67.9 3.1 %collective-permute-start.12 = (bf16[224,128]{1,0:T(8,128)(2,1)S(1)}, bf16[224,128]{1,0:T(8,128)(2,1)S(1)}, u32[]{:S(2)}, u32[]{:S(2)}) collective-permute-start(bf16[224,128]{1,0:T(8,128)(2,1)S(1)} %shard_map.77.refs_0_), channel_id=1, source_target_pairs={{0,8},{2,10},{4,12},{6,14},{8,0},{10,2},{12,4},{14,6},{16,24},{18,... | collective-permute-start | bytes 172040 | tf_op jit(solution)/shard_map/ppermute | solution.py:398
  71.0 1.6 %collective-permute-done.14.refs_3_ = bf16[224,128]{1,0:T(8,128)(2,1)S(1)} collective-permute-done((bf16[224,128]{1,0:T(8,128)(2,1)S(1)}, bf16[224,128]{1,0:T(8,128)(2,1)S(1)}, u32[]{:S(2)}, u32[]{:S(2)}) %collective-permute-start.14) | collective-permute-done | bytes 57376 | tf_op jit(solution)/shard_map/ppermute | solution.py:398
  72.6 1.2 %collective-permute-done.13.refs_2_ = bf16[224,128]{1,0:T(8,128)(2,1)S(1)} collective-permute-done((bf16[224,128]{1,0:T(8,128)(2,1)S(1)}, bf16[224,128]{1,0:T(8,128)(2,1)S(1)}, u32[]{:S(2)}, u32[]{:S(2)}) %collective-permute-start.13) | collective-permute-done | bytes 57376 | tf_op jit(solution)/shard_map/ppermute | solution.py:398
  73.8 1.2 %collective-permute-start.15 = (bf16[448,128]{1,0:T(8,128)(2,1)S(1)}, bf16[448,128]{1,0:T(8,128)(2,1)S(1)}, u32[]{:S(2)}, u32[]{:S(2)}) collective-permute-start(bf16[448,128]{1,0:T(8,128)(2,1)S(1)} %get-tuple-element.32.refs_0_), channel_id=1, source_target_pairs={{0,2},{2,0},{4,6},{6,4},{8,10},{10,8},{12,14},{14,12},{16,18},{18,... | collective-permute-start | bytes 344072 | tf_op jit(solution)/shard_map/ppermute | solution.py:398
  75.0 0.5 collective-permute-start.17
  75.5 1.9 %collective-permute-start.20 = (bf16[448,128]{1,0:T(8,128)(2,1)S(1)}, bf16[448,128]{1,0:T(8,128)(2,1)S(1)}, u32[]{:S(2)}, u32[]{:S(2)}) collective-permute-start(bf16[448,128]{1,0:T(8,128)(2,1)S(1)} %get-tuple-element.33.refs_1_), channel_id=1, source_target_pairs={{0,2},{2,0},{4,6},{6,4},{8,10},{10,8},{12,14},{14,12},{16,18},{18,... | collective-permute-start | bytes 344072 | tf_op jit(solution)/shard_map/ppermute | solution.py:398
  77.4 0.6 collective-permute-start.19
  77.9 0.7 collective-permute-done.15.refs_0_
  78.7 1.5 %collective-permute-start.16 = (bf16[448,128]{1,0:T(8,128)(2,1)S(1)}, bf16[448,128]{1,0:T(8,128)(2,1)S(1)}, u32[]{:S(2)}, u32[]{:S(2)}) collective-permute-start(bf16[448,128]{1,0:T(8,128)(2,1)S(1)} %collective-permute-done.15.refs_0_), channel_id=1, source_target_pairs={{0,4},{2,6},{4,0},{6,2},{8,12},{10,14},{12,8},{14,10},{16,20},{18,... | collective-permute-start | bytes 344072 | tf_op jit(solution)/shard_map/ppermute | solution.py:398
  80.2 0.6 collective-permute-start.18
  80.7 0.3 shard_map.79.refs_2_
  81.1 0.3 shard_map.80.refs_2_
  81.4 0.8 collective-permute-done.19.refs_0_
  82.2 0.3 shard_map.81.sum_ref
  82.5 1.6 %collective-permute-done.16.low_ref = bf16[448,128]{1,0:T(8,128)(2,1)S(1)} collective-permute-done((bf16[448,128]{1,0:T(8,128)(2,1)S(1)}, bf16[448,128]{1,0:T(8,128)(2,1)S(1)}, u32[]{:S(2)}, u32[]{:S(2)}) %collective-permute-start.16) | collective-permute-done | bytes 114720 | tf_op jit(solution)/shard_map/ppermute | solution.py:398
  84.1 1.4 %collective-permute-done.18.high_ref = bf16[448,128]{1,0:T(8,128)(2,1)S(1)} collective-permute-done((bf16[448,128]{1,0:T(8,128)(2,1)S(1)}, bf16[448,128]{1,0:T(8,128)(2,1)S(1)}, u32[]{:S(2)}, u32[]{:S(2)}) %collective-permute-start.18) | collective-permute-done | bytes 114720 | tf_op jit(solution)/shard_map/ppermute | solution.py:398
  85.5 0.7 shard_map.82
  86.3 13.2 %all_to_all.10.refs_0_ = bf16[16,80,128]{2,1,0:T(8,128)(2,1)S(1)} all-to-all(bf16[16,80,128]{2,1,0:T(8,128)(2,1)S(1)} %shard_map.82), channel_id=1, replica_groups=mesh['seq'=16,'head'=2] {'seq'}, dimensions={0} | all-to-all | bytes 655360 | tf_op jit(solution)/shard_map/all_to_all | solution.py:393
  99.5 1.6 %collective-permute-done.21.refs_1_ = bf16[16,80,128]{2,1,0:T(8,128)(2,1)S(1)} collective-permute-done((bf16[16,80,128]{2,1,0:T(8,128)(2,1)S(1)}, bf16[16,80,128]{2,1,0:T(8,128)(2,1)S(1)}, u32[]{:S(2)}, u32[]{:S(2)}) %collective-permute-start.21) | collective-permute-done | bytes 327712 | tf_op jit(solution)/shard_map/ppermute | solution.py:506
  101.1 1.8 %shard_map.83 = bf16[256,2560]{1,0:T(8,128)(2,1)} custom-call(s32[1]{0:T(128)} %bitcast.half_ref, s32[1,256]{1,0:T(1,128)S(1)} %bitcast.9, bf16[16,80,128]{2,1,0:T(8,128)(2,1)S(1)} %all_to_all.10.refs_0_, bf16[16,80,128]{2,1,0:T(8,128)(2,1)S(1)} %collective-permute-done.21.refs_1_, bf16[256,2560]{1,0:T(8,128)(2,1)S(1)} %copy-done.3, ...), custom_call_target="tpu_custom_call" | custom-call | tf_op jit(solution)/shard_map/pallas_call | solution.py:378
  (26 shorter events, 0.1 us)
Async XLA Ops:
  0.0 49.5 %copy-start.1 = (bf16[256,2560]{1,0:T(8,128)(2,1)S(1)}, bf16[256,2560]{1,0:T(8,128)(2,1)}, u32[]{:S(2)}) copy-start(bf16[256,2560]{1,0:T(8,128)(2,1)} %refs_6_.1) | copy-start | bytes 3932164
  0.0 49.5 %copy-start.2 = (bf16[256,2560]{1,0:T(8,128)(2,1)S(1)}, bf16[256,2560]{1,0:T(8,128)(2,1)}, u32[]{:S(2)}) copy-start(bf16[256,2560]{1,0:T(8,128)(2,1)} %refs_7_.1) | copy-start | bytes 3932164
  4.3 24.5 %all-to-all-start = ((bf16[16,72,128]{2,1,0:T(8,128)(2,1)}), bf16[16,72,128]{2,1,0:T(8,128)(2,1)S(1)}, u32[]{:S(2)}, u32[]{:S(2)}) async-start(bf16[16,72,128]{2,1,0:T(8,128)(2,1)} %get-tuple-element.20), calls=%async_computation | async-start | bytes 589824 | tf_op jit(solution)/shard_map/all_to_all | solution.py:393
  12.7 13.8 %collective-permute-start.3 = (bf16[256,640]{1,0:T(8,128)(2,1)}, bf16[256,640]{1,0:T(8,128)(2,1)S(1)}, u32[]{:S(2)}, u32[]{:S(2)}) collective-permute-start(bf16[256,640]{1,0:T(8,128)(2,1)} %get-tuple-element.22), channel_id=1, source_target_pairs={{0,2},{2,0},{4,6},{6,4},{8,10},{10,8},{12,14},{14,12},{16,18},{18,... | collective-permute-start | bytes 983048 | tf_op jit(solution)/shard_map/ppermute | solution.py:398
  14.6 19.0 %collective-permute-start.4 = (bf16[256,640]{1,0:T(8,128)(2,1)}, bf16[256,640]{1,0:T(8,128)(2,1)}, u32[]{:S(2)}, u32[]{:S(2)}) collective-permute-start(bf16[256,640]{1,0:T(8,128)(2,1)} %get-tuple-element.23), channel_id=1, source_target_pairs={{0,2},{2,0},{4,6},{6,4},{8,10},{10,8},{12,14},{14,12},{16,18},{18,... | collective-permute-start | bytes 983048 | tf_op jit(solution)/shard_map/ppermute | solution.py:398
  14.8 38.3 %collective-permute-start.5 = (bf16[256,640]{1,0:T(8,128)(2,1)}, bf16[256,640]{1,0:T(8,128)(2,1)S(1)}, u32[]{:S(2)}, u32[]{:S(2)}) collective-permute-start(bf16[256,640]{1,0:T(8,128)(2,1)} %get-tuple-element.24), channel_id=1, source_target_pairs={{0,4},{2,6},{4,0},{6,2},{8,12},{10,14},{12,8},{14,10},{16,20},{18,... | collective-permute-start | bytes 983048 | tf_op jit(solution)/shard_map/ppermute | solution.py:398
  16.7 36.4 %collective-permute-start.6 = (bf16[256,640]{1,0:T(8,128)(2,1)}, bf16[256,640]{1,0:T(8,128)(2,1)}, u32[]{:S(2)}, u32[]{:S(2)}) collective-permute-start(bf16[256,640]{1,0:T(8,128)(2,1)} %get-tuple-element.25), channel_id=1, source_target_pairs={{0,4},{2,6},{4,0},{6,2},{8,12},{10,14},{12,8},{14,10},{16,20},{18,... | collective-permute-start | bytes 983048 | tf_op jit(solution)/shard_map/ppermute | solution.py:398
  16.8 36.2 %collective-permute-start.7 = (bf16[256,640]{1,0:T(8,128)(2,1)}, bf16[256,640]{1,0:T(8,128)(2,1)}, u32[]{:S(2)}, u32[]{:S(2)}) collective-permute-start(bf16[256,640]{1,0:T(8,128)(2,1)} %get-tuple-element.26), channel_id=1, source_target_pairs={{0,6},{2,4},{4,2},{6,0},{8,14},{10,12},{12,10},{14,8},{16,22},{18,... | collective-permute-start | bytes 983048 | tf_op jit(solution)/shard_map/ppermute | solution.py:398
  26.5 0.7 copy-start.5
  27.3 25.8 %collective-permute-start.8 = (bf16[256,640]{1,0:T(8,128)(2,1)}, bf16[256,640]{1,0:T(8,128)(2,1)}, u32[]{:S(2)}, u32[]{:S(2)}) collective-permute-start(bf16[256,640]{1,0:T(8,128)(2,1)} %get-tuple-element.27), channel_id=1, source_target_pairs={{0,6},{2,4},{4,2},{6,0},{8,14},{10,12},{12,10},{14,8},{16,22},{18,... | collective-permute-start | bytes 983048 | tf_op jit(solution)/shard_map/ppermute | solution.py:398
  33.7 6.0 %collective-permute-start.2 = (bf16[224,128]{1,0:T(8,128)(2,1)S(1)}, bf16[224,128]{1,0:T(8,128)(2,1)S(1)}, u32[]{:S(2)}, u32[]{:S(2)}) collective-permute-start(bf16[224,128]{1,0:T(8,128)(2,1)S(1)} %get-tuple-element.21.refs_0_), channel_id=1, source_target_pairs={{0,24},{2,26},{4,28},{6,30},{8,16},{10,18},{12,20},{14,22},{16,8},... | collective-permute-start | bytes 172040 | tf_op jit(solution)/shard_map/ppermute | solution.py:398
  39.7 5.6 %collective-permute-start.1 = (bf16[224,128]{1,0:T(8,128)(2,1)S(1)}, bf16[224,128]{1,0:T(8,128)(2,1)S(1)}, u32[]{:S(2)}, u32[]{:S(2)}) collective-permute-start(bf16[224,128]{1,0:T(8,128)(2,1)S(1)} %get-tuple-element.21.refs_0_), channel_id=1, source_target_pairs={{0,16},{2,18},{4,20},{6,22},{8,24},{10,26},{12,28},{14,30},{16,0},... | collective-permute-start | bytes 172040 | tf_op jit(solution)/shard_map/ppermute | solution.py:398
  45.3 4.2 %collective-permute-start = (bf16[224,128]{1,0:T(8,128)(2,1)S(1)}, bf16[224,128]{1,0:T(8,128)(2,1)S(1)}, u32[]{:S(2)}, u32[]{:S(2)}) collective-permute-start(bf16[224,128]{1,0:T(8,128)(2,1)S(1)} %get-tuple-element.21.refs_0_), channel_id=1, source_target_pairs={{0,8},{2,10},{4,12},{6,14},{8,0},{10,2},{12,4},{14,6},{16,24},{18,... | collective-permute-start | bytes 172040 | tf_op jit(solution)/shard_map/ppermute | solution.py:398
  49.5 1.0 copy-start.6
  53.1 27.6 %copy-start = (bf16[2560,320]{0,1:T(8,128)(2,1)S(1)}, bf16[2560,320]{0,1:T(8,128)(2,1)}, u32[]{:S(2)}) copy-start(bf16[2560,320]{0,1:T(8,128)(2,1)} %param.13) | copy-start | bytes 4915204
  56.5 4.5 %collective-permute-start.9 = (bf16[240,128]{1,0:T(8,128)(2,1)S(1)}, bf16[240,128]{1,0:T(8,128)(2,1)S(1)}, u32[]{:S(2)}, u32[]{:S(2)}) collective-permute-start(bf16[240,128]{1,0:T(8,128)(2,1)S(1)} %get-tuple-element.29), channel_id=1, source_target_pairs={{0,8},{2,10},{4,12},{6,14},{8,0},{10,2},{12,4},{14,6},{16,24},{18,... | collective-permute-start | bytes 184328 | tf_op jit(solution)/shard_map/ppermute | solution.py:398
  56.6 5.4 %collective-permute-start.10 = (bf16[240,128]{1,0:T(8,128)(2,1)S(1)}, bf16[240,128]{1,0:T(8,128)(2,1)S(1)}, u32[]{:S(2)}, u32[]{:S(2)}) collective-permute-start(bf16[240,128]{1,0:T(8,128)(2,1)S(1)} %get-tuple-element.30), channel_id=1, source_target_pairs={{0,16},{2,18},{4,20},{6,22},{8,24},{10,26},{12,28},{14,30},{16,0},... | collective-permute-start | bytes 184328 | tf_op jit(solution)/shard_map/ppermute | solution.py:398
  59.5 6.7 %collective-permute-start.11 = (bf16[240,128]{1,0:T(8,128)(2,1)S(1)}, bf16[240,128]{1,0:T(8,128)(2,1)S(1)}, u32[]{:S(2)}, u32[]{:S(2)}) collective-permute-start(bf16[240,128]{1,0:T(8,128)(2,1)S(1)} %get-tuple-element.31), channel_id=1, source_target_pairs={{0,24},{2,26},{4,28},{6,30},{8,16},{10,18},{12,20},{14,22},{16,8},... | collective-permute-start | bytes 184328 | tf_op jit(solution)/shard_map/ppermute | solution.py:398
  66.5 6.1 %collective-permute-start.14 = (bf16[224,128]{1,0:T(8,128)(2,1)S(1)}, bf16[224,128]{1,0:T(8,128)(2,1)S(1)}, u32[]{:S(2)}, u32[]{:S(2)}) collective-permute-start(bf16[224,128]{1,0:T(8,128)(2,1)S(1)} %shard_map.77.refs_0_), channel_id=1, source_target_pairs={{0,24},{2,26},{4,28},{6,30},{8,16},{10,18},{12,20},{14,22},{16,8},... | collective-permute-start | bytes 172040 | tf_op jit(solution)/shard_map/ppermute | solution.py:398
  67.9 5.9 %collective-permute-start.13 = (bf16[224,128]{1,0:T(8,128)(2,1)S(1)}, bf16[224,128]{1,0:T(8,128)(2,1)S(1)}, u32[]{:S(2)}, u32[]{:S(2)}) collective-permute-start(bf16[224,128]{1,0:T(8,128)(2,1)S(1)} %shard_map.77.refs_0_), channel_id=1, source_target_pairs={{0,16},{2,18},{4,20},{6,22},{8,24},{10,26},{12,28},{14,30},{16,0},... | collective-permute-start | bytes 172040 | tf_op jit(solution)/shard_map/ppermute | solution.py:398
  67.9 5.9 %collective-permute-start.12 = (bf16[224,128]{1,0:T(8,128)(2,1)S(1)}, bf16[224,128]{1,0:T(8,128)(2,1)S(1)}, u32[]{:S(2)}, u32[]{:S(2)}) collective-permute-start(bf16[224,128]{1,0:T(8,128)(2,1)S(1)} %shard_map.77.refs_0_), channel_id=1, source_target_pairs={{0,8},{2,10},{4,12},{6,14},{8,0},{10,2},{12,4},{14,6},{16,24},{18,... | collective-permute-start | bytes 172040 | tf_op jit(solution)/shard_map/ppermute | solution.py:398
  73.8 4.9 %collective-permute-start.15 = (bf16[448,128]{1,0:T(8,128)(2,1)S(1)}, bf16[448,128]{1,0:T(8,128)(2,1)S(1)}, u32[]{:S(2)}, u32[]{:S(2)}) collective-permute-start(bf16[448,128]{1,0:T(8,128)(2,1)S(1)} %get-tuple-element.32.refs_0_), channel_id=1, source_target_pairs={{0,2},{2,0},{4,6},{6,4},{8,10},{10,8},{12,14},{14,12},{16,18},{18,... | collective-permute-start | bytes 344072 | tf_op jit(solution)/shard_map/ppermute | solution.py:398
  75.0 5.2 %collective-permute-start.17 = (bf16[448,128]{1,0:T(8,128)(2,1)S(1)}, bf16[448,128]{1,0:T(8,128)(2,1)S(1)}, u32[]{:S(2)}, u32[]{:S(2)}) collective-permute-start(bf16[448,128]{1,0:T(8,128)(2,1)S(1)} %get-tuple-element.33.refs_1_), channel_id=1, source_target_pairs={{0,4},{2,6},{4,0},{6,2},{8,12},{10,14},{12,8},{14,10},{16,20},{18,... | collective-permute-start | bytes 344072 | tf_op jit(solution)/shard_map/ppermute | solution.py:398
  75.5 5.6 %collective-permute-start.20 = (bf16[448,128]{1,0:T(8,128)(2,1)S(1)}, bf16[448,128]{1,0:T(8,128)(2,1)S(1)}, u32[]{:S(2)}, u32[]{:S(2)}) collective-permute-start(bf16[448,128]{1,0:T(8,128)(2,1)S(1)} %get-tuple-element.33.refs_1_), channel_id=1, source_target_pairs={{0,2},{2,0},{4,6},{6,4},{8,10},{10,8},{12,14},{14,12},{16,18},{18,... | collective-permute-start | bytes 344072 | tf_op jit(solution)/shard_map/ppermute | solution.py:398
  77.4 4.8 %collective-permute-start.19 = (bf16[448,128]{1,0:T(8,128)(2,1)S(1)}, bf16[448,128]{1,0:T(8,128)(2,1)S(1)}, u32[]{:S(2)}, u32[]{:S(2)}) collective-permute-start(bf16[448,128]{1,0:T(8,128)(2,1)S(1)} %get-tuple-element.32.refs_0_), channel_id=1, source_target_pairs={{0,4},{2,6},{4,0},{6,2},{8,12},{10,14},{12,8},{14,10},{16,20},{18,... | collective-permute-start | bytes 344072 | tf_op jit(solution)/shard_map/ppermute | solution.py:398
  78.7 5.5 %collective-permute-start.16 = (bf16[448,128]{1,0:T(8,128)(2,1)S(1)}, bf16[448,128]{1,0:T(8,128)(2,1)S(1)}, u32[]{:S(2)}, u32[]{:S(2)}) collective-permute-start(bf16[448,128]{1,0:T(8,128)(2,1)S(1)} %collective-permute-done.15.refs_0_), channel_id=1, source_target_pairs={{0,4},{2,6},{4,0},{6,2},{8,12},{10,14},{12,8},{14,10},{16,20},{18,... | collective-permute-start | bytes 344072 | tf_op jit(solution)/shard_map/ppermute | solution.py:398
  80.2 5.4 %collective-permute-start.18 = (bf16[448,128]{1,0:T(8,128)(2,1)S(1)}, bf16[448,128]{1,0:T(8,128)(2,1)S(1)}, u32[]{:S(2)}, u32[]{:S(2)}) collective-permute-start(bf16[448,128]{1,0:T(8,128)(2,1)S(1)} %collective-permute-done.17.refs_1_), channel_id=1, source_target_pairs={{0,2},{2,0},{4,6},{6,4},{8,10},{10,8},{12,14},{14,12},{16,18},{18,... | collective-permute-start | bytes 344072 | tf_op jit(solution)/shard_map/ppermute | solution.py:398
  85.5 15.6 %copy-start.3 = (bf16[256,2560]{1,0:T(8,128)(2,1)S(1)}, bf16[256,2560]{1,0:T(8,128)(2,1)}, u32[]{:S(2)}) copy-start(bf16[256,2560]{1,0:T(8,128)(2,1)} %refs_2_.1) | copy-start | bytes 3932164
  85.5 15.6 %copy-start.4 = (bf16[256,2560]{1,0:T(8,128)(2,1)S(1)}, bf16[256,2560]{1,0:T(8,128)(2,1)}, u32[]{:S(2)}) copy-start(bf16[256,2560]{1,0:T(8,128)(2,1)} %refs_3_.1) | copy-start | bytes 3932164
  85.5 15.6 %copy-start.7 = (s32[256]{0:T(256)S(1)}, s32[256]{0:T(256)}, u32[]{:S(2)}) copy-start(s32[256]{0:T(256)} %param.12) | copy-start | bytes 3076
  99.5 1.6 %collective-permute-start.21 = (bf16[16,80,128]{2,1,0:T(8,128)(2,1)S(1)}, bf16[16,80,128]{2,1,0:T(8,128)(2,1)S(1)}, u32[]{:S(2)}, u32[]{:S(2)}) collective-permute-start(bf16[16,80,128]{2,1,0:T(8,128)(2,1)S(1)} %all_to_all.10.refs_0_), channel_id=1, source_target_pairs={{0,1},{1,0},{2,3},{3,2},{4,5},{5,4},{6,7},{7,6},{8,9},{9,8},{10,11... | collective-permute-start | bytes 983048 | tf_op jit(solution)/shard_map/ppermute | solution.py:506

commit v7 on v6

--- a/solution.py
+++ b/solution.py
@@ -228,7 +228,7 @@
 
 def finish_kernel(plan, where_ref, near_ref, *refs):
     *refs, part_ref, held_ref = refs
-    attention_kernel(plan, 2, False, where_ref, *refs[: -plan.line], part_ref, held_ref)
+    attention_kernel(plan, 1, False, where_ref, *refs[: -plan.line], part_ref, held_ref)
     split_kernel(plan, where_ref, near_ref, part_ref, *refs[-plan.line :])
 
 
@@ -442,11 +442,15 @@
             dma((parts + 1,)), dma((blocks,)),
         ],
     )
-    near_k = [shift(part, i + 1) for i, part in enumerate(near_k)]
+    x_k = shift(near_k[0], 1)
+    y_k = shift(near_k[1], 2)
+    near_k = [x_k, y_k]
     spread = exchange(sent)
-    near_v = [shift(x_v, 1), shift(y_v, 2)]
+    x_v = shift(x_v, 1)
+    y_v = shift(y_v, 2)
+    near_v = [x_v, y_v]
     far = [shift(far_k, 3), shift(far_v, 3)]
-    near, far = [near_k[0], near_v[0]], [near_k[1], near_v[1], *far]
+    near = [part for pair in zip(near_k, near_v) for part in pair]
     chunk, info = call(
         partial(compact_kernel, plan),
         (shape(plan.rows, HD), shape(2, devices, HD, dtype=F32)), me, spread,
@@ -466,11 +470,11 @@
 
     scored_shape = (plan.line, plan.rows + TILE, HD)
     part = attend(
-        partial(attention_kernel, plan, 1, True), 2,
+        partial(attention_kernel, plan, 2, True), 3,
         shape(*scored_shape), *line, *near, keys, values,
     )
     sums = attend(
-        partial(finish_kernel, plan), 2,
+        partial(finish_kernel, plan), 1,
         tuple(shape(plan.rows + TILE, HD) for _ in range(plan.line)),
         part, *line, *far, scratch=[pltpu.VMEM(scored_shape, BF16)],
     )

time: 103 us -> 103 us (level)
  starting transfers between devices: 35.3 us -> 38.1 us
  local copies, waits for them, and re-layouts: 1.72 us -> 0.02 us
    ppermute x21, starting transfers between devices: 27 us -> 32.2 us  [shift(): return lax.ppermute(value, 'seq', pairs)]
    ppermute x21, waiting for transfers between devices: 36.2 us -> 32 us  [shift(): return lax.ppermute(value, 'seq', pairs)]
    all_to_all x1, waiting for transfers between devices: 0.01 us -> 3.52 us  [exchange(): return lax.all_to_all(value, 'seq', split_axis=0, concat_axis=0, tiled=True)]
    all_to_all x1, starting transfers between devices: 8.36 us -> 5.94 us  [exchange(): return lax.all_to_all(value, 'seq', split_axis=0, concat_axis=0, tiled=True)]
    unnamed x16 -> x12, local copies, waits for them, and re-layouts: 1.72 us -> 0.02 us
  transfers between devices with their start and end apart: 23 -> 23, of which waited for: 14 -> 13; matrix products, arithmetic and copies ran while one was open for 0% -> 0% of each run, Pallas kernels for 4% -> 4%
where the time goes in v7:
time: 103 us
  starting transfers between devices  38.1 us (37%)
  waiting for transfers between devices  37.1 us (36%)
  Pallas kernels  14.4 us (14%)
  blocking collectives  13.2 us (13%)
    ppermute x21, starting transfers between devices, shift(): return lax.ppermute(value, 'seq', pairs)  32.2 us
    ppermute x21, waiting for transfers between devices, shift(): return lax.ppermute(value, 'seq', pairs)  32 us
    pallas_call x11, Pallas kernels, call(): pl.pallas_call(kernel, out_shape=out_shape, in_specs=[spec(i, arg) for i,...  14.4 us
    all_to_all x1, blocking collectives, exchange(): return lax.all_to_all(value, 'seq', split_axis=0, concat_axis=0, tiled=True)  13.2 us
    all_to_all x1, starting transfers between devices, exchange(): return lax.all_to_all(value, 'seq', split_axis=0, concat_axis=0, tiled=True)  5.94 us
    all_to_all x1, waiting for transfers between devices, exchange(): return lax.all_to_all(value, 'seq', split_axis=0, concat_axis=0, tiled=True)  3.52 us
  transfers between devices with their start and end apart: 23, of which 13 were waited for; matrix products, arithmetic and copies ran while one was open for 0% of the time, Pallas kernels for 4%

profile of v7, /device:TPU:0, one launch (start us, length us, event | category | flops | bytes accessed | tf_op | source)
XLA Modules:
  0.0 103.0 jit_solution(12285723922102544137)
XLA Ops:
  0.0 4.3 %shard_map.73 = (bf16[16,72,128]{2,1,0:T(8,128)(2,1)}, bf16[256,640]{1,0:T(8,128)(2,1)}, bf16[256,640]{1,0:T(8,128)(2,1)}, bf16[256,640]{1,0:T(8,128)(2,1)}, bf1...) custom-call(s32[1,256]{1,0:T(1,128)} %bitcast.8, bf16[256,2560]{1,0:T(8,128)(2,1)} %q_hbm.1, ...), custom_call_target="tpu_custom_call" | custom-call | tf_op jit(solution)/shard_map/pallas_call | solution.py:378
  4.3 3.0 %collective-permute-start.3 = (bf16[256,640]{1,0:T(8,128)(2,1)}, bf16[256,640]{1,0:T(8,128)(2,1)S(1)}, u32[]{:S(2)}, u32[]{:S(2)}) collective-permute-start(bf16[256,640]{1,0:T(8,128)(2,1)} %get-tuple-element.22), channel_id=1, source_target_pairs={{0,2},{2,0},{4,6},{6,4},{8,10},{10,8},{12,14},{14,12},{16,18},{18,... | collective-permute-start | bytes 983048 | tf_op jit(solution)/shard_map/ppermute | solution.py:398
  7.4 5.9 %all-to-all-start = ((bf16[16,72,128]{2,1,0:T(8,128)(2,1)}), bf16[16,72,128]{2,1,0:T(8,128)(2,1)S(1)}, u32[]{:S(2)}, u32[]{:S(2)}) async-start(bf16[16,72,128]{2,1,0:T(8,128)(2,1)} %get-tuple-element.20), calls=%async_computation | async-start | bytes 589824 | tf_op jit(solution)/shard_map/all_to_all | solution.py:393
  13.3 1.9 %collective-permute-start.4 = (bf16[256,640]{1,0:T(8,128)(2,1)}, bf16[256,640]{1,0:T(8,128)(2,1)}, u32[]{:S(2)}, u32[]{:S(2)}) collective-permute-start(bf16[256,640]{1,0:T(8,128)(2,1)} %get-tuple-element.23), channel_id=1, source_target_pairs={{0,2},{2,0},{4,6},{6,4},{8,10},{10,8},{12,14},{14,12},{16,18},{18,... | collective-permute-start | bytes 983048 | tf_op jit(solution)/shard_map/ppermute | solution.py:398
  15.2 1.5 %collective-permute-start.5 = (bf16[256,640]{1,0:T(8,128)(2,1)}, bf16[256,640]{1,0:T(8,128)(2,1)}, u32[]{:S(2)}, u32[]{:S(2)}) collective-permute-start(bf16[256,640]{1,0:T(8,128)(2,1)} %get-tuple-element.24), channel_id=1, source_target_pairs={{0,4},{2,6},{4,0},{6,2},{8,12},{10,14},{12,8},{14,10},{16,20},{18,... | collective-permute-start | bytes 983048 | tf_op jit(solution)/shard_map/ppermute | solution.py:398
  16.7 0.6 collective-permute-start.6
  17.3 1.5 %collective-permute-start.7 = (bf16[256,640]{1,0:T(8,128)(2,1)}, bf16[256,640]{1,0:T(8,128)(2,1)}, u32[]{:S(2)}, u32[]{:S(2)}) collective-permute-start(bf16[256,640]{1,0:T(8,128)(2,1)} %get-tuple-element.26), channel_id=1, source_target_pairs={{0,6},{2,4},{4,2},{6,0},{8,14},{10,12},{12,10},{14,8},{16,22},{18,... | collective-permute-start | bytes 983048 | tf_op jit(solution)/shard_map/ppermute | solution.py:398
  18.7 0.0 collective-permute-done.3.refs_4_
  18.7 1.5 %collective-permute-start.8 = (bf16[256,640]{1,0:T(8,128)(2,1)}, bf16[256,640]{1,0:T(8,128)(2,1)}, u32[]{:S(2)}, u32[]{:S(2)}) collective-permute-start(bf16[256,640]{1,0:T(8,128)(2,1)} %get-tuple-element.27), channel_id=1, source_target_pairs={{0,6},{2,4},{4,2},{6,0},{8,14},{10,12},{12,10},{14,8},{16,22},{18,... | collective-permute-start | bytes 983048 | tf_op jit(solution)/shard_map/ppermute | solution.py:398
  20.2 3.5 %all-to-all-done.in_ref = bf16[16,72,128]{2,1,0:T(8,128)(2,1)S(1)} async-done(((bf16[16,72,128]{2,1,0:T(8,128)(2,1)}), bf16[16,72,128]{2,1,0:T(8,128)(2,1)S(1)}, u32[]{:S(2)}, u32[]{:S(2)}) %all-to-all-start) | async-done | bytes 294944 | tf_op jit(solution)/shard_map/all_to_all | solution.py:393
  23.7 0.5 shard_map.74
  24.2 2.8 %collective-permute-done.4.refs_5_ = bf16[256,640]{1,0:T(8,128)(2,1)} collective-permute-done((bf16[256,640]{1,0:T(8,128)(2,1)}, bf16[256,640]{1,0:T(8,128)(2,1)}, u32[]{:S(2)}, u32[]{:S(2)}) %collective-permute-start.4) | collective-permute-done | bytes 327712 | tf_op jit(solution)/shard_map/ppermute | solution.py:398
  27.0 3.2 %collective-permute-start.2 = (bf16[224,128]{1,0:T(8,128)(2,1)S(1)}, bf16[224,128]{1,0:T(8,128)(2,1)S(1)}, u32[]{:S(2)}, u32[]{:S(2)}) collective-permute-start(bf16[224,128]{1,0:T(8,128)(2,1)S(1)} %get-tuple-element.21.refs_0_), channel_id=1, source_target_pairs={{0,24},{2,26},{4,28},{6,30},{8,16},{10,18},{12,20},{14,22},{16,8},... | collective-permute-start | bytes 172040 | tf_op jit(solution)/shard_map/ppermute | solution.py:398
  30.1 11.4 %collective-permute-done.5.refs_6_ = bf16[256,640]{1,0:T(8,128)(2,1)} collective-permute-done((bf16[256,640]{1,0:T(8,128)(2,1)}, bf16[256,640]{1,0:T(8,128)(2,1)}, u32[]{:S(2)}, u32[]{:S(2)}) %collective-permute-start.5) | collective-permute-done | bytes 327712 | tf_op jit(solution)/shard_map/ppermute | solution.py:398
  41.6 2.4 %collective-permute-start.1 = (bf16[224,128]{1,0:T(8,128)(2,1)S(1)}, bf16[224,128]{1,0:T(8,128)(2,1)S(1)}, u32[]{:S(2)}, u32[]{:S(2)}) collective-permute-start(bf16[224,128]{1,0:T(8,128)(2,1)S(1)} %get-tuple-element.21.refs_0_), channel_id=1, source_target_pairs={{0,16},{2,18},{4,20},{6,22},{8,24},{10,26},{12,28},{14,30},{16,0},... | collective-permute-start | bytes 172040 | tf_op jit(solution)/shard_map/ppermute | solution.py:398
  44.0 3.5 %collective-permute-done.6.refs_7_ = bf16[256,640]{1,0:T(8,128)(2,1)} collective-permute-done((bf16[256,640]{1,0:T(8,128)(2,1)}, bf16[256,640]{1,0:T(8,128)(2,1)}, u32[]{:S(2)}, u32[]{:S(2)}) %collective-permute-start.6) | collective-permute-done | bytes 327712 | tf_op jit(solution)/shard_map/ppermute | solution.py:398
  47.5 1.5 %collective-permute-start = (bf16[224,128]{1,0:T(8,128)(2,1)S(1)}, bf16[224,128]{1,0:T(8,128)(2,1)S(1)}, u32[]{:S(2)}, u32[]{:S(2)}) collective-permute-start(bf16[224,128]{1,0:T(8,128)(2,1)S(1)} %get-tuple-element.21.refs_0_), channel_id=1, source_target_pairs={{0,8},{2,10},{4,12},{6,14},{8,0},{10,2},{12,4},{14,6},{16,24},{18,... | collective-permute-start | bytes 172040 | tf_op jit(solution)/shard_map/ppermute | solution.py:398
  49.0 0.0 collective-permute-done.2.refs_3_
  49.0 2.7 %collective-permute-done.refs_1_ = bf16[224,128]{1,0:T(8,128)(2,1)S(1)} collective-permute-done((bf16[224,128]{1,0:T(8,128)(2,1)S(1)}, bf16[224,128]{1,0:T(8,128)(2,1)S(1)}, u32[]{:S(2)}, u32[]{:S(2)}) %collective-permute-start) | collective-permute-done | bytes 57376 | tf_op jit(solution)/shard_map/ppermute | solution.py:398
  51.7 3.1 %shard_map.75.near_ref = bf16[4,240,128]{2,1,0:T(8,128)(2,1)S(1)} custom-call(s32[1]{0:T(128)} %bitcast.2.where_ref, bf16[224,128]{1,0:T(8,128)(2,1)S(1)} %get-tuple-element.21.refs_0_, bf16[224,128]{1,0:T(8,128)(2,1)S(1)} %collective-permute-done.refs_1_, bf16[224,128]{1,0:T(8,128)(2,1)S(1)} %collective-permute-done.1.refs_2_, ...), custom_call_target="tpu_custom_call" | custom-call | flops 346030080 | bytes 1966080 | tf_op jit(solution)/shard_map/pallas_call | solution.py:378
  54.9 2.6 %shard_map.76 = (bf16[240,128]{1,0:T(8,128)(2,1)S(1)}, bf16[240,128]{1,0:T(8,128)(2,1)S(1)}, bf16[240,128]{1,0:T(8,128)(2,1)S(1)}, bf16[240,128]{1,0:T(8,128)(2,1)S(1)}) custom-call(s32[1]{0:T(128)} %bitcast.2.where_ref, bf16[4,240,128]{2,1,0:T(8,128)(2,1)S(1)} %shard_map.75.near_ref, bf16[224,128]{1,0:T(8,128)(2,1)S(1)} %get-tuple-element.21.refs_0_, ...), custom_call_target="tpu_custom_call" | custom-call | flops 115343360 | bytes 655360 | tf_op jit(solution)/shard_map/pallas_call | solution.py:378
  57.5 1.6 %collective-permute-start.9 = (bf16[240,128]{1,0:T(8,128)(2,1)S(1)}, bf16[240,128]{1,0:T(8,128)(2,1)S(1)}, u32[]{:S(2)}, u32[]{:S(2)}) collective-permute-start(bf16[240,128]{1,0:T(8,128)(2,1)S(1)} %get-tuple-element.29), channel_id=1, source_target_pairs={{0,8},{2,10},{4,12},{6,14},{8,0},{10,2},{12,4},{14,6},{16,24},{18,... | collective-permute-start | bytes 184328 | tf_op jit(solution)/shard_map/ppermute | solution.py:398
  59.0 2.0 %collective-permute-start.10 = (bf16[240,128]{1,0:T(8,128)(2,1)S(1)}, bf16[240,128]{1,0:T(8,128)(2,1)S(1)}, u32[]{:S(2)}, u32[]{:S(2)}) collective-permute-start(bf16[240,128]{1,0:T(8,128)(2,1)S(1)} %get-tuple-element.30), channel_id=1, source_target_pairs={{0,16},{2,18},{4,20},{6,22},{8,24},{10,26},{12,28},{14,30},{16,0},... | collective-permute-start | bytes 184328 | tf_op jit(solution)/shard_map/ppermute | solution.py:398
  61.0 0.9 collective-permute-start.11
  61.9 3.3 %collective-permute-done.10.refs_2_ = bf16[240,128]{1,0:T(8,128)(2,1)S(1)} collective-permute-done((bf16[240,128]{1,0:T(8,128)(2,1)S(1)}, bf16[240,128]{1,0:T(8,128)(2,1)S(1)}, u32[]{:S(2)}, u32[]{:S(2)}) %collective-permute-start.10) | collective-permute-done | bytes 61472 | tf_op jit(solution)/shard_map/ppermute | solution.py:398
  65.2 1.9 %collective-permute-done.11.refs_3_ = bf16[240,128]{1,0:T(8,128)(2,1)S(1)} collective-permute-done((bf16[240,128]{1,0:T(8,128)(2,1)S(1)}, bf16[240,128]{1,0:T(8,128)(2,1)S(1)}, u32[]{:S(2)}, u32[]{:S(2)}) %collective-permute-start.11) | collective-permute-done | bytes 61472 | tf_op jit(solution)/shard_map/ppermute | solution.py:398
  67.1 0.3 shard_map.77.refs_0_
  67.4 0.9 collective-permute-start.14
  68.3 0.3 collective-permute-start.13
  68.6 3.3 %collective-permute-start.12 = (bf16[224,128]{1,0:T(8,128)(2,1)S(1)}, bf16[224,128]{1,0:T(8,128)(2,1)S(1)}, u32[]{:S(2)}, u32[]{:S(2)}) collective-permute-start(bf16[224,128]{1,0:T(8,128)(2,1)S(1)} %shard_map.77.refs_0_), channel_id=1, source_target_pairs={{0,8},{2,10},{4,12},{6,14},{8,0},{10,2},{12,4},{14,6},{16,24},{18,... | collective-permute-start | bytes 172040 | tf_op jit(solution)/shard_map/ppermute | solution.py:398
  71.9 1.7 %collective-permute-done.14.refs_3_ = bf16[224,128]{1,0:T(8,128)(2,1)S(1)} collective-permute-done((bf16[224,128]{1,0:T(8,128)(2,1)S(1)}, bf16[224,128]{1,0:T(8,128)(2,1)S(1)}, u32[]{:S(2)}, u32[]{:S(2)}) %collective-permute-start.14) | collective-permute-done | bytes 57376 | tf_op jit(solution)/shard_map/ppermute | solution.py:398
  73.6 1.1 %collective-permute-done.13.refs_2_ = bf16[224,128]{1,0:T(8,128)(2,1)S(1)} collective-permute-done((bf16[224,128]{1,0:T(8,128)(2,1)S(1)}, bf16[224,128]{1,0:T(8,128)(2,1)S(1)}, u32[]{:S(2)}, u32[]{:S(2)}) %collective-permute-start.13) | collective-permute-done | bytes 57376 | tf_op jit(solution)/shard_map/ppermute | solution.py:398
  74.7 0.9 collective-permute-start.15
  75.6 1.2 %collective-permute-start.17 = (bf16[448,128]{1,0:T(8,128)(2,1)S(1)}, bf16[448,128]{1,0:T(8,128)(2,1)S(1)}, u32[]{:S(2)}, u32[]{:S(2)}) collective-permute-start(bf16[448,128]{1,0:T(8,128)(2,1)S(1)} %get-tuple-element.33.refs_1_), channel_id=1, source_target_pairs={{0,4},{2,6},{4,0},{6,2},{8,12},{10,14},{12,8},{14,10},{16,20},{18,... | collective-permute-start | bytes 344072 | tf_op jit(solution)/shard_map/ppermute | solution.py:398
  76.8 0.8 collective-permute-start.20
  77.6 1.2 %collective-permute-start.19 = (bf16[448,128]{1,0:T(8,128)(2,1)S(1)}, bf16[448,128]{1,0:T(8,128)(2,1)S(1)}, u32[]{:S(2)}, u32[]{:S(2)}) collective-permute-start(bf16[448,128]{1,0:T(8,128)(2,1)S(1)} %get-tuple-element.32.refs_0_), channel_id=1, source_target_pairs={{0,4},{2,6},{4,0},{6,2},{8,12},{10,14},{12,8},{14,10},{16,20},{18,... | collective-permute-start | bytes 344072 | tf_op jit(solution)/shard_map/ppermute | solution.py:398
  78.8 1.0 collective-permute-done.15.refs_0_
  79.8 1.0 collective-permute-start.16
  80.8 1.1 %collective-permute-start.18 = (bf16[448,128]{1,0:T(8,128)(2,1)S(1)}, bf16[448,128]{1,0:T(8,128)(2,1)S(1)}, u32[]{:S(2)}, u32[]{:S(2)}) collective-permute-start(bf16[448,128]{1,0:T(8,128)(2,1)S(1)} %collective-permute-done.17.refs_1_), channel_id=1, source_target_pairs={{0,2},{2,0},{4,6},{6,4},{8,10},{10,8},{12,14},{14,12},{16,18},{18,... | collective-permute-start | bytes 344072 | tf_op jit(solution)/shard_map/ppermute | solution.py:398
  82.0 0.3 shard_map.79.refs_2_
  82.3 0.3 shard_map.80.refs_2_
  82.6 0.3 shard_map.81.sum_ref
  83.0 1.6 %collective-permute-done.16.low_ref = bf16[448,128]{1,0:T(8,128)(2,1)S(1)} collective-permute-done((bf16[448,128]{1,0:T(8,128)(2,1)S(1)}, bf16[448,128]{1,0:T(8,128)(2,1)S(1)}, u32[]{:S(2)}, u32[]{:S(2)}) %collective-permute-start.16) | collective-permute-done | bytes 114720 | tf_op jit(solution)/shard_map/ppermute | solution.py:398
  84.6 1.0 %collective-permute-done.18.high_ref = bf16[448,128]{1,0:T(8,128)(2,1)S(1)} collective-permute-done((bf16[448,128]{1,0:T(8,128)(2,1)S(1)}, bf16[448,128]{1,0:T(8,128)(2,1)S(1)}, u32[]{:S(2)}, u32[]{:S(2)}) %collective-permute-start.18) | collective-permute-done | bytes 114720 | tf_op jit(solution)/shard_map/ppermute | solution.py:398
  85.6 0.7 shard_map.82
  86.4 13.2 %all_to_all.10.refs_0_ = bf16[16,80,128]{2,1,0:T(8,128)(2,1)S(1)} all-to-all(bf16[16,80,128]{2,1,0:T(8,128)(2,1)S(1)} %shard_map.82), channel_id=1, replica_groups=mesh['seq'=16,'head'=2] {'seq'}, dimensions={0} | all-to-all | bytes 655360 | tf_op jit(solution)/shard_map/all_to_all | solution.py:393
  99.6 1.6 %collective-permute-done.21.refs_1_ = bf16[16,80,128]{2,1,0:T(8,128)(2,1)S(1)} collective-permute-done((bf16[16,80,128]{2,1,0:T(8,128)(2,1)S(1)}, bf16[16,80,128]{2,1,0:T(8,128)(2,1)S(1)}, u32[]{:S(2)}, u32[]{:S(2)}) %collective-permute-start.21) | collective-permute-done | bytes 327712 | tf_op jit(solution)/shard_map/ppermute | solution.py:510
  101.2 1.8 %shard_map.83 = bf16[256,2560]{1,0:T(8,128)(2,1)} custom-call(s32[1]{0:T(128)} %bitcast.half_ref, s32[1,256]{1,0:T(1,128)S(1)} %bitcast.9, bf16[16,80,128]{2,1,0:T(8,128)(2,1)S(1)} %all_to_all.10.refs_0_, bf16[16,80,128]{2,1,0:T(8,128)(2,1)S(1)} %collective-permute-done.21.refs_1_, bf16[256,2560]{1,0:T(8,128)(2,1)S(1)} %copy-done.3, ...), custom_call_target="tpu_custom_call" | custom-call | tf_op jit(solution)/shard_map/pallas_call | solution.py:378
  (22 shorter events, 0.1 us)
Async XLA Ops:
  0.0 51.7 %copy-start.1 = (bf16[256,2560]{1,0:T(8,128)(2,1)S(1)}, bf16[256,2560]{1,0:T(8,128)(2,1)}, u32[]{:S(2)}) copy-start(bf16[256,2560]{1,0:T(8,128)(2,1)} %refs_8_.1) | copy-start | bytes 3932164
  0.0 51.7 %copy-start.2 = (bf16[256,2560]{1,0:T(8,128)(2,1)S(1)}, bf16[256,2560]{1,0:T(8,128)(2,1)}, u32[]{:S(2)}) copy-start(bf16[256,2560]{1,0:T(8,128)(2,1)} %refs_9_.1) | copy-start | bytes 3932164
  4.3 14.4 %collective-permute-start.3 = (bf16[256,640]{1,0:T(8,128)(2,1)}, bf16[256,640]{1,0:T(8,128)(2,1)S(1)}, u32[]{:S(2)}, u32[]{:S(2)}) collective-permute-start(bf16[256,640]{1,0:T(8,128)(2,1)} %get-tuple-element.22), channel_id=1, source_target_pairs={{0,2},{2,0},{4,6},{6,4},{8,10},{10,8},{12,14},{14,12},{16,18},{18,... | collective-permute-start | bytes 983048 | tf_op jit(solution)/shard_map/ppermute | solution.py:398
  7.4 16.4 %all-to-all-start = ((bf16[16,72,128]{2,1,0:T(8,128)(2,1)}), bf16[16,72,128]{2,1,0:T(8,128)(2,1)S(1)}, u32[]{:S(2)}, u32[]{:S(2)}) async-start(bf16[16,72,128]{2,1,0:T(8,128)(2,1)} %get-tuple-element.20), calls=%async_computation | async-start | bytes 589824 | tf_op jit(solution)/shard_map/all_to_all | solution.py:393
  13.3 13.7 %collective-permute-start.4 = (bf16[256,640]{1,0:T(8,128)(2,1)}, bf16[256,640]{1,0:T(8,128)(2,1)}, u32[]{:S(2)}, u32[]{:S(2)}) collective-permute-start(bf16[256,640]{1,0:T(8,128)(2,1)} %get-tuple-element.23), channel_id=1, source_target_pairs={{0,2},{2,0},{4,6},{6,4},{8,10},{10,8},{12,14},{14,12},{16,18},{18,... | collective-permute-start | bytes 983048 | tf_op jit(solution)/shard_map/ppermute | solution.py:398
  15.2 26.3 %collective-permute-start.5 = (bf16[256,640]{1,0:T(8,128)(2,1)}, bf16[256,640]{1,0:T(8,128)(2,1)}, u32[]{:S(2)}, u32[]{:S(2)}) collective-permute-start(bf16[256,640]{1,0:T(8,128)(2,1)} %get-tuple-element.24), channel_id=1, source_target_pairs={{0,4},{2,6},{4,0},{6,2},{8,12},{10,14},{12,8},{14,10},{16,20},{18,... | collective-permute-start | bytes 983048 | tf_op jit(solution)/shard_map/ppermute | solution.py:398
  16.7 30.8 %collective-permute-start.6 = (bf16[256,640]{1,0:T(8,128)(2,1)}, bf16[256,640]{1,0:T(8,128)(2,1)}, u32[]{:S(2)}, u32[]{:S(2)}) collective-permute-start(bf16[256,640]{1,0:T(8,128)(2,1)} %get-tuple-element.25), channel_id=1, source_target_pairs={{0,4},{2,6},{4,0},{6,2},{8,12},{10,14},{12,8},{14,10},{16,20},{18,... | collective-permute-start | bytes 983048 | tf_op jit(solution)/shard_map/ppermute | solution.py:398
  17.3 37.6 %collective-permute-start.7 = (bf16[256,640]{1,0:T(8,128)(2,1)}, bf16[256,640]{1,0:T(8,128)(2,1)}, u32[]{:S(2)}, u32[]{:S(2)}) collective-permute-start(bf16[256,640]{1,0:T(8,128)(2,1)} %get-tuple-element.26), channel_id=1, source_target_pairs={{0,6},{2,4},{4,2},{6,0},{8,14},{10,12},{12,10},{14,8},{16,22},{18,... | collective-permute-start | bytes 983048 | tf_op jit(solution)/shard_map/ppermute | solution.py:398
  18.7 36.1 %collective-permute-start.8 = (bf16[256,640]{1,0:T(8,128)(2,1)}, bf16[256,640]{1,0:T(8,128)(2,1)}, u32[]{:S(2)}, u32[]{:S(2)}) collective-permute-start(bf16[256,640]{1,0:T(8,128)(2,1)} %get-tuple-element.27), channel_id=1, source_target_pairs={{0,6},{2,4},{4,2},{6,0},{8,14},{10,12},{12,10},{14,8},{16,22},{18,... | collective-permute-start | bytes 983048 | tf_op jit(solution)/shard_map/ppermute | solution.py:398
  27.0 22.0 %collective-permute-start.2 = (bf16[224,128]{1,0:T(8,128)(2,1)S(1)}, bf16[224,128]{1,0:T(8,128)(2,1)S(1)}, u32[]{:S(2)}, u32[]{:S(2)}) collective-permute-start(bf16[224,128]{1,0:T(8,128)(2,1)S(1)} %get-tuple-element.21.refs_0_), channel_id=1, source_target_pairs={{0,24},{2,26},{4,28},{6,30},{8,16},{10,18},{12,20},{14,22},{16,8},... | collective-permute-start | bytes 172040 | tf_op jit(solution)/shard_map/ppermute | solution.py:398
  41.6 7.4 %collective-permute-start.1 = (bf16[224,128]{1,0:T(8,128)(2,1)S(1)}, bf16[224,128]{1,0:T(8,128)(2,1)S(1)}, u32[]{:S(2)}, u32[]{:S(2)}) collective-permute-start(bf16[224,128]{1,0:T(8,128)(2,1)S(1)} %get-tuple-element.21.refs_0_), channel_id=1, source_target_pairs={{0,16},{2,18},{4,20},{6,22},{8,24},{10,26},{12,28},{14,30},{16,0},... | collective-permute-start | bytes 172040 | tf_op jit(solution)/shard_map/ppermute | solution.py:398
  47.5 4.2 %collective-permute-start = (bf16[224,128]{1,0:T(8,128)(2,1)S(1)}, bf16[224,128]{1,0:T(8,128)(2,1)S(1)}, u32[]{:S(2)}, u32[]{:S(2)}) collective-permute-start(bf16[224,128]{1,0:T(8,128)(2,1)S(1)} %get-tuple-element.21.refs_0_), channel_id=1, source_target_pairs={{0,8},{2,10},{4,12},{6,14},{8,0},{10,2},{12,4},{14,6},{16,24},{18,... | collective-permute-start | bytes 172040 | tf_op jit(solution)/shard_map/ppermute | solution.py:398
  54.9 27.1 %copy-start = (bf16[2560,320]{0,1:T(8,128)(2,1)S(1)}, bf16[2560,320]{0,1:T(8,128)(2,1)}, u32[]{:S(2)}) copy-start(bf16[2560,320]{0,1:T(8,128)(2,1)} %param.13) | copy-start | bytes 4915204
  57.5 4.5 %collective-permute-start.9 = (bf16[240,128]{1,0:T(8,128)(2,1)S(1)}, bf16[240,128]{1,0:T(8,128)(2,1)S(1)}, u32[]{:S(2)}, u32[]{:S(2)}) collective-permute-start(bf16[240,128]{1,0:T(8,128)(2,1)S(1)} %get-tuple-element.29), channel_id=1, source_target_pairs={{0,8},{2,10},{4,12},{6,14},{8,0},{10,2},{12,4},{14,6},{16,24},{18,... | collective-permute-start | bytes 184328 | tf_op jit(solution)/shard_map/ppermute | solution.py:398
  59.0 6.2 %collective-permute-start.10 = (bf16[240,128]{1,0:T(8,128)(2,1)S(1)}, bf16[240,128]{1,0:T(8,128)(2,1)S(1)}, u32[]{:S(2)}, u32[]{:S(2)}) collective-permute-start(bf16[240,128]{1,0:T(8,128)(2,1)S(1)} %get-tuple-element.30), channel_id=1, source_target_pairs={{0,16},{2,18},{4,20},{6,22},{8,24},{10,26},{12,28},{14,30},{16,0},... | collective-permute-start | bytes 184328 | tf_op jit(solution)/shard_map/ppermute | solution.py:398
  61.0 6.1 %collective-permute-start.11 = (bf16[240,128]{1,0:T(8,128)(2,1)S(1)}, bf16[240,128]{1,0:T(8,128)(2,1)S(1)}, u32[]{:S(2)}, u32[]{:S(2)}) collective-permute-start(bf16[240,128]{1,0:T(8,128)(2,1)S(1)} %get-tuple-element.31), channel_id=1, source_target_pairs={{0,24},{2,26},{4,28},{6,30},{8,16},{10,18},{12,20},{14,22},{16,8},... | collective-permute-start | bytes 184328 | tf_op jit(solution)/shard_map/ppermute | solution.py:398
  67.4 6.2 %collective-permute-start.14 = (bf16[224,128]{1,0:T(8,128)(2,1)S(1)}, bf16[224,128]{1,0:T(8,128)(2,1)S(1)}, u32[]{:S(2)}, u32[]{:S(2)}) collective-permute-start(bf16[224,128]{1,0:T(8,128)(2,1)S(1)} %shard_map.77.refs_0_), channel_id=1, source_target_pairs={{0,24},{2,26},{4,28},{6,30},{8,16},{10,18},{12,20},{14,22},{16,8},... | collective-permute-start | bytes 172040 | tf_op jit(solution)/shard_map/ppermute | solution.py:398
  68.3 6.3 %collective-permute-start.13 = (bf16[224,128]{1,0:T(8,128)(2,1)S(1)}, bf16[224,128]{1,0:T(8,128)(2,1)S(1)}, u32[]{:S(2)}, u32[]{:S(2)}) collective-permute-start(bf16[224,128]{1,0:T(8,128)(2,1)S(1)} %shard_map.77.refs_0_), channel_id=1, source_target_pairs={{0,16},{2,18},{4,20},{6,22},{8,24},{10,26},{12,28},{14,30},{16,0},... | collective-permute-start | bytes 172040 | tf_op jit(solution)/shard_map/ppermute | solution.py:398
  68.6 6.0 %collective-permute-start.12 = (bf16[224,128]{1,0:T(8,128)(2,1)S(1)}, bf16[224,128]{1,0:T(8,128)(2,1)S(1)}, u32[]{:S(2)}, u32[]{:S(2)}) collective-permute-start(bf16[224,128]{1,0:T(8,128)(2,1)S(1)} %shard_map.77.refs_0_), channel_id=1, source_target_pairs={{0,8},{2,10},{4,12},{6,14},{8,0},{10,2},{12,4},{14,6},{16,24},{18,... | collective-permute-start | bytes 172040 | tf_op jit(solution)/shard_map/ppermute | solution.py:398
  74.7 5.1 %collective-permute-start.15 = (bf16[448,128]{1,0:T(8,128)(2,1)S(1)}, bf16[448,128]{1,0:T(8,128)(2,1)S(1)}, u32[]{:S(2)}, u32[]{:S(2)}) collective-permute-start(bf16[448,128]{1,0:T(8,128)(2,1)S(1)} %get-tuple-element.32.refs_0_), channel_id=1, source_target_pairs={{0,2},{2,0},{4,6},{6,4},{8,10},{10,8},{12,14},{14,12},{16,18},{18,... | collective-permute-start | bytes 344072 | tf_op jit(solution)/shard_map/ppermute | solution.py:398
  75.6 5.2 %collective-permute-start.17 = (bf16[448,128]{1,0:T(8,128)(2,1)S(1)}, bf16[448,128]{1,0:T(8,128)(2,1)S(1)}, u32[]{:S(2)}, u32[]{:S(2)}) collective-permute-start(bf16[448,128]{1,0:T(8,128)(2,1)S(1)} %get-tuple-element.33.refs_1_), channel_id=1, source_target_pairs={{0,4},{2,6},{4,0},{6,2},{8,12},{10,14},{12,8},{14,10},{16,20},{18,... | collective-permute-start | bytes 344072 | tf_op jit(solution)/shard_map/ppermute | solution.py:398
  76.8 5.5 %collective-permute-start.20 = (bf16[448,128]{1,0:T(8,128)(2,1)S(1)}, bf16[448,128]{1,0:T(8,128)(2,1)S(1)}, u32[]{:S(2)}, u32[]{:S(2)}) collective-permute-start(bf16[448,128]{1,0:T(8,128)(2,1)S(1)} %get-tuple-element.33.refs_1_), channel_id=1, source_target_pairs={{0,2},{2,0},{4,6},{6,4},{8,10},{10,8},{12,14},{14,12},{16,18},{18,... | collective-permute-start | bytes 344072 | tf_op jit(solution)/shard_map/ppermute | solution.py:398
  77.6 5.0 %collective-permute-start.19 = (bf16[448,128]{1,0:T(8,128)(2,1)S(1)}, bf16[448,128]{1,0:T(8,128)(2,1)S(1)}, u32[]{:S(2)}, u32[]{:S(2)}) collective-permute-start(bf16[448,128]{1,0:T(8,128)(2,1)S(1)} %get-tuple-element.32.refs_0_), channel_id=1, source_target_pairs={{0,4},{2,6},{4,0},{6,2},{8,12},{10,14},{12,8},{14,10},{16,20},{18,... | collective-permute-start | bytes 344072 | tf_op jit(solution)/shard_map/ppermute | solution.py:398
  79.8 4.8 %collective-permute-start.16 = (bf16[448,128]{1,0:T(8,128)(2,1)S(1)}, bf16[448,128]{1,0:T(8,128)(2,1)S(1)}, u32[]{:S(2)}, u32[]{:S(2)}) collective-permute-start(bf16[448,128]{1,0:T(8,128)(2,1)S(1)} %collective-permute-done.15.refs_0_), channel_id=1, source_target_pairs={{0,4},{2,6},{4,0},{6,2},{8,12},{10,14},{12,8},{14,10},{16,20},{18,... | collective-permute-start | bytes 344072 | tf_op jit(solution)/shard_map/ppermute | solution.py:398
  80.8 4.8 %collective-permute-start.18 = (bf16[448,128]{1,0:T(8,128)(2,1)S(1)}, bf16[448,128]{1,0:T(8,128)(2,1)S(1)}, u32[]{:S(2)}, u32[]{:S(2)}) collective-permute-start(bf16[448,128]{1,0:T(8,128)(2,1)S(1)} %collective-permute-done.17.refs_1_), channel_id=1, source_target_pairs={{0,2},{2,0},{4,6},{6,4},{8,10},{10,8},{12,14},{14,12},{16,18},{18,... | collective-permute-start | bytes 344072 | tf_op jit(solution)/shard_map/ppermute | solution.py:398
  85.6 15.6 %copy-start.3 = (bf16[256,2560]{1,0:T(8,128)(2,1)S(1)}, bf16[256,2560]{1,0:T(8,128)(2,1)}, u32[]{:S(2)}) copy-start(bf16[256,2560]{1,0:T(8,128)(2,1)} %refs_2_.1) | copy-start | bytes 3932164
  85.6 15.6 %copy-start.4 = (bf16[256,2560]{1,0:T(8,128)(2,1)S(1)}, bf16[256,2560]{1,0:T(8,128)(2,1)}, u32[]{:S(2)}) copy-start(bf16[256,2560]{1,0:T(8,128)(2,1)} %refs_3_.1) | copy-start | bytes 3932164
  85.6 15.6 %copy-start.5 = (s32[256]{0:T(256)S(1)}, s32[256]{0:T(256)}, u32[]{:S(2)}) copy-start(s32[256]{0:T(256)} %param.12) | copy-start | bytes 3076
  99.6 1.6 %collective-permute-start.21 = (bf16[16,80,128]{2,1,0:T(8,128)(2,1)S(1)}, bf16[16,80,128]{2,1,0:T(8,128)(2,1)S(1)}, u32[]{:S(2)}, u32[]{:S(2)}) collective-permute-start(bf16[16,80,128]{2,1,0:T(8,128)(2,1)S(1)} %all_to_all.10.refs_0_), channel_id=1, source_target_pairs={{0,1},{1,0},{2,3},{3,2},{4,5},{5,4},{6,7},{7,6},{8,9},{9,8},{10,11... | collective-permute-start | bytes 983048 | tf_op jit(solution)/shard_map/ppermute | solution.py:510

commit v8 on v7

--- a/solution.py
+++ b/solution.py
@@ -115,13 +115,21 @@
         copy.wait()
 
 
-def compact_kernel(plan, where_ref, in_ref, out_ref, info_ref):
+def compact_kernel(plan, where_ref, act_ref, in_ref, out_ref, pick_ref, chosen_ref, active_ref):
     devices, cap = plan.devices, plan.cap
     count = jnp.max(in_ref[:, plan.spans * cap :, :].astype(F32), axis=1)
     earlier = (iota((devices, devices), 1) < iota((devices, devices), 0)).astype(BF16)
     offset = jnp.dot(earlier, count.astype(BF16), preferred_element_type=F32)
-    info_ref[0] = count
-    info_ref[1] = offset
+    chosen = own_selection(act_ref[...].astype(F32), cap)
+    chosen_ref[...] = chosen
+    active_ref[...] = lax.dot_general(
+        chosen, jnp.ones((cap, HD), BF16), ROWS_BOTH, preferred_element_type=F32
+    )
+    for device in range(devices):
+        slot = iota((cap, plan.tok), 0)
+        here = iota((cap, plan.tok), 1) - offset[device : device + 1, 0:1] == slot
+        pick = (here & (slot < count[device : device + 1, 0:1])).astype(F32).astype(BF16)
+        pick_ref[device * cap : (device + 1) * cap, :] = pick
     slots = devices * cap
     place = iota((devices, slots), 1) - iota((devices, slots), 0) * cap
     held = (place >= 0) & (place < jnp.minimum(count[:, 0:1], float(cap)))
@@ -276,33 +284,23 @@
     out_ref[...] = total
 
 
-def place_kernel(plan, step, where_ref, w_ref, low_ref, high_ref, sum_ref, info_ref, out_ref):
-    devices, cap, tok = plan.devices, plan.cap, plan.tok
+def place_kernel(plan, step, where_ref, w_ref, low_ref, high_ref, sum_ref, pick_ref, out_ref):
+    devices, cap = plan.devices, plan.cap
     quad = (where_ref[0] & (QUAD - 1)) ^ step
     proj = sum_ref[...] + project_group(plan, quad, (low_ref, high_ref), w_ref)
-    picks = []
-    for device in range(devices):
-        place = iota((cap, tok), 0)
-        count = info_ref[0, device : device + 1, 0:1]
-        offset = info_ref[1, device : device + 1, 0:1]
-        picks.append(
-            ((iota((cap, tok), 1) - offset == place) & (place < count)).astype(F32).astype(BF16)
-        )
-    pick = jnp.concatenate(picks, axis=0)
-    laid = jnp.dot(pick, proj.astype(BF16), preferred_element_type=F32)
+    laid = jnp.dot(pick_ref[...], proj.astype(BF16), preferred_element_type=F32)
     for device in range(devices):
         rows = laid[device * cap : (device + 1) * cap]
         out_ref[device] = pack_rows(rows, cap, w_ref.shape[0]).astype(BF16)
 
 
-def update_kernel(plan, halves, half_ref, act_ref, *refs):
+def update_kernel(plan, halves, half_ref, chosen_ref, active_ref, *refs):
     *term_refs, hidden_ref, cached_ref, out_hbm, held_ref, sems = refs
     cap, width = plan.cap, hidden_ref.shape[1] * halves // plan.devices
     wide = math.lcm(width, HD)
     blocks, steps = wide // width, hidden_ref.shape[1] // wide
-    chosen = own_selection(act_ref[...].astype(F32), cap)
-    mask = lax.dot_general(chosen, jnp.ones((cap, HD), BF16), ROWS_BOTH, preferred_element_type=F32)
-    active = mask[:, 0:1] > 0
+    chosen = chosen_ref[...]
+    active = active_ref[:, 0:1] > 0
     copies = []
     for step in range(steps):
         terms = []
@@ -451,9 +449,13 @@
     near_v = [x_v, y_v]
     far = [shift(far_k, 3), shift(far_v, 3)]
     near = [part for pair in zip(near_k, near_v) for part in pair]
-    chunk, info = call(
+    chunk, pick, chosen, is_active = call(
         partial(compact_kernel, plan),
-        (shape(plan.rows, HD), shape(2, devices, HD, dtype=F32)), me, spread,
+        (
+            shape(plan.rows, HD), shape(devices * cap, plan.tok), shape(cap, tok_dev),
+            shape(tok_dev, HD, dtype=F32),
+        ),
+        me, act, spread,
     )
     line = line_gather(plan, chunk)
     scored = plan.own_heads * plan.tok * tok_dev
@@ -501,7 +503,7 @@
         )
     terms = call(
         partial(place_kernel, plan, QUAD - 1),
-        shape(devices, packing(cap, columns)[0], HD), me, w_rows, *groups[QUAD - 1], proj, info,
+        shape(devices, packing(cap, columns)[0], HD), me, w_rows, *groups[QUAD - 1], proj, pick,
     )
     arrived = exchange(terms)
 
@@ -513,7 +515,7 @@
         term_args = [lax.all_to_all(split, "head", split_axis=0, concat_axis=0, tiled=True)]
     return call(
         partial(update_kernel, plan, halves),
-        shape(tok_dev, features), half, act, *term_args, hidden, cached, out_hbm=(0,),
+        shape(tok_dev, features), half, chosen, is_active, *term_args, hidden, cached, out_hbm=(0,),
         scratch_shapes=[
             pltpu.VMEM((tok_dev, features), BF16),
             dma((features // math.lcm(columns, HD),)),

time: 103 us -> 103 us (level)
  transfers between devices with their start and end apart: 23 -> 23, of which waited for: 13 -> 13; matrix products, arithmetic and copies ran while one was open for 0% -> 0% of each run, Pallas kernels for 4% -> 5%
where the time goes in v8:
time: 103 us
  starting transfers between devices  38.1 us (37%)
  waiting for transfers between devices  37 us (36%)
  Pallas kernels  14.5 us (14%)
  blocking collectives  13.2 us (13%)
    ppermute x21, starting transfers between devices, shift(): return lax.ppermute(value, 'seq', pairs)  32.2 us
    ppermute x21, waiting for transfers between devices, shift(): return lax.ppermute(value, 'seq', pairs)  31.9 us
    pallas_call x11, Pallas kernels, call(): pl.pallas_call(kernel, out_shape=out_shape, in_specs=[spec(i, arg) for i,...  14.5 us
    all_to_all x1, blocking collectives, exchange(): return lax.all_to_all(value, 'seq', split_axis=0, concat_axis=0, tiled=True)  13.2 us
    all_to_all x1, starting transfers between devices, exchange(): return lax.all_to_all(value, 'seq', split_axis=0, concat_axis=0, tiled=True)  5.93 us
    all_to_all x1, waiting for transfers between devices, exchange(): return lax.all_to_all(value, 'seq', split_axis=0, concat_axis=0, tiled=True)  3.52 us
  transfers between devices with their start and end apart: 23, of which 13 were waited for; matrix products, arithmetic and copies ran while one was open for 0% of the time, Pallas kernels for 5%

profile of v8, /device:TPU:0, one launch (start us, length us, event | category | flops | bytes accessed | tf_op | source)
XLA Modules:
  0.0 103.0 jit_solution(8612855910301013023)
XLA Ops:
  0.0 4.4 %shard_map.73 = (bf16[16,72,128]{2,1,0:T(8,128)(2,1)}, bf16[256,640]{1,0:T(8,128)(2,1)}, bf16[256,640]{1,0:T(8,128)(2,1)}, bf16[256,640]{1,0:T(8,128)(2,1)}, bf1...) custom-call(s32[1,256]{1,0:T(1,128)} %bitcast.8, bf16[256,2560]{1,0:T(8,128)(2,1)} %q_hbm.1, ...), custom_call_target="tpu_custom_call" | custom-call | tf_op jit(solution)/shard_map/pallas_call | solution.py:376
  4.4 3.1 %collective-permute-start.3 = (bf16[256,640]{1,0:T(8,128)(2,1)}, bf16[256,640]{1,0:T(8,128)(2,1)S(1)}, u32[]{:S(2)}, u32[]{:S(2)}) collective-permute-start(bf16[256,640]{1,0:T(8,128)(2,1)} %get-tuple-element.26), channel_id=1, source_target_pairs={{0,2},{2,0},{4,6},{6,4},{8,10},{10,8},{12,14},{14,12},{16,18},{18,... | collective-permute-start | bytes 983048 | tf_op jit(solution)/shard_map/ppermute | solution.py:396
  7.5 5.9 %all-to-all-start = ((bf16[16,72,128]{2,1,0:T(8,128)(2,1)}), bf16[16,72,128]{2,1,0:T(8,128)(2,1)S(1)}, u32[]{:S(2)}, u32[]{:S(2)}) async-start(bf16[16,72,128]{2,1,0:T(8,128)(2,1)} %get-tuple-element.22), calls=%async_computation | async-start | bytes 589824 | tf_op jit(solution)/shard_map/all_to_all | solution.py:391
  13.5 1.9 %collective-permute-start.4 = (bf16[256,640]{1,0:T(8,128)(2,1)}, bf16[256,640]{1,0:T(8,128)(2,1)}, u32[]{:S(2)}, u32[]{:S(2)}) collective-permute-start(bf16[256,640]{1,0:T(8,128)(2,1)} %get-tuple-element.27), channel_id=1, source_target_pairs={{0,2},{2,0},{4,6},{6,4},{8,10},{10,8},{12,14},{14,12},{16,18},{18,... | collective-permute-start | bytes 983048 | tf_op jit(solution)/shard_map/ppermute | solution.py:396
  15.4 1.5 %collective-permute-start.5 = (bf16[256,640]{1,0:T(8,128)(2,1)}, bf16[256,640]{1,0:T(8,128)(2,1)}, u32[]{:S(2)}, u32[]{:S(2)}) collective-permute-start(bf16[256,640]{1,0:T(8,128)(2,1)} %get-tuple-element.28), channel_id=1, source_target_pairs={{0,4},{2,6},{4,0},{6,2},{8,12},{10,14},{12,8},{14,10},{16,20},{18,... | collective-permute-start | bytes 983048 | tf_op jit(solution)/shard_map/ppermute | solution.py:396
  16.9 0.6 collective-permute-start.6
  17.4 1.5 %collective-permute-start.7 = (bf16[256,640]{1,0:T(8,128)(2,1)}, bf16[256,640]{1,0:T(8,128)(2,1)}, u32[]{:S(2)}, u32[]{:S(2)}) collective-permute-start(bf16[256,640]{1,0:T(8,128)(2,1)} %get-tuple-element.30), channel_id=1, source_target_pairs={{0,6},{2,4},{4,2},{6,0},{8,14},{10,12},{12,10},{14,8},{16,22},{18,... | collective-permute-start | bytes 983048 | tf_op jit(solution)/shard_map/ppermute | solution.py:396
  18.9 1.5 %collective-permute-start.8 = (bf16[256,640]{1,0:T(8,128)(2,1)}, bf16[256,640]{1,0:T(8,128)(2,1)}, u32[]{:S(2)}, u32[]{:S(2)}) collective-permute-start(bf16[256,640]{1,0:T(8,128)(2,1)} %get-tuple-element.31), channel_id=1, source_target_pairs={{0,6},{2,4},{4,2},{6,0},{8,14},{10,12},{12,10},{14,8},{16,22},{18,... | collective-permute-start | bytes 983048 | tf_op jit(solution)/shard_map/ppermute | solution.py:396
  20.4 3.5 %all-to-all-done.in_ref = bf16[16,72,128]{2,1,0:T(8,128)(2,1)S(1)} async-done(((bf16[16,72,128]{2,1,0:T(8,128)(2,1)}), bf16[16,72,128]{2,1,0:T(8,128)(2,1)S(1)}, u32[]{:S(2)}, u32[]{:S(2)}) %all-to-all-start) | async-done | bytes 294944 | tf_op jit(solution)/shard_map/all_to_all | solution.py:391
  23.9 0.6 shard_map.74
  24.5 2.6 %collective-permute-done.4.refs_5_ = bf16[256,640]{1,0:T(8,128)(2,1)} collective-permute-done((bf16[256,640]{1,0:T(8,128)(2,1)}, bf16[256,640]{1,0:T(8,128)(2,1)}, u32[]{:S(2)}, u32[]{:S(2)}) %collective-permute-start.4) | collective-permute-done | bytes 327712 | tf_op jit(solution)/shard_map/ppermute | solution.py:396
  27.1 3.2 %collective-permute-start.2 = (bf16[224,128]{1,0:T(8,128)(2,1)S(1)}, bf16[224,128]{1,0:T(8,128)(2,1)S(1)}, u32[]{:S(2)}, u32[]{:S(2)}) collective-permute-start(bf16[224,128]{1,0:T(8,128)(2,1)S(1)} %get-tuple-element.25.refs_0_), channel_id=1, source_target_pairs={{0,24},{2,26},{4,28},{6,30},{8,16},{10,18},{12,20},{14,22},{16,8},... | collective-permute-start | bytes 172040 | tf_op jit(solution)/shard_map/ppermute | solution.py:396
  30.3 11.4 %collective-permute-done.5.refs_6_ = bf16[256,640]{1,0:T(8,128)(2,1)} collective-permute-done((bf16[256,640]{1,0:T(8,128)(2,1)}, bf16[256,640]{1,0:T(8,128)(2,1)}, u32[]{:S(2)}, u32[]{:S(2)}) %collective-permute-start.5) | collective-permute-done | bytes 327712 | tf_op jit(solution)/shard_map/ppermute | solution.py:396
  41.7 2.4 %collective-permute-start.1 = (bf16[224,128]{1,0:T(8,128)(2,1)S(1)}, bf16[224,128]{1,0:T(8,128)(2,1)S(1)}, u32[]{:S(2)}, u32[]{:S(2)}) collective-permute-start(bf16[224,128]{1,0:T(8,128)(2,1)S(1)} %get-tuple-element.25.refs_0_), channel_id=1, source_target_pairs={{0,16},{2,18},{4,20},{6,22},{8,24},{10,26},{12,28},{14,30},{16,0},... | collective-permute-start | bytes 172040 | tf_op jit(solution)/shard_map/ppermute | solution.py:396
  44.2 3.5 %collective-permute-done.6.refs_7_ = bf16[256,640]{1,0:T(8,128)(2,1)} collective-permute-done((bf16[256,640]{1,0:T(8,128)(2,1)}, bf16[256,640]{1,0:T(8,128)(2,1)}, u32[]{:S(2)}, u32[]{:S(2)}) %collective-permute-start.6) | collective-permute-done | bytes 327712 | tf_op jit(solution)/shard_map/ppermute | solution.py:396
  47.7 1.5 %collective-permute-start = (bf16[224,128]{1,0:T(8,128)(2,1)S(1)}, bf16[224,128]{1,0:T(8,128)(2,1)S(1)}, u32[]{:S(2)}, u32[]{:S(2)}) collective-permute-start(bf16[224,128]{1,0:T(8,128)(2,1)S(1)} %get-tuple-element.25.refs_0_), channel_id=1, source_target_pairs={{0,8},{2,10},{4,12},{6,14},{8,0},{10,2},{12,4},{14,6},{16,24},{18,... | collective-permute-start | bytes 172040 | tf_op jit(solution)/shard_map/ppermute | solution.py:396
  49.2 2.7 %collective-permute-done.refs_1_ = bf16[224,128]{1,0:T(8,128)(2,1)S(1)} collective-permute-done((bf16[224,128]{1,0:T(8,128)(2,1)S(1)}, bf16[224,128]{1,0:T(8,128)(2,1)S(1)}, u32[]{:S(2)}, u32[]{:S(2)}) %collective-permute-start) | collective-permute-done | bytes 57376 | tf_op jit(solution)/shard_map/ppermute | solution.py:396
  51.9 3.1 %shard_map.75.near_ref = bf16[4,240,128]{2,1,0:T(8,128)(2,1)S(1)} custom-call(s32[1]{0:T(128)} %bitcast.1.where_ref, bf16[224,128]{1,0:T(8,128)(2,1)S(1)} %get-tuple-element.25.refs_0_, bf16[224,128]{1,0:T(8,128)(2,1)S(1)} %collective-permute-done.refs_1_, bf16[224,128]{1,0:T(8,128)(2,1)S(1)} %collective-permute-done.1.refs_2_, ...), custom_call_target="tpu_custom_call" | custom-call | flops 346030080 | bytes 1966080 | tf_op jit(solution)/shard_map/pallas_call | solution.py:376
  55.0 0.0 collective-permute-done.7.refs_4_
  55.0 0.0 collective-permute-done.8.refs_5_
  55.0 2.6 %shard_map.76 = (bf16[240,128]{1,0:T(8,128)(2,1)S(1)}, bf16[240,128]{1,0:T(8,128)(2,1)S(1)}, bf16[240,128]{1,0:T(8,128)(2,1)S(1)}, bf16[240,128]{1,0:T(8,128)(2,1)S(1)}) custom-call(s32[1]{0:T(128)} %bitcast.1.where_ref, bf16[4,240,128]{2,1,0:T(8,128)(2,1)S(1)} %shard_map.75.near_ref, bf16[224,128]{1,0:T(8,128)(2,1)S(1)} %get-tuple-element.25.refs_0_, ...), custom_call_target="tpu_custom_call" | custom-call | flops 115343360 | bytes 655360 | tf_op jit(solution)/shard_map/pallas_call | solution.py:376
  57.6 1.6 %collective-permute-start.9 = (bf16[240,128]{1,0:T(8,128)(2,1)S(1)}, bf16[240,128]{1,0:T(8,128)(2,1)S(1)}, u32[]{:S(2)}, u32[]{:S(2)}) collective-permute-start(bf16[240,128]{1,0:T(8,128)(2,1)S(1)} %get-tuple-element.33), channel_id=1, source_target_pairs={{0,8},{2,10},{4,12},{6,14},{8,0},{10,2},{12,4},{14,6},{16,24},{18,... | collective-permute-start | bytes 184328 | tf_op jit(solution)/shard_map/ppermute | solution.py:396
  59.2 2.0 %collective-permute-start.10 = (bf16[240,128]{1,0:T(8,128)(2,1)S(1)}, bf16[240,128]{1,0:T(8,128)(2,1)S(1)}, u32[]{:S(2)}, u32[]{:S(2)}) collective-permute-start(bf16[240,128]{1,0:T(8,128)(2,1)S(1)} %get-tuple-element.34), channel_id=1, source_target_pairs={{0,16},{2,18},{4,20},{6,22},{8,24},{10,26},{12,28},{14,30},{16,0},... | collective-permute-start | bytes 184328 | tf_op jit(solution)/shard_map/ppermute | solution.py:396
  61.2 0.9 collective-permute-start.11
  62.1 3.3 %collective-permute-done.10.refs_2_ = bf16[240,128]{1,0:T(8,128)(2,1)S(1)} collective-permute-done((bf16[240,128]{1,0:T(8,128)(2,1)S(1)}, bf16[240,128]{1,0:T(8,128)(2,1)S(1)}, u32[]{:S(2)}, u32[]{:S(2)}) %collective-permute-start.10) | collective-permute-done | bytes 61472 | tf_op jit(solution)/shard_map/ppermute | solution.py:396
  65.3 1.9 %collective-permute-done.11.refs_3_ = bf16[240,128]{1,0:T(8,128)(2,1)S(1)} collective-permute-done((bf16[240,128]{1,0:T(8,128)(2,1)S(1)}, bf16[240,128]{1,0:T(8,128)(2,1)S(1)}, u32[]{:S(2)}, u32[]{:S(2)}) %collective-permute-start.11) | collective-permute-done | bytes 61472 | tf_op jit(solution)/shard_map/ppermute | solution.py:396
  67.3 0.3 shard_map.77.refs_0_
  67.6 0.9 collective-permute-start.14
  68.5 0.3 collective-permute-start.13
  68.7 3.3 %collective-permute-start.12 = (bf16[224,128]{1,0:T(8,128)(2,1)S(1)}, bf16[224,128]{1,0:T(8,128)(2,1)S(1)}, u32[]{:S(2)}, u32[]{:S(2)}) collective-permute-start(bf16[224,128]{1,0:T(8,128)(2,1)S(1)} %shard_map.77.refs_0_), channel_id=1, source_target_pairs={{0,8},{2,10},{4,12},{6,14},{8,0},{10,2},{12,4},{14,6},{16,24},{18,... | collective-permute-start | bytes 172040 | tf_op jit(solution)/shard_map/ppermute | solution.py:396
  72.0 1.7 %collective-permute-done.14.refs_3_ = bf16[224,128]{1,0:T(8,128)(2,1)S(1)} collective-permute-done((bf16[224,128]{1,0:T(8,128)(2,1)S(1)}, bf16[224,128]{1,0:T(8,128)(2,1)S(1)}, u32[]{:S(2)}, u32[]{:S(2)}) %collective-permute-start.14) | collective-permute-done | bytes 57376 | tf_op jit(solution)/shard_map/ppermute | solution.py:396
  73.7 1.1 %collective-permute-done.13.refs_2_ = bf16[224,128]{1,0:T(8,128)(2,1)S(1)} collective-permute-done((bf16[224,128]{1,0:T(8,128)(2,1)S(1)}, bf16[224,128]{1,0:T(8,128)(2,1)S(1)}, u32[]{:S(2)}, u32[]{:S(2)}) %collective-permute-start.13) | collective-permute-done | bytes 57376 | tf_op jit(solution)/shard_map/ppermute | solution.py:396
  74.8 0.9 collective-permute-start.15
  75.8 1.2 %collective-permute-start.17 = (bf16[448,128]{1,0:T(8,128)(2,1)S(1)}, bf16[448,128]{1,0:T(8,128)(2,1)S(1)}, u32[]{:S(2)}, u32[]{:S(2)}) collective-permute-start(bf16[448,128]{1,0:T(8,128)(2,1)S(1)} %get-tuple-element.37.refs_1_), channel_id=1, source_target_pairs={{0,4},{2,6},{4,0},{6,2},{8,12},{10,14},{12,8},{14,10},{16,20},{18,... | collective-permute-start | bytes 344072 | tf_op jit(solution)/shard_map/ppermute | solution.py:396
  77.0 0.8 collective-permute-start.20
  77.8 1.2 %collective-permute-start.19 = (bf16[448,128]{1,0:T(8,128)(2,1)S(1)}, bf16[448,128]{1,0:T(8,128)(2,1)S(1)}, u32[]{:S(2)}, u32[]{:S(2)}) collective-permute-start(bf16[448,128]{1,0:T(8,128)(2,1)S(1)} %get-tuple-element.36.refs_0_), channel_id=1, source_target_pairs={{0,4},{2,6},{4,0},{6,2},{8,12},{10,14},{12,8},{14,10},{16,20},{18,... | collective-permute-start | bytes 344072 | tf_op jit(solution)/shard_map/ppermute | solution.py:396
  79.0 1.0 collective-permute-done.15.refs_0_
  80.0 1.0 collective-permute-start.16
  81.0 1.1 %collective-permute-start.18 = (bf16[448,128]{1,0:T(8,128)(2,1)S(1)}, bf16[448,128]{1,0:T(8,128)(2,1)S(1)}, u32[]{:S(2)}, u32[]{:S(2)}) collective-permute-start(bf16[448,128]{1,0:T(8,128)(2,1)S(1)} %collective-permute-done.17.refs_1_), channel_id=1, source_target_pairs={{0,2},{2,0},{4,6},{6,4},{8,10},{10,8},{12,14},{14,12},{16,18},{18,... | collective-permute-start | bytes 344072 | tf_op jit(solution)/shard_map/ppermute | solution.py:396
  82.1 0.3 shard_map.79.refs_2_
  82.4 0.3 shard_map.80.refs_2_
  82.8 0.3 shard_map.81.sum_ref
  83.1 1.6 %collective-permute-done.16.low_ref = bf16[448,128]{1,0:T(8,128)(2,1)S(1)} collective-permute-done((bf16[448,128]{1,0:T(8,128)(2,1)S(1)}, bf16[448,128]{1,0:T(8,128)(2,1)S(1)}, u32[]{:S(2)}, u32[]{:S(2)}) %collective-permute-start.16) | collective-permute-done | bytes 114720 | tf_op jit(solution)/shard_map/ppermute | solution.py:396
  84.7 1.0 collective-permute-done.18.high_ref
  85.8 0.7 shard_map.82
  86.5 13.2 %all_to_all.10.refs_0_ = bf16[16,80,128]{2,1,0:T(8,128)(2,1)S(1)} all-to-all(bf16[16,80,128]{2,1,0:T(8,128)(2,1)S(1)} %shard_map.82), channel_id=1, replica_groups=mesh['seq'=16,'head'=2] {'seq'}, dimensions={0} | all-to-all | bytes 655360 | tf_op jit(solution)/shard_map/all_to_all | solution.py:391
  99.7 1.6 %collective-permute-done.21.refs_1_ = bf16[16,80,128]{2,1,0:T(8,128)(2,1)S(1)} collective-permute-done((bf16[16,80,128]{2,1,0:T(8,128)(2,1)S(1)}, bf16[16,80,128]{2,1,0:T(8,128)(2,1)S(1)}, u32[]{:S(2)}, u32[]{:S(2)}) %collective-permute-start.21) | collective-permute-done | bytes 327712 | tf_op jit(solution)/shard_map/ppermute | solution.py:512
  101.3 1.6 %shard_map.83 = bf16[256,2560]{1,0:T(8,128)(2,1)} custom-call(s32[1]{0:T(128)} %bitcast.half_ref, bf16[32,256]{1,0:T(8,128)(2,1)S(1)} %get-tuple-element.23.chosen_ref, f32[256,128]{1,0:T(8,128)S(1)} %get-tuple-element.24.active_ref, bf16[16,80,128]{2,1,0:T(8,128)(2,1)S(1)} %all_to_all.10.refs_0_, bf16[16,80,128]{2,1,0:T(8,128)(2,1)S(1)} %collective-permute-done.21.refs_1_, ...), custom_call_target="tpu_custom_call" | custom-call | tf_op jit(solution)/shard_map/pallas_call | solution.py:376
  (22 shorter events, 0.1 us)
Async XLA Ops:
  0.0 23.9 %copy-start.5 = (s32[256]{0:T(256)S(1)}, s32[256]{0:T(256)}, u32[]{:S(2)}) copy-start(s32[256]{0:T(256)} %param.12) | copy-start | bytes 3076
  0.0 51.9 %copy-start.1 = (bf16[256,2560]{1,0:T(8,128)(2,1)S(1)}, bf16[256,2560]{1,0:T(8,128)(2,1)}, u32[]{:S(2)}) copy-start(bf16[256,2560]{1,0:T(8,128)(2,1)} %refs_8_.1) | copy-start | bytes 3932164
  0.0 51.9 %copy-start.2 = (bf16[256,2560]{1,0:T(8,128)(2,1)S(1)}, bf16[256,2560]{1,0:T(8,128)(2,1)}, u32[]{:S(2)}) copy-start(bf16[256,2560]{1,0:T(8,128)(2,1)} %refs_9_.1) | copy-start | bytes 3932164
  4.4 14.5 %collective-permute-start.3 = (bf16[256,640]{1,0:T(8,128)(2,1)}, bf16[256,640]{1,0:T(8,128)(2,1)S(1)}, u32[]{:S(2)}, u32[]{:S(2)}) collective-permute-start(bf16[256,640]{1,0:T(8,128)(2,1)} %get-tuple-element.26), channel_id=1, source_target_pairs={{0,2},{2,0},{4,6},{6,4},{8,10},{10,8},{12,14},{14,12},{16,18},{18,... | collective-permute-start | bytes 983048 | tf_op jit(solution)/shard_map/ppermute | solution.py:396
  7.5 16.3 %all-to-all-start = ((bf16[16,72,128]{2,1,0:T(8,128)(2,1)}), bf16[16,72,128]{2,1,0:T(8,128)(2,1)S(1)}, u32[]{:S(2)}, u32[]{:S(2)}) async-start(bf16[16,72,128]{2,1,0:T(8,128)(2,1)} %get-tuple-element.22), calls=%async_computation | async-start | bytes 589824 | tf_op jit(solution)/shard_map/all_to_all | solution.py:391
  13.5 13.7 %collective-permute-start.4 = (bf16[256,640]{1,0:T(8,128)(2,1)}, bf16[256,640]{1,0:T(8,128)(2,1)}, u32[]{:S(2)}, u32[]{:S(2)}) collective-permute-start(bf16[256,640]{1,0:T(8,128)(2,1)} %get-tuple-element.27), channel_id=1, source_target_pairs={{0,2},{2,0},{4,6},{6,4},{8,10},{10,8},{12,14},{14,12},{16,18},{18,... | collective-permute-start | bytes 983048 | tf_op jit(solution)/shard_map/ppermute | solution.py:396
  15.4 26.3 %collective-permute-start.5 = (bf16[256,640]{1,0:T(8,128)(2,1)}, bf16[256,640]{1,0:T(8,128)(2,1)}, u32[]{:S(2)}, u32[]{:S(2)}) collective-permute-start(bf16[256,640]{1,0:T(8,128)(2,1)} %get-tuple-element.28), channel_id=1, source_target_pairs={{0,4},{2,6},{4,0},{6,2},{8,12},{10,14},{12,8},{14,10},{16,20},{18,... | collective-permute-start | bytes 983048 | tf_op jit(solution)/shard_map/ppermute | solution.py:396
  16.9 30.8 %collective-permute-start.6 = (bf16[256,640]{1,0:T(8,128)(2,1)}, bf16[256,640]{1,0:T(8,128)(2,1)}, u32[]{:S(2)}, u32[]{:S(2)}) collective-permute-start(bf16[256,640]{1,0:T(8,128)(2,1)} %get-tuple-element.29), channel_id=1, source_target_pairs={{0,4},{2,6},{4,0},{6,2},{8,12},{10,14},{12,8},{14,10},{16,20},{18,... | collective-permute-start | bytes 983048 | tf_op jit(solution)/shard_map/ppermute | solution.py:396
  17.4 37.6 %collective-permute-start.7 = (bf16[256,640]{1,0:T(8,128)(2,1)}, bf16[256,640]{1,0:T(8,128)(2,1)}, u32[]{:S(2)}, u32[]{:S(2)}) collective-permute-start(bf16[256,640]{1,0:T(8,128)(2,1)} %get-tuple-element.30), channel_id=1, source_target_pairs={{0,6},{2,4},{4,2},{6,0},{8,14},{10,12},{12,10},{14,8},{16,22},{18,... | collective-permute-start | bytes 983048 | tf_op jit(solution)/shard_map/ppermute | solution.py:396
  18.9 36.1 %collective-permute-start.8 = (bf16[256,640]{1,0:T(8,128)(2,1)}, bf16[256,640]{1,0:T(8,128)(2,1)}, u32[]{:S(2)}, u32[]{:S(2)}) collective-permute-start(bf16[256,640]{1,0:T(8,128)(2,1)} %get-tuple-element.31), channel_id=1, source_target_pairs={{0,6},{2,4},{4,2},{6,0},{8,14},{10,12},{12,10},{14,8},{16,22},{18,... | collective-permute-start | bytes 983048 | tf_op jit(solution)/shard_map/ppermute | solution.py:396
  27.1 22.0 %collective-permute-start.2 = (bf16[224,128]{1,0:T(8,128)(2,1)S(1)}, bf16[224,128]{1,0:T(8,128)(2,1)S(1)}, u32[]{:S(2)}, u32[]{:S(2)}) collective-permute-start(bf16[224,128]{1,0:T(8,128)(2,1)S(1)} %get-tuple-element.25.refs_0_), channel_id=1, source_target_pairs={{0,24},{2,26},{4,28},{6,30},{8,16},{10,18},{12,20},{14,22},{16,8},... | collective-permute-start | bytes 172040 | tf_op jit(solution)/shard_map/ppermute | solution.py:396
  41.7 7.4 %collective-permute-start.1 = (bf16[224,128]{1,0:T(8,128)(2,1)S(1)}, bf16[224,128]{1,0:T(8,128)(2,1)S(1)}, u32[]{:S(2)}, u32[]{:S(2)}) collective-permute-start(bf16[224,128]{1,0:T(8,128)(2,1)S(1)} %get-tuple-element.25.refs_0_), channel_id=1, source_target_pairs={{0,16},{2,18},{4,20},{6,22},{8,24},{10,26},{12,28},{14,30},{16,0},... | collective-permute-start | bytes 172040 | tf_op jit(solution)/shard_map/ppermute | solution.py:396
  47.7 4.2 %collective-permute-start = (bf16[224,128]{1,0:T(8,128)(2,1)S(1)}, bf16[224,128]{1,0:T(8,128)(2,1)S(1)}, u32[]{:S(2)}, u32[]{:S(2)}) collective-permute-start(bf16[224,128]{1,0:T(8,128)(2,1)S(1)} %get-tuple-element.25.refs_0_), channel_id=1, source_target_pairs={{0,8},{2,10},{4,12},{6,14},{8,0},{10,2},{12,4},{14,6},{16,24},{18,... | collective-permute-start | bytes 172040 | tf_op jit(solution)/shard_map/ppermute | solution.py:396
  55.0 27.1 %copy-start = (bf16[2560,320]{0,1:T(8,128)(2,1)S(1)}, bf16[2560,320]{0,1:T(8,128)(2,1)}, u32[]{:S(2)}) copy-start(bf16[2560,320]{0,1:T(8,128)(2,1)} %param.13) | copy-start | bytes 4915204
  57.6 4.5 %collective-permute-start.9 = (bf16[240,128]{1,0:T(8,128)(2,1)S(1)}, bf16[240,128]{1,0:T(8,128)(2,1)S(1)}, u32[]{:S(2)}, u32[]{:S(2)}) collective-permute-start(bf16[240,128]{1,0:T(8,128)(2,1)S(1)} %get-tuple-element.33), channel_id=1, source_target_pairs={{0,8},{2,10},{4,12},{6,14},{8,0},{10,2},{12,4},{14,6},{16,24},{18,... | collective-permute-start | bytes 184328 | tf_op jit(solution)/shard_map/ppermute | solution.py:396
  59.2 6.2 %collective-permute-start.10 = (bf16[240,128]{1,0:T(8,128)(2,1)S(1)}, bf16[240,128]{1,0:T(8,128)(2,1)S(1)}, u32[]{:S(2)}, u32[]{:S(2)}) collective-permute-start(bf16[240,128]{1,0:T(8,128)(2,1)S(1)} %get-tuple-element.34), channel_id=1, source_target_pairs={{0,16},{2,18},{4,20},{6,22},{8,24},{10,26},{12,28},{14,30},{16,0},... | collective-permute-start | bytes 184328 | tf_op jit(solution)/shard_map/ppermute | solution.py:396
  61.2 6.1 %collective-permute-start.11 = (bf16[240,128]{1,0:T(8,128)(2,1)S(1)}, bf16[240,128]{1,0:T(8,128)(2,1)S(1)}, u32[]{:S(2)}, u32[]{:S(2)}) collective-permute-start(bf16[240,128]{1,0:T(8,128)(2,1)S(1)} %get-tuple-element.35), channel_id=1, source_target_pairs={{0,24},{2,26},{4,28},{6,30},{8,16},{10,18},{12,20},{14,22},{16,8},... | collective-permute-start | bytes 184328 | tf_op jit(solution)/shard_map/ppermute | solution.py:396
  67.6 6.2 %collective-permute-start.14 = (bf16[224,128]{1,0:T(8,128)(2,1)S(1)}, bf16[224,128]{1,0:T(8,128)(2,1)S(1)}, u32[]{:S(2)}, u32[]{:S(2)}) collective-permute-start(bf16[224,128]{1,0:T(8,128)(2,1)S(1)} %shard_map.77.refs_0_), channel_id=1, source_target_pairs={{0,24},{2,26},{4,28},{6,30},{8,16},{10,18},{12,20},{14,22},{16,8},... | collective-permute-start | bytes 172040 | tf_op jit(solution)/shard_map/ppermute | solution.py:396
  68.5 6.3 %collective-permute-start.13 = (bf16[224,128]{1,0:T(8,128)(2,1)S(1)}, bf16[224,128]{1,0:T(8,128)(2,1)S(1)}, u32[]{:S(2)}, u32[]{:S(2)}) collective-permute-start(bf16[224,128]{1,0:T(8,128)(2,1)S(1)} %shard_map.77.refs_0_), channel_id=1, source_target_pairs={{0,16},{2,18},{4,20},{6,22},{8,24},{10,26},{12,28},{14,30},{16,0},... | collective-permute-start | bytes 172040 | tf_op jit(solution)/shard_map/ppermute | solution.py:396
  68.7 6.0 %collective-permute-start.12 = (bf16[224,128]{1,0:T(8,128)(2,1)S(1)}, bf16[224,128]{1,0:T(8,128)(2,1)S(1)}, u32[]{:S(2)}, u32[]{:S(2)}) collective-permute-start(bf16[224,128]{1,0:T(8,128)(2,1)S(1)} %shard_map.77.refs_0_), channel_id=1, source_target_pairs={{0,8},{2,10},{4,12},{6,14},{8,0},{10,2},{12,4},{14,6},{16,24},{18,... | collective-permute-start | bytes 172040 | tf_op jit(solution)/shard_map/ppermute | solution.py:396
  74.8 5.1 %collective-permute-start.15 = (bf16[448,128]{1,0:T(8,128)(2,1)S(1)}, bf16[448,128]{1,0:T(8,128)(2,1)S(1)}, u32[]{:S(2)}, u32[]{:S(2)}) collective-permute-start(bf16[448,128]{1,0:T(8,128)(2,1)S(1)} %get-tuple-element.36.refs_0_), channel_id=1, source_target_pairs={{0,2},{2,0},{4,6},{6,4},{8,10},{10,8},{12,14},{14,12},{16,18},{18,... | collective-permute-start | bytes 344072 | tf_op jit(solution)/shard_map/ppermute | solution.py:396
  75.8 5.2 %collective-permute-start.17 = (bf16[448,128]{1,0:T(8,128)(2,1)S(1)}, bf16[448,128]{1,0:T(8,128)(2,1)S(1)}, u32[]{:S(2)}, u32[]{:S(2)}) collective-permute-start(bf16[448,128]{1,0:T(8,128)(2,1)S(1)} %get-tuple-element.37.refs_1_), channel_id=1, source_target_pairs={{0,4},{2,6},{4,0},{6,2},{8,12},{10,14},{12,8},{14,10},{16,20},{18,... | collective-permute-start | bytes 344072 | tf_op jit(solution)/shard_map/ppermute | solution.py:396
  77.0 5.5 %collective-permute-start.20 = (bf16[448,128]{1,0:T(8,128)(2,1)S(1)}, bf16[448,128]{1,0:T(8,128)(2,1)S(1)}, u32[]{:S(2)}, u32[]{:S(2)}) collective-permute-start(bf16[448,128]{1,0:T(8,128)(2,1)S(1)} %get-tuple-element.37.refs_1_), channel_id=1, source_target_pairs={{0,2},{2,0},{4,6},{6,4},{8,10},{10,8},{12,14},{14,12},{16,18},{18,... | collective-permute-start | bytes 344072 | tf_op jit(solution)/shard_map/ppermute | solution.py:396
  77.8 5.0 %collective-permute-start.19 = (bf16[448,128]{1,0:T(8,128)(2,1)S(1)}, bf16[448,128]{1,0:T(8,128)(2,1)S(1)}, u32[]{:S(2)}, u32[]{:S(2)}) collective-permute-start(bf16[448,128]{1,0:T(8,128)(2,1)S(1)} %get-tuple-element.36.refs_0_), channel_id=1, source_target_pairs={{0,4},{2,6},{4,0},{6,2},{8,12},{10,14},{12,8},{14,10},{16,20},{18,... | collective-permute-start | bytes 344072 | tf_op jit(solution)/shard_map/ppermute | solution.py:396
  80.0 4.8 %collective-permute-start.16 = (bf16[448,128]{1,0:T(8,128)(2,1)S(1)}, bf16[448,128]{1,0:T(8,128)(2,1)S(1)}, u32[]{:S(2)}, u32[]{:S(2)}) collective-permute-start(bf16[448,128]{1,0:T(8,128)(2,1)S(1)} %collective-permute-done.15.refs_0_), channel_id=1, source_target_pairs={{0,4},{2,6},{4,0},{6,2},{8,12},{10,14},{12,8},{14,10},{16,20},{18,... | collective-permute-start | bytes 344072 | tf_op jit(solution)/shard_map/ppermute | solution.py:396
  81.0 4.8 %collective-permute-start.18 = (bf16[448,128]{1,0:T(8,128)(2,1)S(1)}, bf16[448,128]{1,0:T(8,128)(2,1)S(1)}, u32[]{:S(2)}, u32[]{:S(2)}) collective-permute-start(bf16[448,128]{1,0:T(8,128)(2,1)S(1)} %collective-permute-done.17.refs_1_), channel_id=1, source_target_pairs={{0,2},{2,0},{4,6},{6,4},{8,10},{10,8},{12,14},{14,12},{16,18},{18,... | collective-permute-start | bytes 344072 | tf_op jit(solution)/shard_map/ppermute | solution.py:396
  85.8 15.6 %copy-start.3 = (bf16[256,2560]{1,0:T(8,128)(2,1)S(1)}, bf16[256,2560]{1,0:T(8,128)(2,1)}, u32[]{:S(2)}) copy-start(bf16[256,2560]{1,0:T(8,128)(2,1)} %refs_2_.1) | copy-start | bytes 3932164
  85.8 15.6 %copy-start.4 = (bf16[256,2560]{1,0:T(8,128)(2,1)S(1)}, bf16[256,2560]{1,0:T(8,128)(2,1)}, u32[]{:S(2)}) copy-start(bf16[256,2560]{1,0:T(8,128)(2,1)} %refs_3_.1) | copy-start | bytes 3932164
  99.7 1.6 %collective-permute-start.21 = (bf16[16,80,128]{2,1,0:T(8,128)(2,1)S(1)}, bf16[16,80,128]{2,1,0:T(8,128)(2,1)S(1)}, u32[]{:S(2)}, u32[]{:S(2)}) collective-permute-start(bf16[16,80,128]{2,1,0:T(8,128)(2,1)S(1)} %all_to_all.10.refs_0_), channel_id=1, source_target_pairs={{0,1},{1,0},{2,3},{3,2},{4,5},{5,4},{6,7},{7,6},{8,9},{9,8},{10,11... | collective-permute-start | bytes 983048 | tf_op jit(solution)/shard_map/ppermute | solution.py:512
